TPU v7x, 128 devices: a whole 4x4x4 slice. The times are simulated.
128 devices in a mesh: sec: 4 (over y_hi, core), tile: 32 (over x, y_lo, z).
Axes of the slice: x: 4, y: 4 (y_hi: 2, y_lo: 2; y = y_hi * 2 + y_lo), z: 4, core: 2. Of those that a mesh axis runs over, the one named last changes fastest.
Arguments:
- displacement: float32 [2, 64, 512, 2048], P(None, 'sec', 'tile'), may hold values from -6 to 6
- stiff_right: float32 [64, 512, 2048], P('sec', 'tile'), may hold values from 0.3 to 3
- stiff_down: float32 [64, 512, 2048], P('sec', 'tile'), may hold values from 0.3 to 3
- bilinear: float32 [128], replicated, may hold values from 0.15 to 0.6
- match_source: int32 [128, 3, 3, 32], P(('sec', 'tile')), may hold values from 0 to 4095, as said below
- match_target: int32 [128, 3, 3, 32], P(('sec', 'tile')), may hold values from 0 to 4095
- match_count: int32 [128, 3, 3], P(('sec', 'tile')), may hold values from 0 to 32, as said below
- match_weight: float32 [128, 3, 3, 32], P(('sec', 'tile')), may hold values from 0.3 to 3
Outputs:
- relaxed: float32 [2, 64, 512, 2048], P(None, 'sec', 'tile')
Inputs may be any that keep to these rules, and one draw needn't show every extreme that they name: `match_count`: counts toward owners that do not exist are 0. Every source device has 32 live slots toward some existing neighbouring owner, and one device receives 32 live slots from each of its neighbours and itself; slots at or past the count are ignored. `match_source`: the source block and the target block of every slot lie in adjacent sections, at most two node rows and one block column apart in the whole stack.
All inputs are finite; a program needn't handle non-finite values.
Results may differ from a plain program's by a relative error of at most 0.00002.
Values sent between devices are 32-bit elements; how exact they have to be, the bound alone decides.
No kernel may reach another device: no remote copies, remote signals or barrier semaphores. Data moves between devices by JAX's collectives and lax.ppermute only.
A program may use at most 128 MiB of HBM per device.

v0:
```python
import jax
import jax.numpy as jnp
from jax import lax
from jax.sharding import PartitionSpec as P

ITERS = 4


def shifted(value, axis, steps):
    count = lax.axis_size(axis)
    first, last = (max(0, -steps), min(count, count - steps))
    return lax.ppermute(value, axis, [(source, source + steps) for source in range(first, last)])


def extended(array, sides, width):
    for axis, dim in sides:
        size, length = (lax.axis_size(axis), array.shape[dim])
        up = [(i, (i + 1) % size) for i in range(size - 1)]
        down = [(j, i) for i, j in up]
        last = lax.slice_in_dim(array, length - width, length, axis=dim)
        first = lax.slice_in_dim(array, 0, width, axis=dim)
        before = lax.ppermute(last, axis, up)
        after = lax.ppermute(first, axis, down)
        array = jnp.concatenate([before, array, after], axis=dim)
    return array


def resample(blocks, bilinear):
    following = jnp.concatenate([blocks[..., 1:], blocks[..., -1:]], axis=-1)
    return blocks + bilinear * (following - blocks)


def send_near(outgoing):
    rows_out = []
    for first in range(3):
        columns_out = []
        for second in range(3):
            piece = outgoing[:, 2 - first, 2 - second]
            if first != 1:
                piece = shifted(piece, "sec", 1 - first)
            if second != 1:
                piece = shifted(piece, "tile", 1 - second)
            columns_out.append(piece)
        rows_out.append(jnp.stack(columns_out, axis=1))
    return jnp.stack(rows_out, axis=1)


def on_device(
    displacement,
    stiff_right,
    stiff_down,
    bilinear,
    match_source,
    match_target,
    match_count,
    match_weight,
):
    sections, rows, width = stiff_right.shape
    blocks_row = width // 128
    local_blocks = sections * rows * blocks_row
    slots = match_weight.shape[3]
    sec_count = lax.axis_size("sec")
    tile_count = lax.axis_size("tile")
    last_tile = lax.axis_index("tile") == tile_count - 1
    offset = jnp.arange(3, dtype=jnp.int32) - 1
    owner_sec = lax.axis_index("sec") + offset
    owner_tile = lax.axis_index("tile") + offset
    valid = ((owner_sec >= 0) & (owner_sec < sec_count))[:, None] & (
        (owner_tile >= 0) & (owner_tile < tile_count)
    )[None, :]
    column_pos = jnp.arange(width)[None, None, :]
    row_pos = jnp.arange(rows)[None, :, None]
    k_right = jnp.where(column_pos == width - 1, 0.0, stiff_right)
    k_down = jnp.where((row_pos == rows - 1) & last_tile, 0.0, stiff_down)
    k_left = jnp.concatenate(
        [jnp.zeros((sections, rows, 1), jnp.float32), k_right[:, :, :-1]], axis=2
    )
    upper_rim = shifted(k_down[:, -1:, :], "tile", 1)
    k_up = jnp.concatenate([upper_rim, k_down[:, :-1, :]], axis=1)
    requests = extended(match_target[0], (("sec", 0), ("tile", 1)), 1)[0::2, 0::2]
    sources = match_source[0]
    live = (jnp.arange(slots, dtype=jnp.int32)[None, None, :] < match_count[0][:, :, None]) & valid[
        :, :, None
    ]
    live_weight = jnp.where(live, match_weight[0], 0.0)
    flat_sources = sources.reshape(-1)
    match_diag = (
        jnp.zeros((local_blocks,), jnp.float32).at[flat_sources].add(live_weight.reshape(-1))
    )
    match_diag = jnp.broadcast_to(match_diag[:, None], (local_blocks, 128)).reshape(
        sections, rows, width
    )
    diag = 1.0 + k_right + k_left + k_down + k_up + match_diag
    zero_col = jnp.zeros((2, sections, rows, 1), jnp.float32)
    relaxed = displacement
    for step in range(ITERS):
        padded = extended(relaxed, (("tile", 2),), 1)
        above = padded[:, :, :-2, :]
        below = padded[:, :, 2:, :]
        right = jnp.concatenate([relaxed[..., 1:], zero_col], axis=-1)
        left = jnp.concatenate([zero_col, relaxed[..., :-1]], axis=-1)
        spring = (
            k_right * (right - relaxed)
            + k_left * (left - relaxed)
            + k_down * (below - relaxed)
            + k_up * (above - relaxed)
        )
        blocked = relaxed.reshape(2, local_blocks, 128)
        outgoing = resample(jnp.take(blocked, requests, axis=1), bilinear)
        interp = send_near(outgoing)
        source_now = jnp.take(blocked, sources, axis=1)
        term = live_weight[None, :, :, :, None] * (interp - source_now)
        matchforce = (
            jnp.zeros((2, local_blocks, 128), jnp.float32)
            .at[:, flat_sources]
            .add(term.reshape(2, -1, 128))
        )
        matchforce = matchforce.reshape(2, sections, rows, width)
        relaxed = relaxed + 0.8 * (spring + matchforce) / diag
    return relaxed


def solution(mesh):
    in_specs = (
        P(None, "sec", "tile", None),
        P("sec", "tile", None),
        P("sec", "tile", None),
        P(),
        P(("sec", "tile"), None, None, None),
        P(("sec", "tile"), None, None, None),
        P(("sec", "tile"), None, None),
        P(("sec", "tile"), None, None, None),
    )
    out_specs = P(None, "sec", "tile", None)
    return jax.shard_map(
        on_device, mesh=mesh, in_specs=in_specs, out_specs=out_specs, check_vma=False
    )
```

profile of v0, /device:TPU:6, one launch (start us, length us, event | category | flops | bytes accessed | tf_op | source)
XLA Modules:
  0.0 627.1 jit_solution(368074529208046780)
XLA Ops:
  9.8 8.1 %fusion.63 = (f32[2,16,16,2047]{3,2,1,0:T(8,128)}, f32[2,16,16,2047]{3,2,1,0:T(8,128)}) fusion(f32[2,16,16,2048]{3,2,1,0:T(8,128)} %param.10), kind=kLoop, calls=%fused_computation.171 | loop fusion | bytes 16769024 | tf_op jit(solution)/shard_map/slice | solution.py:100
  21.3 5.0 copy_select_fusion.1
  26.5 7.2 %collective-permute-start.6 = (s32[5,1,32]{2,1,0:T(1,128)S(1)}, s32[5,1,32]{2,1,0:T(1,128)S(1)}, u32[]{:S(2)}, u32[]{:S(2)}) collective-permute-start(s32[5,1,32]{2,1,0:T(1,128)S(1)} %get-tuple-element.63), channel_id=1, source_target_pairs={{1,0},{2,1},{3,2},{4,3},{5,4},{6,5},{7,6},{8,7},{9,8},{10,9},{11,1... | collective-permute-start | bytes 1928 | tf_op jit(solution)/shard_map/ppermute | solution.py:23
  35.7 4.9 reshape.154
  40.6 8.8 %copy.68 = f32[2,4096,128]{2,0,1:T(2,128)} copy(f32[2,4096,128]{2,1,0:T(8,128)} %reshape.154) | data formatting | bytes 8388608 | tf_op jit(solution)/shard_map/reshape | solution.py:108
  58.3 6.9 %collective-permute-start.13 = (f32[2,32,128]{2,0,1:T(2,128)S(1)}, f32[2,32,128]{2,0,1:T(2,128)S(1)}, u32[]{:S(2)}, u32[]{:S(2)}) collective-permute-start(f32[2,32,128]{2,0,1:T(2,128)S(1)} %get-tuple-element.57), channel_id=1, source_target_pairs={{1,0},{2,1},{3,2},{4,3},{5,4},{6,5},{7,6},{8,7},{9,8},{10,9},{11,1... | collective-permute-start | bytes 98312 | tf_op jit(solution)/shard_map/ppermute | solution.py:12
  92.7 5.5 collective-permute-start.10
  98.3 6.0 collective-permute-start.7
  104.3 6.3 %collective-permute-start.18 = (f32[2,32,128]{2,0,1:T(2,128)}, f32[2,32,128]{2,0,1:T(2,128)S(1)}, u32[]{:S(2)}, u32[]{:S(2)}) collective-permute-start(f32[2,32,128]{2,0,1:T(2,128)} %collective-permute-done.17), channel_id=1, source_target_pairs={{1,0},{2,1},{3,2},{4,3},{5,4},{6,5},{7,6},{8,7},{9,8},{10,9},{11,1... | collective-permute-start | bytes 98312 | tf_op jit(solution)/shard_map/ppermute | solution.py:12
  114.6 6.9 %collective-permute-start = (f32[2,16,1,2048]{3,2,1,0:T(1,128)S(1)}, f32[2,16,1,2048]{3,2,1,0:T(1,128)S(1)}, u32[]{:S(2)}, u32[]{:S(2)}) collective-permute-start(f32[2,16,1,2048]{3,2,1,0:T(1,128)S(1)} %get-tuple-element.22), channel_id=1, source_target_pairs={{1,0},{2,1},{3,2},{4,3},{5,4},{6,5},{7,6},{8,7},{9,8},{10,9},{11,1... | collective-permute-start | bytes 786440 | tf_op jit(solution)/shard_map/ppermute | solution.py:23
  131.3 4.6 collective-permute-done.8
  139.6 29.7 %scatter_fusion = f32[2,4096,128]{2,0,1:T(2,128)} fusion(f32[2,4096,128]{2,0,1:T(2,128)} %broadcast.153.clone, s32[288]{0:T(512)S(1)} %fusion.55, f32[288,2,128]{2,1,0:T(2,128)S(1)} %bitcast.212), kind=kCustom, calls=%fused_computation.8 | custom fusion | flops 73728 | bytes 885888 | tf_op jit(solution)/shard_map/scatter-add | solution.py:116
  169.3 4.5 copy.70
  173.8 4.9 reshape.156
  178.7 7.4 %pad_maximum_fusion.8 = (f32[16,16,2048]{2,0,1:T(8,128)S(1)}, f32[16,16,2048]{2,0,1:T(8,128)S(1)}) fusion(f32[16,15,2048]{2,0,1:T(8,128)} %slice.338, f32[16,1,2048]{2,0,1:T(8,128)} %collective-permute-done.1, f32[16,16,2048]{2,0,1:T(8,128)} %broadcast_in_dim.53, f32[16,16,2047]{2,0,1:T(8,128)} %bitcast.201, f32[16,16,2048]{2,1,0:T(8,128)} %param.11, ...), kind=kLoop, calls=%fused_computation.61 | loop fusion | flops 4194304 | bytes 14681104 | tf_op jit(solution)/shard_map/concatenate | solution.py:79
  191.3 10.9 %fusion.36 = f32[2,16,16,2048]{3,2,1,0:T(8,128)} fusion(f32[2,16,16,2048]{3,2,1,0:T(8,128)S(1)} %copy-done, f32[2,16,16,2048]{3,2,1,0:T(8,128)} %reshape.156, f32[2,16,1,2048]{3,2,1,0:T(1,128)S(1)} %collective-permute-done.2, f32[2,16,1,2048]{3,2,1,0:T(1,128)S(1)} %collective-permute-done, f32[2,16,16,2047]{3,2,1,0:T(8,128)} %get-tuple-element.21, ...), kind=kLoop, calls=%fused_computation.56 | loop fusion | flops 17825792 | bytes 31977472 | tf_op jit(solution)/shard_map/add | solution.py:119
  202.3 4.9 reshape.157
  207.2 9.3 %copy.73 = f32[2,4096,128]{2,0,1:T(2,128)} copy(f32[2,4096,128]{2,1,0:T(8,128)} %reshape.157) | data formatting | bytes 8388608 | tf_op jit(solution)/shard_map/reshape | solution.py:108
  221.0 8.1 %fusion.61 = (f32[2,16,16,2047]{3,2,1,0:T(8,128)}, f32[2,16,16,2047]{3,2,1,0:T(8,128)}) fusion(f32[2,16,16,2048]{3,2,1,0:T(8,128)} %fusion.36), kind=kLoop, calls=%fused_computation.169 | loop fusion | bytes 16769024 | tf_op jit(solution)/shard_map/slice | solution.py:100
  250.0 5.7 collective-permute-start.21
  255.8 5.5 collective-permute-start.32
  267.3 6.9 %collective-permute-start.19 = (f32[2,16,1,2048]{3,2,1,0:T(1,128)S(1)}, f32[2,16,1,2048]{3,2,1,0:T(1,128)S(1)}, u32[]{:S(2)}, u32[]{:S(2)}) collective-permute-start(f32[2,16,1,2048]{3,2,1,0:T(1,128)S(1)} %get-tuple-element.18), channel_id=1, source_target_pairs={{1,0},{2,1},{3,2},{4,3},{5,4},{6,5},{7,6},{8,7},{9,8},{10,9},{11,1... | collective-permute-start | bytes 786440 | tf_op jit(solution)/shard_map/ppermute | solution.py:23
  281.3 5.5 collective-permute-done.22
  290.7 28.5 %scatter_fusion.1 = f32[2,4096,128]{2,0,1:T(2,128)} fusion(f32[2,4096,128]{2,0,1:T(2,128)} %broadcast.153.clone.1, s32[288]{0:T(512)S(1)} %fusion.55, f32[288,2,128]{2,1,0:T(2,128)S(1)} %bitcast.213), kind=kCustom, calls=%fused_computation.10 | custom fusion | flops 73728 | bytes 885888 | tf_op jit(solution)/shard_map/scatter-add | solution.py:116
  319.2 4.5 copy.75
  323.7 4.9 reshape.159
  328.6 15.1 %fusion.26 = f32[2,16,16,2048]{3,2,1,0:T(8,128)} fusion(f32[2,16,16,2048]{3,2,1,0:T(8,128)} %fusion.36, f32[2,16,16,2048]{3,2,1,0:T(8,128)} %reshape.159, f32[2,16,1,2048]{3,2,1,0:T(1,128)S(1)} %collective-permute-done.20, f32[2,16,1,2048]{3,2,1,0:T(1,128)S(1)} %collective-permute-done.19, f32[2,16,16,2047]{3,2,1,0:T(8,128)} %get-tuple-element.17, ...), kind=kLoop, calls=%fused_computation.44 | loop fusion | flops 17825792 | bytes 31977472 | tf_op jit(solution)/shard_map/add | solution.py:119
  343.7 4.9 reshape.160
  348.6 8.7 %copy.76 = f32[2,4096,128]{2,0,1:T(2,128)} copy(f32[2,4096,128]{2,1,0:T(8,128)} %reshape.160) | data formatting | bytes 8388608 | tf_op jit(solution)/shard_map/reshape | solution.py:108
  361.8 8.1 %fusion.59 = (f32[2,16,16,2047]{3,2,1,0:T(8,128)}, f32[2,16,16,2047]{3,2,1,0:T(8,128)}) fusion(f32[2,16,16,2048]{3,2,1,0:T(8,128)} %fusion.26), kind=kLoop, calls=%fused_computation.167 | loop fusion | bytes 16769024 | tf_op jit(solution)/shard_map/slice | solution.py:100
  390.9 5.7 collective-permute-start.35
  396.6 4.8 collective-permute-start.46
  407.6 6.9 %collective-permute-start.33 = (f32[2,16,1,2048]{3,2,1,0:T(1,128)S(1)}, f32[2,16,1,2048]{3,2,1,0:T(1,128)S(1)}, u32[]{:S(2)}, u32[]{:S(2)}) collective-permute-start(f32[2,16,1,2048]{3,2,1,0:T(1,128)S(1)} %get-tuple-element.14), channel_id=1, source_target_pairs={{1,0},{2,1},{3,2},{4,3},{5,4},{6,5},{7,6},{8,7},{9,8},{10,9},{11,1... | collective-permute-start | bytes 786440 | tf_op jit(solution)/shard_map/ppermute | solution.py:23
  421.5 5.5 collective-permute-done.36
  430.9 29.7 %scatter_fusion.2 = f32[2,4096,128]{2,0,1:T(2,128)} fusion(f32[2,4096,128]{2,0,1:T(2,128)} %broadcast.153.clone.2, s32[288]{0:T(512)S(1)} %fusion.55, f32[288,2,128]{2,1,0:T(2,128)S(1)} %bitcast.214), kind=kCustom, calls=%fused_computation.11 | custom fusion | flops 73728 | bytes 885888 | tf_op jit(solution)/shard_map/scatter-add | solution.py:116
  460.7 4.5 copy.78
  465.1 4.9 reshape.162
  470.0 15.1 %fusion.16 = f32[2,16,16,2048]{3,2,1,0:T(8,128)} fusion(f32[2,16,16,2048]{3,2,1,0:T(8,128)} %fusion.26, f32[2,16,16,2048]{3,2,1,0:T(8,128)} %reshape.162, f32[2,16,1,2048]{3,2,1,0:T(1,128)S(1)} %collective-permute-done.34, f32[2,16,1,2048]{3,2,1,0:T(1,128)S(1)} %collective-permute-done.33, f32[2,16,16,2047]{3,2,1,0:T(8,128)} %get-tuple-element.13, ...), kind=kLoop, calls=%fused_computation.32 | loop fusion | flops 17825792 | bytes 31977472 | tf_op jit(solution)/shard_map/add | solution.py:119
  485.2 4.9 reshape.163
  490.0 8.8 %copy.79 = f32[2,4096,128]{2,0,1:T(2,128)} copy(f32[2,4096,128]{2,1,0:T(8,128)} %reshape.163) | data formatting | bytes 8388608 | tf_op jit(solution)/shard_map/reshape | solution.py:108
  503.3 8.1 %fusion.57 = (f32[2,16,16,2047]{3,2,1,0:T(8,128)}, f32[2,16,16,2047]{3,2,1,0:T(8,128)}) fusion(f32[2,16,16,2048]{3,2,1,0:T(8,128)} %fusion.16), kind=kLoop, calls=%fused_computation.165 | loop fusion | bytes 16769024 | tf_op jit(solution)/shard_map/slice | solution.py:100
  532.4 5.7 collective-permute-start.49
  538.1 4.9 collective-permute-start.60
  549.1 6.9 %collective-permute-start.47 = (f32[2,16,1,2048]{3,2,1,0:T(1,128)S(1)}, f32[2,16,1,2048]{3,2,1,0:T(1,128)S(1)}, u32[]{:S(2)}, u32[]{:S(2)}) collective-permute-start(f32[2,16,1,2048]{3,2,1,0:T(1,128)S(1)} %get-tuple-element.10), channel_id=1, source_target_pairs={{1,0},{2,1},{3,2},{4,3},{5,4},{6,5},{7,6},{8,7},{9,8},{10,9},{11,1... | collective-permute-start | bytes 786440 | tf_op jit(solution)/shard_map/ppermute | solution.py:23
  563.1 5.5 collective-permute-done.50
  572.5 29.7 %scatter_fusion.3 = f32[2,4096,128]{2,0,1:T(2,128)} fusion(f32[2,4096,128]{2,0,1:T(2,128)} %broadcast.153, s32[288]{0:T(512)S(1)} %fusion.55, f32[288,2,128]{2,1,0:T(2,128)S(1)} %bitcast.211), kind=kCustom, calls=%fused_computation.12 | custom fusion | flops 73728 | bytes 885888 | tf_op jit(solution)/shard_map/scatter-add | solution.py:116
  606.7 4.9 reshape.165
  611.5 15.1 %fusion.6 = f32[2,16,16,2048]{3,2,1,0:T(8,128)} fusion(f32[2,16,16,2048]{3,2,1,0:T(8,128)} %fusion.16, f32[2,16,16,2048]{3,2,1,0:T(8,128)} %reshape.165, f32[2,16,1,2048]{3,2,1,0:T(1,128)S(1)} %collective-permute-done.48, f32[2,16,1,2048]{3,2,1,0:T(1,128)S(1)} %collective-permute-done.47, f32[2,16,16,2047]{3,2,1,0:T(8,128)} %get-tuple-element.9, ...), kind=kLoop, calls=%fused_computation.20 | loop fusion | flops 17825792 | bytes 31977472 | tf_op jit(solution)/shard_map/add | solution.py:119
  (214 shorter events, 205.4 us)
Async XLA Ops:
  0.7 25.8 %collective-permute-start.4 = (s32[1,3,32]{2,0,1:T(1,128)S(1)}, s32[1,3,32]{2,0,1:T(1,128)S(1)}, u32[]{:S(2)}, u32[]{:S(2)}) collective-permute-start(s32[1,3,32]{2,0,1:T(1,128)S(1)} %get-tuple-element.65), channel_id=1, source_target_pairs={{32,0},{64,32},{96,64},{33,1},{65,33},{97,65},{34,2},{66,34},{98,6... | collective-permute-start | bytes 1160 | tf_op jit(solution)/shard_map/ppermute | solution.py:23
  2.0 24.5 %collective-permute-start.3 = (s32[1,3,32]{2,0,1:T(1,128)S(1)}, s32[1,3,32]{2,0,1:T(1,128)S(1)}, u32[]{:S(2)}, u32[]{:S(2)}) collective-permute-start(s32[1,3,32]{2,0,1:T(1,128)S(1)} %get-tuple-element.64), channel_id=1, source_target_pairs={{0,32},{32,64},{64,96},{1,33},{33,65},{65,97},{2,34},{34,66},{66,9... | collective-permute-start | bytes 1160 | tf_op jit(solution)/shard_map/ppermute | solution.py:22
  26.5 23.0 %collective-permute-start.6 = (s32[5,1,32]{2,1,0:T(1,128)S(1)}, s32[5,1,32]{2,1,0:T(1,128)S(1)}, u32[]{:S(2)}, u32[]{:S(2)}) collective-permute-start(s32[5,1,32]{2,1,0:T(1,128)S(1)} %get-tuple-element.63), channel_id=1, source_target_pairs={{1,0},{2,1},{3,2},{4,3},{5,4},{6,5},{7,6},{8,7},{9,8},{10,9},{11,1... | collective-permute-start | bytes 1928 | tf_op jit(solution)/shard_map/ppermute | solution.py:23
  55.7 37.0 %collective-permute-start.17 = (f32[2,32,128]{2,0,1:T(2,128)S(1)}, f32[2,32,128]{2,0,1:T(2,128)}, u32[]{:S(2)}, u32[]{:S(2)}) collective-permute-start(f32[2,32,128]{2,0,1:T(2,128)S(1)} %get-tuple-element.54), channel_id=1, source_target_pairs={{32,0},{64,32},{96,64},{33,1},{65,33},{97,65},{34,2},{66,34},{98,6... | collective-permute-start | bytes 98312 | tf_op jit(solution)/shard_map/ppermute | solution.py:12
  57.0 41.3 %collective-permute-start.14 = (f32[2,32,128]{2,0,1:T(2,128)S(1)}, f32[2,32,128]{2,0,1:T(2,128)}, u32[]{:S(2)}, u32[]{:S(2)}) collective-permute-start(f32[2,32,128]{2,0,1:T(2,128)S(1)} %get-tuple-element.56), channel_id=1, source_target_pairs={{32,0},{64,32},{96,64},{33,1},{65,33},{97,65},{34,2},{66,34},{98,6... | collective-permute-start | bytes 98312 | tf_op jit(solution)/shard_map/ppermute | solution.py:12
  58.3 46.0 %collective-permute-start.13 = (f32[2,32,128]{2,0,1:T(2,128)S(1)}, f32[2,32,128]{2,0,1:T(2,128)S(1)}, u32[]{:S(2)}, u32[]{:S(2)}) collective-permute-start(f32[2,32,128]{2,0,1:T(2,128)S(1)} %get-tuple-element.57), channel_id=1, source_target_pairs={{1,0},{2,1},{3,2},{4,3},{5,4},{6,5},{7,6},{8,7},{9,8},{10,9},{11,1... | collective-permute-start | bytes 98312 | tf_op jit(solution)/shard_map/ppermute | solution.py:12
  65.2 45.4 %collective-permute-start.12 = (f32[2,32,128]{2,0,1:T(2,128)S(1)}, f32[2,32,128]{2,0,1:T(2,128)S(1)}, u32[]{:S(2)}, u32[]{:S(2)}) collective-permute-start(f32[2,32,128]{2,0,1:T(2,128)S(1)} %get-tuple-element.59), channel_id=1, source_target_pairs={{0,1},{1,2},{2,3},{3,4},{4,5},{5,6},{6,7},{7,8},{8,9},{9,10},{10,1... | collective-permute-start | bytes 98312 | tf_op jit(solution)/shard_map/ppermute | solution.py:12
  91.4 21.2 %collective-permute-start.16 = (f32[2,32,128]{2,0,1:T(2,128)S(1)}, f32[2,32,128]{2,0,1:T(2,128)S(1)}, u32[]{:S(2)}, u32[]{:S(2)}) collective-permute-start(f32[2,32,128]{2,0,1:T(2,128)S(1)} %get-tuple-element.55), channel_id=1, source_target_pairs={{32,0},{64,32},{96,64},{33,1},{65,33},{97,65},{34,2},{66,34},{98,6... | collective-permute-start | bytes 98312 | tf_op jit(solution)/shard_map/ppermute | solution.py:12
  92.7 21.9 %collective-permute-start.10 = (f32[2,32,128]{2,0,1:T(2,128)S(1)}, f32[2,32,128]{2,0,1:T(2,128)S(1)}, u32[]{:S(2)}, u32[]{:S(2)}) collective-permute-start(f32[2,32,128]{2,0,1:T(2,128)S(1)} %get-tuple-element.60), channel_id=1, source_target_pairs={{0,32},{32,64},{64,96},{1,33},{33,65},{65,97},{2,34},{34,66},{66,9... | collective-permute-start | bytes 98312 | tf_op jit(solution)/shard_map/ppermute | solution.py:12
  98.3 23.3 %collective-permute-start.7 = (f32[2,32,128]{2,0,1:T(2,128)}, f32[2,32,128]{2,0,1:T(2,128)S(1)}, u32[]{:S(2)}, u32[]{:S(2)}) collective-permute-start(f32[2,32,128]{2,0,1:T(2,128)} %get-tuple-element.53), channel_id=1, source_target_pairs={{0,32},{32,64},{64,96},{1,33},{33,65},{65,97},{2,34},{34,66},{66,9... | collective-permute-start | bytes 98312 | tf_op jit(solution)/shard_map/ppermute | solution.py:12
  104.3 18.8 %collective-permute-start.18 = (f32[2,32,128]{2,0,1:T(2,128)}, f32[2,32,128]{2,0,1:T(2,128)S(1)}, u32[]{:S(2)}, u32[]{:S(2)}) collective-permute-start(f32[2,32,128]{2,0,1:T(2,128)} %collective-permute-done.17), channel_id=1, source_target_pairs={{1,0},{2,1},{3,2},{4,3},{5,4},{6,5},{7,6},{8,7},{9,8},{10,9},{11,1... | collective-permute-start | bytes 98312 | tf_op jit(solution)/shard_map/ppermute | solution.py:12
  112.7 78.7 %collective-permute-start.2 = (f32[2,16,1,2048]{3,2,1,0:T(1,128)}, f32[2,16,1,2048]{3,2,1,0:T(1,128)S(1)}, u32[]{:S(2)}, u32[]{:S(2)}) collective-permute-start(f32[2,16,1,2048]{3,2,1,0:T(1,128)} %get-tuple-element.23), channel_id=1, source_target_pairs={{0,1},{1,2},{2,3},{3,4},{4,5},{5,6},{6,7},{7,8},{8,9},{9,10},{10,1... | collective-permute-start | bytes 786440 | tf_op jit(solution)/shard_map/ppermute | solution.py:22
  114.6 76.7 %collective-permute-start = (f32[2,16,1,2048]{3,2,1,0:T(1,128)S(1)}, f32[2,16,1,2048]{3,2,1,0:T(1,128)S(1)}, u32[]{:S(2)}, u32[]{:S(2)}) collective-permute-start(f32[2,16,1,2048]{3,2,1,0:T(1,128)S(1)} %get-tuple-element.22), channel_id=1, source_target_pairs={{1,0},{2,1},{3,2},{4,3},{5,4},{6,5},{7,6},{8,7},{9,8},{10,9},{11,1... | collective-permute-start | bytes 786440 | tf_op jit(solution)/shard_map/ppermute | solution.py:23
  129.1 49.7 %collective-permute-start.1 = (f32[16,1,2048]{2,0,1:T(8,128)}, f32[16,1,2048]{2,0,1:T(8,128)}, u32[]{:S(2)}, u32[]{:S(2)}) collective-permute-start(f32[16,1,2048]{2,0,1:T(8,128)} %slice.337), channel_id=1, source_target_pairs={{0,1},{1,2},{2,3},{3,4},{4,5},{5,6},{6,7},{7,8},{8,9},{9,10},{10,1... | collective-permute-start | bytes 393224 | tf_op jit(solution)/shard_map/ppermute | solution.py:12
  229.9 16.4 %collective-permute-start.31 = (f32[2,32,128]{2,0,1:T(2,128)S(1)}, f32[2,32,128]{2,0,1:T(2,128)}, u32[]{:S(2)}, u32[]{:S(2)}) collective-permute-start(f32[2,32,128]{2,0,1:T(2,128)S(1)} %get-tuple-element.45), channel_id=1, source_target_pairs={{32,0},{64,32},{96,64},{33,1},{65,33},{97,65},{34,2},{66,34},{98,6... | collective-permute-start | bytes 98312 | tf_op jit(solution)/shard_map/ppermute | solution.py:12
  231.2 18.8 %collective-permute-start.28 = (f32[2,32,128]{2,0,1:T(2,128)S(1)}, f32[2,32,128]{2,0,1:T(2,128)S(1)}, u32[]{:S(2)}, u32[]{:S(2)}) collective-permute-start(f32[2,32,128]{2,0,1:T(2,128)S(1)} %get-tuple-element.47), channel_id=1, source_target_pairs={{32,0},{64,32},{96,64},{33,1},{65,33},{97,65},{34,2},{66,34},{98,6... | collective-permute-start | bytes 98312 | tf_op jit(solution)/shard_map/ppermute | solution.py:12
  232.5 23.3 %collective-permute-start.27 = (f32[2,32,128]{2,0,1:T(2,128)S(1)}, f32[2,32,128]{2,0,1:T(2,128)S(1)}, u32[]{:S(2)}, u32[]{:S(2)}) collective-permute-start(f32[2,32,128]{2,0,1:T(2,128)S(1)} %get-tuple-element.48), channel_id=1, source_target_pairs={{1,0},{2,1},{3,2},{4,3},{5,4},{6,5},{7,6},{8,7},{9,8},{10,9},{11,1... | collective-permute-start | bytes 98312 | tf_op jit(solution)/shard_map/ppermute | solution.py:12
  234.8 26.4 %collective-permute-start.26 = (f32[2,32,128]{2,0,1:T(2,128)S(1)}, f32[2,32,128]{2,0,1:T(2,128)S(1)}, u32[]{:S(2)}, u32[]{:S(2)}) collective-permute-start(f32[2,32,128]{2,0,1:T(2,128)S(1)} %get-tuple-element.50), channel_id=1, source_target_pairs={{0,1},{1,2},{2,3},{3,4},{4,5},{5,6},{6,7},{7,8},{8,9},{9,10},{10,1... | collective-permute-start | bytes 98312 | tf_op jit(solution)/shard_map/ppermute | solution.py:12
  245.0 18.2 %collective-permute-start.30 = (f32[2,32,128]{2,0,1:T(2,128)S(1)}, f32[2,32,128]{2,0,1:T(2,128)S(1)}, u32[]{:S(2)}, u32[]{:S(2)}) collective-permute-start(f32[2,32,128]{2,0,1:T(2,128)S(1)} %get-tuple-element.46), channel_id=1, source_target_pairs={{32,0},{64,32},{96,64},{33,1},{65,33},{97,65},{34,2},{66,34},{98,6... | collective-permute-start | bytes 98312 | tf_op jit(solution)/shard_map/ppermute | solution.py:12
  246.3 19.1 %collective-permute-start.24 = (f32[2,32,128]{2,0,1:T(2,128)S(1)}, f32[2,32,128]{2,0,1:T(2,128)S(1)}, u32[]{:S(2)}, u32[]{:S(2)}) collective-permute-start(f32[2,32,128]{2,0,1:T(2,128)S(1)} %get-tuple-element.51), channel_id=1, source_target_pairs={{0,32},{32,64},{64,96},{1,33},{33,65},{65,97},{2,34},{34,66},{66,9... | collective-permute-start | bytes 98312 | tf_op jit(solution)/shard_map/ppermute | solution.py:12
  250.0 17.3 %collective-permute-start.21 = (f32[2,32,128]{2,0,1:T(2,128)S(1)}, f32[2,32,128]{2,0,1:T(2,128)S(1)}, u32[]{:S(2)}, u32[]{:S(2)}) collective-permute-start(f32[2,32,128]{2,0,1:T(2,128)S(1)} %get-tuple-element.44), channel_id=1, source_target_pairs={{0,32},{32,64},{64,96},{1,33},{33,65},{65,97},{2,34},{34,66},{66,9... | collective-permute-start | bytes 98312 | tf_op jit(solution)/shard_map/ppermute | solution.py:12
  255.8 18.5 %collective-permute-start.32 = (f32[2,32,128]{2,0,1:T(2,128)}, f32[2,32,128]{2,0,1:T(2,128)S(1)}, u32[]{:S(2)}, u32[]{:S(2)}) collective-permute-start(f32[2,32,128]{2,0,1:T(2,128)} %collective-permute-done.31), channel_id=1, source_target_pairs={{1,0},{2,1},{3,2},{4,3},{5,4},{6,5},{7,6},{8,7},{9,8},{10,9},{11,1... | collective-permute-start | bytes 98312 | tf_op jit(solution)/shard_map/ppermute | solution.py:12
  261.2 16.7 %collective-permute-start.29 = (f32[2,32,128]{2,0,1:T(2,128)S(1)}, f32[2,32,128]{2,0,1:T(2,128)S(1)}, u32[]{:S(2)}, u32[]{:S(2)}) collective-permute-start(f32[2,32,128]{2,0,1:T(2,128)S(1)} %collective-permute-done.28), channel_id=1, source_target_pairs={{0,1},{1,2},{2,3},{3,4},{4,5},{5,6},{6,7},{7,8},{8,9},{9,10},{10,1... | collective-permute-start | bytes 98312 | tf_op jit(solution)/shard_map/ppermute | solution.py:12
  263.2 17.0 %collective-permute-start.23 = (f32[2,32,128]{2,0,1:T(2,128)S(1)}, f32[2,32,128]{2,0,1:T(2,128)S(1)}, u32[]{:S(2)}, u32[]{:S(2)}) collective-permute-start(f32[2,32,128]{2,0,1:T(2,128)S(1)} %get-tuple-element.52), channel_id=1, source_target_pairs={{0,32},{32,64},{64,96},{1,33},{33,65},{65,97},{2,34},{34,66},{66,9... | collective-permute-start | bytes 98312 | tf_op jit(solution)/shard_map/ppermute | solution.py:12
  265.4 63.2 %collective-permute-start.20 = (f32[2,16,1,2048]{3,2,1,0:T(1,128)}, f32[2,16,1,2048]{3,2,1,0:T(1,128)S(1)}, u32[]{:S(2)}, u32[]{:S(2)}) collective-permute-start(f32[2,16,1,2048]{3,2,1,0:T(1,128)} %get-tuple-element.19), channel_id=1, source_target_pairs={{0,1},{1,2},{2,3},{3,4},{4,5},{5,6},{6,7},{7,8},{8,9},{9,10},{10,1... | collective-permute-start | bytes 786440 | tf_op jit(solution)/shard_map/ppermute | solution.py:22
  267.3 61.3 %collective-permute-start.19 = (f32[2,16,1,2048]{3,2,1,0:T(1,128)S(1)}, f32[2,16,1,2048]{3,2,1,0:T(1,128)S(1)}, u32[]{:S(2)}, u32[]{:S(2)}) collective-permute-start(f32[2,16,1,2048]{3,2,1,0:T(1,128)S(1)} %get-tuple-element.18), channel_id=1, source_target_pairs={{1,0},{2,1},{3,2},{4,3},{5,4},{6,5},{7,6},{8,7},{9,8},{10,9},{11,1... | collective-permute-start | bytes 786440 | tf_op jit(solution)/shard_map/ppermute | solution.py:23
  372.0 18.8 %collective-permute-start.42 = (f32[2,32,128]{2,0,1:T(2,128)S(1)}, f32[2,32,128]{2,0,1:T(2,128)S(1)}, u32[]{:S(2)}, u32[]{:S(2)}) collective-permute-start(f32[2,32,128]{2,0,1:T(2,128)S(1)} %get-tuple-element.38), channel_id=1, source_target_pairs={{32,0},{64,32},{96,64},{33,1},{65,33},{97,65},{34,2},{66,34},{98,6... | collective-permute-start | bytes 98312 | tf_op jit(solution)/shard_map/ppermute | solution.py:12
  373.3 23.3 %collective-permute-start.41 = (f32[2,32,128]{2,0,1:T(2,128)S(1)}, f32[2,32,128]{2,0,1:T(2,128)S(1)}, u32[]{:S(2)}, u32[]{:S(2)}) collective-permute-start(f32[2,32,128]{2,0,1:T(2,128)S(1)} %get-tuple-element.39), channel_id=1, source_target_pairs={{1,0},{2,1},{3,2},{4,3},{5,4},{6,5},{7,6},{8,7},{9,8},{10,9},{11,1... | collective-permute-start | bytes 98312 | tf_op jit(solution)/shard_map/ppermute | solution.py:12
  375.3 26.2 %collective-permute-start.40 = (f32[2,32,128]{2,0,1:T(2,128)S(1)}, f32[2,32,128]{2,0,1:T(2,128)S(1)}, u32[]{:S(2)}, u32[]{:S(2)}) collective-permute-start(f32[2,32,128]{2,0,1:T(2,128)S(1)} %get-tuple-element.41), channel_id=1, source_target_pairs={{0,1},{1,2},{2,3},{3,4},{4,5},{5,6},{6,7},{7,8},{8,9},{9,10},{10,1... | collective-permute-start | bytes 98312 | tf_op jit(solution)/shard_map/ppermute | solution.py:12
  385.8 17.6 %collective-permute-start.44 = (f32[2,32,128]{2,0,1:T(2,128)S(1)}, f32[2,32,128]{2,0,1:T(2,128)S(1)}, u32[]{:S(2)}, u32[]{:S(2)}) collective-permute-start(f32[2,32,128]{2,0,1:T(2,128)S(1)} %get-tuple-element.37), channel_id=1, source_target_pairs={{32,0},{64,32},{96,64},{33,1},{65,33},{97,65},{34,2},{66,34},{98,6... | collective-permute-start | bytes 98312 | tf_op jit(solution)/shard_map/ppermute | solution.py:12
  387.2 18.5 %collective-permute-start.38 = (f32[2,32,128]{2,0,1:T(2,128)S(1)}, f32[2,32,128]{2,0,1:T(2,128)S(1)}, u32[]{:S(2)}, u32[]{:S(2)}) collective-permute-start(f32[2,32,128]{2,0,1:T(2,128)S(1)} %get-tuple-element.42), channel_id=1, source_target_pairs={{0,32},{32,64},{64,96},{1,33},{33,65},{65,97},{2,34},{34,66},{66,9... | collective-permute-start | bytes 98312 | tf_op jit(solution)/shard_map/ppermute | solution.py:12
  390.9 16.6 %collective-permute-start.35 = (f32[2,32,128]{2,0,1:T(2,128)S(1)}, f32[2,32,128]{2,0,1:T(2,128)S(1)}, u32[]{:S(2)}, u32[]{:S(2)}) collective-permute-start(f32[2,32,128]{2,0,1:T(2,128)S(1)} %get-tuple-element.35), channel_id=1, source_target_pairs={{0,32},{32,64},{64,96},{1,33},{33,65},{65,97},{2,34},{34,66},{66,9... | collective-permute-start | bytes 98312 | tf_op jit(solution)/shard_map/ppermute | solution.py:12
  396.6 17.9 %collective-permute-start.46 = (f32[2,32,128]{2,0,1:T(2,128)}, f32[2,32,128]{2,0,1:T(2,128)S(1)}, u32[]{:S(2)}, u32[]{:S(2)}) collective-permute-start(f32[2,32,128]{2,0,1:T(2,128)} %collective-permute-done.45), channel_id=1, source_target_pairs={{1,0},{2,1},{3,2},{4,3},{5,4},{6,5},{7,6},{8,7},{9,8},{10,9},{11,1... | collective-permute-start | bytes 98312 | tf_op jit(solution)/shard_map/ppermute | solution.py:12
  401.5 16.7 %collective-permute-start.43 = (f32[2,32,128]{2,0,1:T(2,128)S(1)}, f32[2,32,128]{2,0,1:T(2,128)S(1)}, u32[]{:S(2)}, u32[]{:S(2)}) collective-permute-start(f32[2,32,128]{2,0,1:T(2,128)S(1)} %collective-permute-done.42), channel_id=1, source_target_pairs={{0,1},{1,2},{2,3},{3,4},{4,5},{5,6},{6,7},{7,8},{8,9},{9,10},{10,1... | collective-permute-start | bytes 98312 | tf_op jit(solution)/shard_map/ppermute | solution.py:12
  403.5 17.0 %collective-permute-start.37 = (f32[2,32,128]{2,0,1:T(2,128)S(1)}, f32[2,32,128]{2,0,1:T(2,128)S(1)}, u32[]{:S(2)}, u32[]{:S(2)}) collective-permute-start(f32[2,32,128]{2,0,1:T(2,128)S(1)} %get-tuple-element.43), channel_id=1, source_target_pairs={{0,32},{32,64},{64,96},{1,33},{33,65},{65,97},{2,34},{34,66},{66,9... | collective-permute-start | bytes 98312 | tf_op jit(solution)/shard_map/ppermute | solution.py:12
  405.6 64.4 %collective-permute-start.34 = (f32[2,16,1,2048]{3,2,1,0:T(1,128)}, f32[2,16,1,2048]{3,2,1,0:T(1,128)S(1)}, u32[]{:S(2)}, u32[]{:S(2)}) collective-permute-start(f32[2,16,1,2048]{3,2,1,0:T(1,128)} %get-tuple-element.15), channel_id=1, source_target_pairs={{0,1},{1,2},{2,3},{3,4},{4,5},{5,6},{6,7},{7,8},{8,9},{9,10},{10,1... | collective-permute-start | bytes 786440 | tf_op jit(solution)/shard_map/ppermute | solution.py:22
  407.6 62.5 %collective-permute-start.33 = (f32[2,16,1,2048]{3,2,1,0:T(1,128)S(1)}, f32[2,16,1,2048]{3,2,1,0:T(1,128)S(1)}, u32[]{:S(2)}, u32[]{:S(2)}) collective-permute-start(f32[2,16,1,2048]{3,2,1,0:T(1,128)S(1)} %get-tuple-element.14), channel_id=1, source_target_pairs={{1,0},{2,1},{3,2},{4,3},{5,4},{6,5},{7,6},{8,7},{9,8},{10,9},{11,1... | collective-permute-start | bytes 786440 | tf_op jit(solution)/shard_map/ppermute | solution.py:23
  513.5 18.8 %collective-permute-start.56 = (f32[2,32,128]{2,0,1:T(2,128)S(1)}, f32[2,32,128]{2,0,1:T(2,128)S(1)}, u32[]{:S(2)}, u32[]{:S(2)}) collective-permute-start(f32[2,32,128]{2,0,1:T(2,128)S(1)} %get-tuple-element.29), channel_id=1, source_target_pairs={{32,0},{64,32},{96,64},{33,1},{65,33},{97,65},{34,2},{66,34},{98,6... | collective-permute-start | bytes 98312 | tf_op jit(solution)/shard_map/ppermute | solution.py:12
  514.8 23.3 %collective-permute-start.55 = (f32[2,32,128]{2,0,1:T(2,128)S(1)}, f32[2,32,128]{2,0,1:T(2,128)S(1)}, u32[]{:S(2)}, u32[]{:S(2)}) collective-permute-start(f32[2,32,128]{2,0,1:T(2,128)S(1)} %get-tuple-element.30), channel_id=1, source_target_pairs={{1,0},{2,1},{3,2},{4,3},{5,4},{6,5},{7,6},{8,7},{9,8},{10,9},{11,1... | collective-permute-start | bytes 98312 | tf_op jit(solution)/shard_map/ppermute | solution.py:12
  516.7 26.3 %collective-permute-start.54 = (f32[2,32,128]{2,0,1:T(2,128)S(1)}, f32[2,32,128]{2,0,1:T(2,128)S(1)}, u32[]{:S(2)}, u32[]{:S(2)}) collective-permute-start(f32[2,32,128]{2,0,1:T(2,128)S(1)} %get-tuple-element.32), channel_id=1, source_target_pairs={{0,1},{1,2},{2,3},{3,4},{4,5},{5,6},{6,7},{7,8},{8,9},{9,10},{10,1... | collective-permute-start | bytes 98312 | tf_op jit(solution)/shard_map/ppermute | solution.py:12
  527.3 17.7 %collective-permute-start.58 = (f32[2,32,128]{2,0,1:T(2,128)S(1)}, f32[2,32,128]{2,0,1:T(2,128)S(1)}, u32[]{:S(2)}, u32[]{:S(2)}) collective-permute-start(f32[2,32,128]{2,0,1:T(2,128)S(1)} %get-tuple-element.28), channel_id=1, source_target_pairs={{32,0},{64,32},{96,64},{33,1},{65,33},{97,65},{34,2},{66,34},{98,6... | collective-permute-start | bytes 98312 | tf_op jit(solution)/shard_map/ppermute | solution.py:12
  528.6 18.5 %collective-permute-start.52 = (f32[2,32,128]{2,0,1:T(2,128)S(1)}, f32[2,32,128]{2,0,1:T(2,128)S(1)}, u32[]{:S(2)}, u32[]{:S(2)}) collective-permute-start(f32[2,32,128]{2,0,1:T(2,128)S(1)} %get-tuple-element.33), channel_id=1, source_target_pairs={{0,32},{32,64},{64,96},{1,33},{33,65},{65,97},{2,34},{34,66},{66,9... | collective-permute-start | bytes 98312 | tf_op jit(solution)/shard_map/ppermute | solution.py:12
  532.4 16.7 %collective-permute-start.49 = (f32[2,32,128]{2,0,1:T(2,128)S(1)}, f32[2,32,128]{2,0,1:T(2,128)S(1)}, u32[]{:S(2)}, u32[]{:S(2)}) collective-permute-start(f32[2,32,128]{2,0,1:T(2,128)S(1)} %get-tuple-element.26), channel_id=1, source_target_pairs={{0,32},{32,64},{64,96},{1,33},{33,65},{65,97},{2,34},{34,66},{66,9... | collective-permute-start | bytes 98312 | tf_op jit(solution)/shard_map/ppermute | solution.py:12
  538.1 18.0 %collective-permute-start.60 = (f32[2,32,128]{2,0,1:T(2,128)}, f32[2,32,128]{2,0,1:T(2,128)S(1)}, u32[]{:S(2)}, u32[]{:S(2)}) collective-permute-start(f32[2,32,128]{2,0,1:T(2,128)} %collective-permute-done.59), channel_id=1, source_target_pairs={{1,0},{2,1},{3,2},{4,3},{5,4},{6,5},{7,6},{8,7},{9,8},{10,9},{11,1... | collective-permute-start | bytes 98312 | tf_op jit(solution)/shard_map/ppermute | solution.py:12
  543.0 16.7 %collective-permute-start.57 = (f32[2,32,128]{2,0,1:T(2,128)S(1)}, f32[2,32,128]{2,0,1:T(2,128)S(1)}, u32[]{:S(2)}, u32[]{:S(2)}) collective-permute-start(f32[2,32,128]{2,0,1:T(2,128)S(1)} %collective-permute-done.56), channel_id=1, source_target_pairs={{0,1},{1,2},{2,3},{3,4},{4,5},{5,6},{6,7},{7,8},{8,9},{9,10},{10,1... | collective-permute-start | bytes 98312 | tf_op jit(solution)/shard_map/ppermute | solution.py:12
  545.0 17.0 %collective-permute-start.51 = (f32[2,32,128]{2,0,1:T(2,128)S(1)}, f32[2,32,128]{2,0,1:T(2,128)S(1)}, u32[]{:S(2)}, u32[]{:S(2)}) collective-permute-start(f32[2,32,128]{2,0,1:T(2,128)S(1)} %get-tuple-element.34), channel_id=1, source_target_pairs={{0,32},{32,64},{64,96},{1,33},{33,65},{65,97},{2,34},{34,66},{66,9... | collective-permute-start | bytes 98312 | tf_op jit(solution)/shard_map/ppermute | solution.py:12
  547.2 64.4 %collective-permute-start.48 = (f32[2,16,1,2048]{3,2,1,0:T(1,128)}, f32[2,16,1,2048]{3,2,1,0:T(1,128)S(1)}, u32[]{:S(2)}, u32[]{:S(2)}) collective-permute-start(f32[2,16,1,2048]{3,2,1,0:T(1,128)} %get-tuple-element.11), channel_id=1, source_target_pairs={{0,1},{1,2},{2,3},{3,4},{4,5},{5,6},{6,7},{7,8},{8,9},{9,10},{10,1... | collective-permute-start | bytes 786440 | tf_op jit(solution)/shard_map/ppermute | solution.py:22
  549.1 62.4 %collective-permute-start.47 = (f32[2,16,1,2048]{3,2,1,0:T(1,128)S(1)}, f32[2,16,1,2048]{3,2,1,0:T(1,128)S(1)}, u32[]{:S(2)}, u32[]{:S(2)}) collective-permute-start(f32[2,16,1,2048]{3,2,1,0:T(1,128)S(1)} %get-tuple-element.10), channel_id=1, source_target_pairs={{1,0},{2,1},{3,2},{4,3},{5,4},{6,5},{7,6},{8,7},{9,8},{10,9},{11,1... | collective-permute-start | bytes 786440 | tf_op jit(solution)/shard_map/ppermute | solution.py:23
  (21 other events, 240.0 us)
where the time goes:
time: 639 us; the launch traced here: 627 us
  other arithmetic  204 us (32%)
  local copies, waits for them, and re-layouts  203 us (32%)
  starting transfers between devices  194 us (30%)
  waiting for transfers between devices  24.4 us (4%)
    ppermute x49, starting transfers between devices, shifted(): lax.ppermute(value, axis, [(source, source + steps) for source in range(f...  145 us
    scatter-add x4, other arithmetic, on_device(): matchforce = jnp.zeros((2, local_blocks, 128), jnp.float32).at[:, flat_so...  118 us
    add x4, other arithmetic, on_device(): relaxed = relaxed + 0.8 * (spring + matchforce) / diag  56.3 us
    reshape x8, local copies, waits for them, and re-layouts, on_device(): blocked = relaxed.reshape(2, local_blocks, 128)  55.2 us
    ppermute x6, starting transfers between devices, extended(): after = lax.ppermute(first, axis, down)  36.2 us
    slice x4, local copies, waits for them, and re-layouts, on_device(): right = jnp.concatenate([relaxed[..., 1:], zero_col], axis=-1)  32.3 us
    ppermute x49, waiting for transfers between devices, shifted(): lax.ppermute(value, axis, [(source, source + steps) for source in range(f...  24.3 us
    reshape x4, local copies, waits for them, and re-layouts, on_device(): matchforce = matchforce.reshape(2, sections, rows, width)  19.5 us
  transfers between devices with their start and end apart: 61, of which 7 were waited for; matrix products, arithmetic and copies ran while one was open for 42% of the time, Pallas kernels for 0%

commit v1 on v0

v1 whole, which is shorter than its diff:
```python
import jax
import jax.numpy as jnp
from jax import lax
from jax.experimental import pallas as pl
from jax.experimental.pallas import tpu as pltpu
from jax.sharding import PartitionSpec as P

ITERS = 4
SEC = 16
ROW = 16
WID = 2048
LANE = 128
COLS = WID // LANE
CAP = 32
SEG = 3 * CAP
ROWS_MSG = 2 * SEC * COLS
T_MSG = ROWS_MSG + 2 * SEG

VM = pl.BlockSpec(memory_space=pltpu.VMEM)
SM = pl.BlockSpec(memory_space=pltpu.SMEM)


def vmem(*shape):
    return pltpu.VMEM(shape, jnp.float32)


def kernel_call(body, outs, n_smem, n_vmem, aliases=None, scratch=(), cost=0):
    return pl.pallas_call(
        body,
        out_shape=tuple(outs),
        in_specs=[SM] * n_smem + [VM] * n_vmem,
        out_specs=tuple(VM for _ in outs),
        scratch_shapes=list(scratch),
        input_output_aliases=aliases or {},
        compiler_params=pltpu.CompilerParams(vmem_limit_bytes=4 * 2**20),
        cost_estimate=pl.CostEstimate(flops=cost, bytes_accessed=cost, transcendentals=0),
        name=body.__name__,
    )


def swaps(count, first):
    pairs = [(i, i + 1) for i in range(first, count - 1, 2)]
    return pairs + [(j, i) for i, j in pairs]


def exchange(to_a, to_b, axis):
    count = lax.axis_size(axis)
    from_b = lax.ppermute(to_b, axis, swaps(count, 1))
    from_a = lax.ppermute(to_a, axis, swaps(count, 0))
    return from_a, from_b


def place(block):
    return (block >> 8) & 15, block & 15, (block >> 4) & 15


def lanes(j):
    return slice(j * LANE, (j + 1) * LANE)


def iota(dim):
    return lax.broadcasted_iota(jnp.int32, (ROW, LANE), dim)


def setup_kernel(src, weight, keep, kr_in, kd_in, kr_ref, kd_ref, dg_ref, rim_ref):
    lane, row = iota(1), iota(0)
    kept = keep[0]

    def section(s, _):
        before = jnp.zeros((ROW, LANE), jnp.float32)
        for j in range(COLS):
            kr = kr_in[s, :, lanes(j)]
            if j == COLS - 1:
                kr = jnp.where(lane == LANE - 1, 0.0, kr)
            kr_ref[s, j] = kr
            turned = pltpu.roll(kr, 1, 1)
            left = jnp.where(lane == 0, before, turned)
            before = turned
            kd = kd_in[s, :, lanes(j)]
            inner = jnp.where(row == ROW - 1, 0.0, kd)
            kd_ref[s, j] = inner
            down = jnp.where(row == ROW - 1, kd * kept, kd)
            rim_ref[pl.ds(j * SEC + s, 1), :] = down[ROW - 1 :, :]
            dg_ref[s, j] = 1.0 + kr + left + down + pltpu.roll(inner, 1, 0)
        return 0

    lax.fori_loop(0, SEC, section, 0)

    def slots(i, _):
        for j in range(8):
            s, c, r = place(src[i * 8 + j])
            dg_ref[s, c, pl.ds(r, 1), :] += weight[i * 8 + j]
        return 0

    lax.fori_loop(0, 9 * CAP // 8, slots, 0)


def load_kernel(field_in, u_ref):
    def section(s, _):
        for m in range(2):
            for j in range(COLS):
                u_ref[m, s, j] = field_in[m, s, :, lanes(j)]
        return 0

    lax.fori_loop(0, SEC, section, 0)


def coefficient_kernel(src, weight, parity, dg_in, got_a, got_b, rim, cc_ref, ca_ref, cb_ref, cw_ref):
    odd = parity[0] == 1

    def column(j, _):
        at = pl.ds(pl.multiple_of(j * SEC, SEC), SEC)
        upper = jnp.where(odd, got_a[at, :], got_b[at, :])
        cc_ref[:, j, 0, :] = dg_in[:, j, 0, :] + upper
        cc_ref[:, j, 1:, :] = dg_in[:, j, 1:, :]
        return 0

    lax.fori_loop(0, COLS, column, 0)

    def section(s, _):
        for j in range(COLS):
            cc_ref[s, j] = 0.8 / cc_ref[s, j]
        return 0

    lax.fori_loop(0, SEC, section, 0)

    def rims(j, _):
        at = pl.ds(pl.multiple_of(j * SEC, SEC), SEC)
        first = cc_ref[:, j, 0, :] * jnp.where(odd, got_a[at, :], got_b[at, :])
        last = cc_ref[:, j, ROW - 1, :] * rim[at, :]
        ca_ref[at, :] = jnp.where(odd, first, last)
        cb_ref[at, :] = jnp.where(odd, last, first)
        return 0

    lax.fori_loop(0, COLS, rims, 0)

    def slots(i, _):
        for j in range(8):
            k = i * 8 + j
            s, c, r = place(src[k])
            cw_ref[pl.ds(k, 1), :] = cc_ref[s, c, pl.ds(r, 1), :] * weight[k]
        return 0

    lax.fori_loop(0, 9 * CAP // 8, slots, 0)


def pack_blocks(wanted, start, count, u_ref, msg_ref, at, stride):
    def slots(i, _):
        for j in range(8):
            k = i * 8 + j
            s, c, r = place(wanted[start + k])
            for m in range(2):
                msg_ref[pl.ds(at + m * stride + k, 1), :] = u_ref[m, s, c, pl.ds(r, 1), :]
        return 0

    lax.fori_loop(0, count // 8, slots, 0)


def each_rows(fn):
    def column(j, _):
        for m in range(2):
            fn(m, j, pl.ds(pl.multiple_of((m * COLS + j) * SEC, SEC), SEC))
        return 0

    lax.fori_loop(0, COLS, column, 0)


def pack_messages(wanted, parity, u_ref, a_ref, b_ref):
    def rows(row_a, row_b):
        def copy(m, j, at):
            a_ref[at, :] = u_ref[m, :, j, row_a, :]
            b_ref[at, :] = u_ref[m, :, j, row_b, :]

        each_rows(copy)

    pl.when(parity[0] == 0)(lambda: rows(ROW - 1, 0))
    pl.when(parity[0] == 1)(lambda: rows(0, ROW - 1))
    pack_blocks(wanted, 0, SEG, u_ref, a_ref, ROWS_MSG, SEG)
    pack_blocks(wanted, SEG, SEG, u_ref, b_ref, ROWS_MSG, SEG)


def pack_kernel(wanted, parity, u_ref, a_ref, b_ref):
    pack_messages(wanted, parity, u_ref, a_ref, b_ref)


def terms(blocks, fraction, scale):
    return scale * (blocks + fraction * (pltpu.roll(blocks, LANE - 1, 1) - blocks))


def scatter(src, start, count, u_ref, term_ref, stride):
    def slots(i, _):
        for j in range(8):
            k = i * 8 + j
            s, c, r = place(src[start + k])
            for m in range(2):
                u_ref[m, s, c, pl.ds(r, 1), :] += term_ref[pl.ds(m * stride + k, 1), :]
        return 0

    lax.fori_loop(0, count // 8, slots, 0)


LOCAL = 4 * CAP


def dense_kernel(src, local_target, wanted_sec, u_in, kr_ref, kd_ref, cc_ref, cw_ref, frac_ref, u_ref, own_a, own_b, term_ref):
    lane = iota(1)

    def section(s, _):
        for m in range(2):
            load = lambda j: u_in[m, s, j]
            here = load(0)
            here_turned = pltpu.roll(here, LANE - 1, 1)
            before = jnp.zeros((ROW, LANE), jnp.float32)
            for j in range(COLS):
                kr = kr_ref[s, j]
                kd = kd_ref[s, j]
                cc = cc_ref[s, j]
                if j + 1 < COLS:
                    after = load(j + 1)
                    after_turned = pltpu.roll(after, LANE - 1, 1)
                    right = jnp.where(lane == LANE - 1, after_turned, here_turned)
                else:
                    after, after_turned, right = None, None, here_turned
                turned = pltpu.roll(kr * here, 1, 1)
                total = here + kr * right + jnp.where(lane == 0, before, turned)
                total = total + kd * pltpu.roll(here, ROW - 1, 0) + pltpu.roll(kd * here, 1, 0)
                u_ref[m, s, j] = 0.2 * here + cc * total
                here, here_turned, before = after, after_turned, turned
        return 0

    lax.fori_loop(0, SEC, section, 0)
    pack_blocks(local_target, 0, CAP, u_in, term_ref, 0, CAP)
    fraction = frac_ref[...]
    scale = cw_ref[pl.ds(LOCAL, CAP), :]
    for m in range(2):
        at = pl.ds(m * CAP, CAP)
        term_ref[at, :] = terms(term_ref[at, :], fraction, scale)
    scatter(src, LOCAL, CAP, u_ref, term_ref, CAP)
    pack_blocks(wanted_sec, 0, CAP, u_in, own_a, 0, CAP)
    pack_blocks(wanted_sec, CAP, CAP, u_in, own_b, 0, CAP)


def relay_kernel(from_a, from_b, own_a, own_b, a_ref, b_ref):
    for m in range(2):
        for out, own, seg in ((a_ref, own_a, 0), (b_ref, own_b, 2)):
            there = ROWS_MSG + m * SEG + seg * CAP
            out[pl.ds(m * SEG, CAP), :] = from_a[pl.ds(there, CAP), :]
            out[pl.ds(m * SEG + CAP, CAP), :] = own[pl.ds(m * CAP, CAP), :]
            out[pl.ds(m * SEG + 2 * CAP, CAP), :] = from_b[pl.ds(there, CAP), :]


def tile_kernel(src, parity, u_in, from_a, from_b, ca_ref, cb_ref, cw_ref, frac_ref, u_ref, term_ref):
    def rows(row_a, row_b):
        def add(m, j, at):
            own = pl.ds(pl.multiple_of(j * SEC, SEC), SEC)
            u_ref[m, :, j, row_a, :] += ca_ref[own, :] * from_a[at, :]
            u_ref[m, :, j, row_b, :] += cb_ref[own, :] * from_b[at, :]

        each_rows(add)

    pl.when(parity[0] == 0)(lambda: rows(ROW - 1, 0))
    pl.when(parity[0] == 1)(lambda: rows(0, ROW - 1))
    fraction = frac_ref[...]
    for message, start in ((from_a, SEG), (from_b, SEG + 2 * CAP)):
        scale = cw_ref[pl.ds(start, CAP), :]
        for m in range(2):
            blocks = message[pl.ds(ROWS_MSG + m * SEG + CAP, CAP), :]
            term_ref[pl.ds(m * CAP, CAP), :] = terms(blocks, fraction, scale)
        scatter(src, start, CAP, u_ref, term_ref, CAP)


def section_adds(src, from_a, from_b, cw_ref, frac_ref, u_ref, term_ref):
    fraction = frac_ref[...]
    for message, start in ((from_a, 0), (from_b, 2 * SEG)):
        scale = cw_ref[pl.ds(start, SEG), :]
        for m in range(2):
            at = pl.ds(m * SEG, SEG)
            term_ref[at, :] = terms(message[at, :], fraction, scale)
        scatter(src, start, SEG, u_ref, term_ref, SEG)


def finish_kernel(src, wanted, parity, u_in, from_a, from_b, cw_ref, frac_ref, u_ref, a_ref, b_ref, term_ref):
    section_adds(src, from_a, from_b, cw_ref, frac_ref, u_ref, term_ref)
    pack_messages(wanted, parity, u_ref, a_ref, b_ref)


def last_kernel(src, u_in, from_a, from_b, cw_ref, frac_ref, u_ref, out_ref, term_ref, held_ref, sem):
    section_adds(src, from_a, from_b, cw_ref, frac_ref, u_ref, term_ref)

    def section(s, _):
        for m in range(2):
            for j in range(COLS):
                held_ref[m, s, :, lanes(j)] = u_ref[m, s, j]
            pltpu.make_async_copy(held_ref.at[m, s], out_ref.at[m, s], sem).start()
        return 0

    lax.fori_loop(0, SEC, section, 0)
    pltpu.make_async_copy(held_ref, out_ref, sem).wait()


def on_device(
    displacement,
    stiff_right,
    stiff_down,
    bilinear,
    match_source,
    match_target,
    match_count,
    match_weight,
):
    sec_count, tile_count = lax.axis_size("sec"), lax.axis_size("tile")
    sec, tile = lax.axis_index("sec"), lax.axis_index("tile")
    offset = jnp.arange(3, dtype=jnp.int32) - 1
    owner_sec, owner_tile = sec + offset, tile + offset
    valid = ((owner_sec >= 0) & (owner_sec < sec_count))[:, None] & (
        (owner_tile >= 0) & (owner_tile < tile_count)
    )[None, :]
    live = (jnp.arange(CAP, dtype=jnp.int32) < match_count[0][:, :, None]) & valid[:, :, None]

    def ordered(array):
        array = jnp.where(sec % 2 == 0, array[::-1], array)
        return jnp.where(tile % 2 == 0, array[:, ::-1], array)

    source = ordered(match_source[0]).reshape(-1)
    target = ordered(match_target[0])
    weight = ordered(jnp.where(live, match_weight[0], 0.0)).reshape(-1)
    parity = (tile % 2).astype(jnp.int32).reshape(1)
    keep = jnp.where(tile == tile_count - 1, 0.0, 1.0).astype(jnp.float32).reshape(1)
    fraction = jnp.where(jnp.arange(LANE) == LANE - 1, 0.0, bilinear).reshape(1, LANE)

    grid = (SEC, COLS, ROW, LANE)
    field = (2,) + grid
    rims = SEC * COLS
    asked_a, asked_b = exchange(target[0], target[2], "sec")
    kr, kd, dg, rim = kernel_call(setup_kernel, [vmem(*grid), vmem(*grid), vmem(*grid), vmem(rims, LANE)], 3, 2, cost=20_000_000)(
        source, weight, keep, stiff_right, stiff_down
    )
    (u,) = kernel_call(load_kernel, [vmem(*field)], 0, 1, cost=2_000_000)(displacement)

    def request(e):
        asked = jnp.concatenate([asked_a[e], target[1, e], asked_b[e]]).astype(jnp.float32)
        asked = jnp.pad(asked.reshape(1, SEG), ((0, 7), (0, LANE - SEG)))
        return jnp.concatenate([rim, asked], axis=0)

    got_a, got_b = exchange(request(0), request(2), "tile")
    wanted = jnp.concatenate([got_a[rims, :SEG], got_b[rims, :SEG]]).astype(jnp.int32)
    wanted_sec = jnp.concatenate([asked_a[1], asked_b[1]])
    cc, ca, cb, cw = kernel_call(
        coefficient_kernel, [vmem(*grid), vmem(rims, LANE), vmem(rims, LANE), vmem(9 * CAP, LANE)], 3, 4, cost=10_000_000
    )(source, weight, parity, dg, got_a, got_b, rim)

    messages = [vmem(T_MSG, LANE), vmem(T_MSG, LANE)]
    to_a, to_b = kernel_call(pack_kernel, messages, 2, 1, cost=1_000_000)(wanted, parity, u)
    local_target = target[1, 1]
    for step in range(ITERS):
        tile_a, tile_b = exchange(to_a, to_b, "tile")
        v, own_a, own_b = kernel_call(
            dense_kernel,
            [vmem(*field), vmem(2 * CAP, LANE), vmem(2 * CAP, LANE)],
            3,
            6,
            scratch=[vmem(2 * CAP, LANE)],
            cost=20_000_000,
        )(source, local_target, wanted_sec, u, kr, kd, cc, cw, fraction)
        sec_to_a, sec_to_b = kernel_call(relay_kernel, [vmem(2 * SEG, LANE)] * 2, 0, 4, cost=200_000)(
            tile_a, tile_b, own_a, own_b
        )
        sec_a, sec_b = exchange(sec_to_a, sec_to_b, "sec")
        (v,) = kernel_call(
            tile_kernel, [vmem(*field)], 2, 7, aliases={2: 0}, scratch=[vmem(2 * CAP, LANE)], cost=2_000_000
        )(source, parity, v, tile_a, tile_b, ca, cb, cw, fraction)
        if step + 1 < ITERS:
            u, to_a, to_b = kernel_call(
                finish_kernel, [vmem(*field)] + messages, 3, 5, aliases={3: 0}, scratch=[vmem(2 * SEG, LANE)], cost=2_000_000
            )(source, wanted, parity, v, sec_a, sec_b, cw, fraction)
        else:
            _, out = pl.pallas_call(
                last_kernel,
                out_shape=(vmem(*field), jax.ShapeDtypeStruct(displacement.shape, jnp.float32)),
                in_specs=[SM] + [VM] * 5,
                out_specs=(VM, pl.BlockSpec(memory_space=pl.ANY)),
                scratch_shapes=[vmem(2 * SEG, LANE), vmem(2, SEC, ROW, WID), pltpu.SemaphoreType.DMA],
                input_output_aliases={1: 0},
                compiler_params=pltpu.CompilerParams(vmem_limit_bytes=8 * 2**20),
            )(source, v, sec_a, sec_b, cw, fraction)
    return out


def solution(mesh):
    in_specs = (
        P(None, "sec", "tile", None),
        P("sec", "tile", None),
        P("sec", "tile", None),
        P(),
        P(("sec", "tile"), None, None, None),
        P(("sec", "tile"), None, None, None),
        P(("sec", "tile"), None, None),
        P(("sec", "tile"), None, None, None),
    )
    out_specs = P(None, "sec", "tile", None)
    return jax.shard_map(
        on_device, mesh=mesh, in_specs=in_specs, out_specs=out_specs, check_vma=False
    )
```

time: 639 us -> 121 us (0.19)
  the two profiles are of different devices: /device:TPU:6 before, /device:TPU:7 now
where the time goes in v1:
time: 121 us
  starting transfers between devices  53.9 us (45%)
  Pallas kernels  46 us (38%)
  waiting for transfers between devices  13.5 us (11%)
  local copies, waits for them, and re-layouts  5.84 us (5%)
  other arithmetic  1.22 us (1%)
    ppermute x10, starting transfers between devices, exchange(): from_b = lax.ppermute(to_b, axis, swaps(count, 1))  50.7 us
    pallas_call x4, Pallas kernels, on_device(): kernel_call(dense_kernel, [vmem(*field), vmem(2 * CAP, LANE), vmem(2 * CA...  18.3 us
    ppermute x10, waiting for transfers between devices, exchange(): from_b = lax.ppermute(to_b, axis, swaps(count, 1))  13.5 us
    pallas_call x3, Pallas kernels, on_device(): kernel_call(finish_kernel, [vmem(*field)] + messages, 3, 5, aliases={3: 0...  8.47 us
    pallas_call x4, Pallas kernels, on_device(): kernel_call(tile_kernel, [vmem(*field)], 2, 7, aliases={2: 0}, scratch=[v...  7.1 us
    unnamed x11, local copies, waits for them, and re-layouts  5.55 us
    pallas_call x1, Pallas kernels, on_device(): pl.pallas_call(last_kernel, out_shape=(vmem(*field), jax.ShapeDtypeStruct...  3.68 us
    pallas_call x1, Pallas kernels, on_device(): kernel_call(setup_kernel, [vmem(*grid), vmem(*grid), vmem(*grid), vmem(ri...  3.63 us
  transfers between devices with their start and end apart: 20, of which 9 were waited for; matrix products, arithmetic and copies ran while one was open for 2% of the time, Pallas kernels for 27%

profile of v1, /device:TPU:7, one launch (start us, length us, event | category | flops | bytes accessed | tf_op | source)
XLA Modules:
  0.0 120.9 jit_solution(145815292759424509)
XLA Ops:
  0.0 0.7 copy.26
  0.7 0.7 copy.25
  1.4 0.8 collective-permute-start
  2.2 4.7 %collective-permute-start.1 = (s32[3,32]{1,0:T(4,128)S(1)}, s32[3,32]{1,0:T(4,128)S(1)}, u32[]{:S(2)}, u32[]{:S(2)}) collective-permute-start(s32[3,32]{1,0:T(4,128)S(1)} %get-tuple-element.91), channel_id=1, source_target_pairs={{32,64},{64,32},{33,65},{65,33},{34,66},{66,34},{35,67},{67,35},{3... | collective-permute-start | bytes 1160 | tf_op jit(solution)/shard_map/ppermute | solution.py:48
  7.0 0.7 copy.27
  7.7 0.8 bitcast_select_fusion
  8.5 0.1 reshape.141.weight
  8.6 0.1 reshape.139.src
  8.7 1.7 %copy-done.1 = f32[16,16,2048]{2,1,0:T(8,128)S(1)} copy-done((f32[16,16,2048]{2,1,0:T(8,128)S(1)}, f32[16,16,2048]{2,1,0:T(8,128)}, u32[]{:S(2)}) %copy-start.1) | copy-done | bytes 2097176
  10.5 1.7 %copy-done.2 = f32[16,16,2048]{2,1,0:T(8,128)S(1)} copy-done((f32[16,16,2048]{2,1,0:T(8,128)S(1)}, f32[16,16,2048]{2,1,0:T(8,128)}, u32[]{:S(2)}) %copy-start.2) | copy-done | bytes 2097176
  12.2 3.6 %setup_kernel.1 = (f32[16,16,16,128]{3,2,1,0:T(8,128)S(1)}, f32[16,16,16,128]{3,2,1,0:T(8,128)S(1)}, f32[16,16,16,128]{3,2,1,0:T(8,128)S(1)}, f32[256,128]{1,0:T(8,128)S(1)}) custom-call(s32[288]{0:T(512)S(1)} %reshape.139.src, f32[288]{0:T(512)S(1)} %reshape.141.weight, f32[1]{0:T(128)} %bitcast.6.keep, f32[16,16,2048]{2,1,0:T(8,128)S(1)} %copy-done.1, ...), custom_call_target="tpu_custom_call" | custom-call | flops 20000000 | bytes 20000000 | tf_op jit(solution)/shard_map/setup_kernel/pallas_call | solution.py:335
  16.1 1.7 %collective-permute-start.2 = (f32[264,128]{1,0:T(8,128)S(1)}, f32[264,128]{1,0:T(8,128)S(1)}, u32[]{:S(2)}, u32[]{:S(2)}) collective-permute-start(f32[264,128]{1,0:T(8,128)S(1)} %get-tuple-element.85), channel_id=1, source_target_pairs={{0,1},{2,3},{4,5},{6,7},{8,9},{10,11},{12,13},{14,15},{16,17},{18,... | collective-permute-start | bytes 405512 | tf_op jit(solution)/shard_map/ppermute | solution.py:49
  17.8 0.3 load_kernel.1.u_in.u_ref
  18.1 4.5 %collective-permute-start.3 = (f32[264,128]{1,0:T(8,128)S(1)}, f32[264,128]{1,0:T(8,128)S(1)}, u32[]{:S(2)}, u32[]{:S(2)}) collective-permute-start(f32[264,128]{1,0:T(8,128)S(1)} %get-tuple-element.86), channel_id=1, source_target_pairs={{1,2},{3,4},{5,6},{7,8},{9,10},{11,12},{13,14},{15,16},{17,18},{19... | collective-permute-start | bytes 405512 | tf_op jit(solution)/shard_map/ppermute | solution.py:48
  22.7 4.2 %collective-permute-done.3.got_b = f32[264,128]{1,0:T(8,128)S(1)} collective-permute-done((f32[264,128]{1,0:T(8,128)S(1)}, f32[264,128]{1,0:T(8,128)S(1)}, u32[]{:S(2)}, u32[]{:S(2)}) %collective-permute-start.3) | collective-permute-done | bytes 135200 | tf_op jit(solution)/shard_map/ppermute | solution.py:48
  27.0 1.6 %pack_kernel.1 = (f32[704,128]{1,0:T(8,128)S(1)}, f32[704,128]{1,0:T(8,128)S(1)}) custom-call(s32[192]{0:T(256)S(1)} %maximum_convert_fusion.wanted, s32[1]{0:T(128)} %bitcast.parity, f32[2,16,16,16,128]{4,3,2,1,0:T(8,128)S(1)} %load_kernel.1.u_in.u_ref), custom_call_target="tpu_custom_call" | custom-call | flops 1000000 | bytes 1000000 | tf_op jit(solution)/shard_map/pack_kernel/pallas_call | solution.py:353
  28.6 0.1 collective-permute-start.4
  28.7 4.5 %collective-permute-start.5 = (f32[704,128]{1,0:T(8,128)S(1)}, f32[704,128]{1,0:T(8,128)S(1)}, u32[]{:S(2)}, u32[]{:S(2)}) collective-permute-start(f32[704,128]{1,0:T(8,128)S(1)} %get-tuple-element.53), channel_id=1, source_target_pairs={{1,2},{3,4},{5,6},{7,8},{9,10},{11,12},{13,14},{15,16},{17,18},{19... | collective-permute-start | bytes 1081352 | tf_op jit(solution)/shard_map/ppermute | solution.py:48
  33.3 2.8 %coefficient_kernel.1 = (f32[16,16,16,128]{3,2,1,0:T(8,128)S(1)}, f32[256,128]{1,0:T(8,128)S(1)}, f32[256,128]{1,0:T(8,128)S(1)}, f32[288,128]{1,0:T(8,128)S(1)}) custom-call(s32[288]{0:T(512)S(1)} %reshape.139.src, f32[288]{0:T(512)S(1)} %reshape.141.weight, s32[1]{0:T(128)} %bitcast.parity, f32[16,16,16,128]{3,2,1,0:T(8,128)S(1)} %get-tuple-element.48.dg_in, ...), custom_call_target="tpu_custom_call" | custom-call | flops 10000000 | bytes 10000000 | tf_op jit(solution)/shard_map/coefficient_kernel/pallas_call | solution.py:348
  36.1 4.6 %dense_kernel.4 = (f32[2,16,16,16,128]{4,3,2,1,0:T(8,128)S(1)}, f32[64,128]{1,0:T(8,128)S(1)}, f32[64,128]{1,0:T(8,128)S(1)}) custom-call(s32[288]{0:T(512)S(1)} %reshape.139.src, s32[32]{0:T(128)S(1)} %get-tuple-element.89.local_target, s32[64]{0:T(128)S(1)} %pad_add_fusion.wanted_sec, f32[2,16,16,16,128]{4,3,2,1,0:T(8,128)S(1)} %load_kernel.1.u_in.u_ref, ...), custom_call_target="tpu_custom_call" | custom-call | flops 20000000 | bytes 20000000 | tf_op jit(solution)/shard_map/dense_kernel/pallas_call | solution.py:357
  40.7 0.9 collective-permute-done.5.from_b
  41.7 4.7 %collective-permute-start.7 = (f32[192,128]{1,0:T(8,128)S(1)}, f32[192,128]{1,0:T(8,128)S(1)}, u32[]{:S(2)}, u32[]{:S(2)}) collective-permute-start(f32[192,128]{1,0:T(8,128)S(1)} %get-tuple-element.59), channel_id=1, source_target_pairs={{32,64},{64,32},{33,65},{65,33},{34,66},{66,34},{35,67},{67,35},{3... | collective-permute-start | bytes 294920 | tf_op jit(solution)/shard_map/ppermute | solution.py:48
  46.4 1.8 %tile_kernel.4.u_in = f32[2,16,16,16,128]{4,3,2,1,0:T(8,128)S(1)} custom-call(s32[288]{0:T(512)S(1)} %reshape.139.src, s32[1]{0:T(128)} %bitcast.parity, f32[2,16,16,16,128]{4,3,2,1,0:T(8,128)S(1)} %get-tuple-element.51.u_in, f32[704,128]{1,0:T(8,128)S(1)} %collective-permute-done.4.from_a, ...), custom_call_target="tpu_custom_call", output_to_operand_aliasing={{}: (2, {})} | custom-call | flops 2000000 | bytes 2000000 | tf_op jit(solution)/shard_map/tile_kernel/pallas_call | solution.py:369
  48.2 0.9 collective-permute-done.7.from_b
  49.1 2.8 %finish_kernel.3 = (f32[2,16,16,16,128]{4,3,2,1,0:T(8,128)S(1)}, f32[704,128]{1,0:T(8,128)S(1)}, f32[704,128]{1,0:T(8,128)S(1)}) custom-call(s32[288]{0:T(512)S(1)} %reshape.139.src, s32[192]{0:T(256)S(1)} %maximum_convert_fusion.wanted, s32[1]{0:T(128)} %bitcast.parity, ...), custom_call_target="tpu_custom_call", output_to_operand_aliasing={{0}: (3, {})} | custom-call | flops 2000000 | bytes 2000000 | tf_op jit(solution)/shard_map/finish_kernel/pallas_call | solution.py:373
  52.0 0.1 collective-permute-start.8
  52.1 5.4 %collective-permute-start.9 = (f32[704,128]{1,0:T(8,128)S(1)}, f32[704,128]{1,0:T(8,128)S(1)}, u32[]{:S(2)}, u32[]{:S(2)}) collective-permute-start(f32[704,128]{1,0:T(8,128)S(1)} %get-tuple-element.63), channel_id=1, source_target_pairs={{1,2},{3,4},{5,6},{7,8},{9,10},{11,12},{13,14},{15,16},{17,18},{19... | collective-permute-start | bytes 1081352 | tf_op jit(solution)/shard_map/ppermute | solution.py:48
  57.5 4.6 %dense_kernel.5 = (f32[2,16,16,16,128]{4,3,2,1,0:T(8,128)S(1)}, f32[64,128]{1,0:T(8,128)S(1)}, f32[64,128]{1,0:T(8,128)S(1)}) custom-call(s32[288]{0:T(512)S(1)} %reshape.139.src, s32[32]{0:T(128)S(1)} %get-tuple-element.89.local_target, s32[64]{0:T(128)S(1)} %pad_add_fusion.wanted_sec, f32[2,16,16,16,128]{4,3,2,1,0:T(8,128)S(1)} %get-tuple-element.60.u_in, ...), custom_call_target="tpu_custom_call" | custom-call | flops 20000000 | bytes 20000000 | tf_op jit(solution)/shard_map/dense_kernel/pallas_call | solution.py:357
  62.1 1.1 collective-permute-done.9.from_b
  63.4 5.9 %collective-permute-start.11 = (f32[192,128]{1,0:T(8,128)S(1)}, f32[192,128]{1,0:T(8,128)S(1)}, u32[]{:S(2)}, u32[]{:S(2)}) collective-permute-start(f32[192,128]{1,0:T(8,128)S(1)} %get-tuple-element.67), channel_id=1, source_target_pairs={{32,64},{64,32},{33,65},{65,33},{34,66},{66,34},{35,67},{67,35},{3... | collective-permute-start | bytes 294920 | tf_op jit(solution)/shard_map/ppermute | solution.py:48
  69.3 1.8 %tile_kernel.5.u_in = f32[2,16,16,16,128]{4,3,2,1,0:T(8,128)S(1)} custom-call(s32[288]{0:T(512)S(1)} %reshape.139.src, s32[1]{0:T(128)} %bitcast.parity, f32[2,16,16,16,128]{4,3,2,1,0:T(8,128)S(1)} %get-tuple-element.61.u_in, f32[704,128]{1,0:T(8,128)S(1)} %collective-permute-done.8.from_a, ...), custom_call_target="tpu_custom_call", output_to_operand_aliasing={{}: (2, {})} | custom-call | flops 2000000 | bytes 2000000 | tf_op jit(solution)/shard_map/tile_kernel/pallas_call | solution.py:369
  71.1 0.5 collective-permute-done.11.from_b
  71.6 2.8 %finish_kernel.4 = (f32[2,16,16,16,128]{4,3,2,1,0:T(8,128)S(1)}, f32[704,128]{1,0:T(8,128)S(1)}, f32[704,128]{1,0:T(8,128)S(1)}) custom-call(s32[288]{0:T(512)S(1)} %reshape.139.src, s32[192]{0:T(256)S(1)} %maximum_convert_fusion.wanted, s32[1]{0:T(128)} %bitcast.parity, ...), custom_call_target="tpu_custom_call", output_to_operand_aliasing={{0}: (3, {})} | custom-call | flops 2000000 | bytes 2000000 | tf_op jit(solution)/shard_map/finish_kernel/pallas_call | solution.py:373
  74.5 4.6 %collective-permute-start.13 = (f32[704,128]{1,0:T(8,128)S(1)}, f32[704,128]{1,0:T(8,128)S(1)}, u32[]{:S(2)}, u32[]{:S(2)}) collective-permute-start(f32[704,128]{1,0:T(8,128)S(1)} %get-tuple-element.71), channel_id=1, source_target_pairs={{1,2},{3,4},{5,6},{7,8},{9,10},{11,12},{13,14},{15,16},{17,18},{19... | collective-permute-start | bytes 1081352 | tf_op jit(solution)/shard_map/ppermute | solution.py:48
  79.2 4.6 %dense_kernel.6 = (f32[2,16,16,16,128]{4,3,2,1,0:T(8,128)S(1)}, f32[64,128]{1,0:T(8,128)S(1)}, f32[64,128]{1,0:T(8,128)S(1)}) custom-call(s32[288]{0:T(512)S(1)} %reshape.139.src, s32[32]{0:T(128)S(1)} %get-tuple-element.89.local_target, s32[64]{0:T(128)S(1)} %pad_add_fusion.wanted_sec, f32[2,16,16,16,128]{4,3,2,1,0:T(8,128)S(1)} %get-tuple-element.68.u_in, ...), custom_call_target="tpu_custom_call" | custom-call | flops 20000000 | bytes 20000000 | tf_op jit(solution)/shard_map/dense_kernel/pallas_call | solution.py:357
  83.8 2.0 %collective-permute-done.13.from_b = f32[704,128]{1,0:T(8,128)S(1)} collective-permute-done((f32[704,128]{1,0:T(8,128)S(1)}, f32[704,128]{1,0:T(8,128)S(1)}, u32[]{:S(2)}, u32[]{:S(2)}) %collective-permute-start.13) | collective-permute-done | bytes 360480 | tf_op jit(solution)/shard_map/ppermute | solution.py:48
  85.9 6.2 %collective-permute-start.15 = (f32[192,128]{1,0:T(8,128)S(1)}, f32[192,128]{1,0:T(8,128)S(1)}, u32[]{:S(2)}, u32[]{:S(2)}) collective-permute-start(f32[192,128]{1,0:T(8,128)S(1)} %get-tuple-element.75), channel_id=1, source_target_pairs={{32,64},{64,32},{33,65},{65,33},{34,66},{66,34},{35,67},{67,35},{3... | collective-permute-start | bytes 294920 | tf_op jit(solution)/shard_map/ppermute | solution.py:48
  92.1 1.8 %tile_kernel.6.u_in = f32[2,16,16,16,128]{4,3,2,1,0:T(8,128)S(1)} custom-call(s32[288]{0:T(512)S(1)} %reshape.139.src, s32[1]{0:T(128)} %bitcast.parity, f32[2,16,16,16,128]{4,3,2,1,0:T(8,128)S(1)} %get-tuple-element.69.u_in, f32[704,128]{1,0:T(8,128)S(1)} %collective-permute-done.12.from_a, ...), custom_call_target="tpu_custom_call", output_to_operand_aliasing={{}: (2, {})} | custom-call | flops 2000000 | bytes 2000000 | tf_op jit(solution)/shard_map/tile_kernel/pallas_call | solution.py:369
  93.9 0.5 collective-permute-done.15.from_b
  94.4 2.8 %finish_kernel.5 = (f32[2,16,16,16,128]{4,3,2,1,0:T(8,128)S(1)}, f32[704,128]{1,0:T(8,128)S(1)}, f32[704,128]{1,0:T(8,128)S(1)}) custom-call(s32[288]{0:T(512)S(1)} %reshape.139.src, s32[192]{0:T(256)S(1)} %maximum_convert_fusion.wanted, s32[1]{0:T(128)} %bitcast.parity, ...), custom_call_target="tpu_custom_call", output_to_operand_aliasing={{0}: (3, {})} | custom-call | flops 2000000 | bytes 2000000 | tf_op jit(solution)/shard_map/finish_kernel/pallas_call | solution.py:373
  97.2 0.1 collective-permute-start.16
  97.3 3.8 %collective-permute-start.17 = (f32[704,128]{1,0:T(8,128)S(1)}, f32[704,128]{1,0:T(8,128)S(1)}, u32[]{:S(2)}, u32[]{:S(2)}) collective-permute-start(f32[704,128]{1,0:T(8,128)S(1)} %get-tuple-element.79), channel_id=1, source_target_pairs={{1,2},{3,4},{5,6},{7,8},{9,10},{11,12},{13,14},{15,16},{17,18},{19... | collective-permute-start | bytes 1081352 | tf_op jit(solution)/shard_map/ppermute | solution.py:48
  101.2 4.6 %dense_kernel.7 = (f32[2,16,16,16,128]{4,3,2,1,0:T(8,128)S(1)}, f32[64,128]{1,0:T(8,128)S(1)}, f32[64,128]{1,0:T(8,128)S(1)}) custom-call(s32[288]{0:T(512)S(1)} %reshape.139.src, s32[32]{0:T(128)S(1)} %get-tuple-element.89.local_target, s32[64]{0:T(128)S(1)} %pad_add_fusion.wanted_sec, f32[2,16,16,16,128]{4,3,2,1,0:T(8,128)S(1)} %get-tuple-element.76.u_in, ...), custom_call_target="tpu_custom_call" | custom-call | flops 20000000 | bytes 20000000 | tf_op jit(solution)/shard_map/dense_kernel/pallas_call | solution.py:357
  105.8 2.8 %collective-permute-done.17.from_b = f32[704,128]{1,0:T(8,128)S(1)} collective-permute-done((f32[704,128]{1,0:T(8,128)S(1)}, f32[704,128]{1,0:T(8,128)S(1)}, u32[]{:S(2)}, u32[]{:S(2)}) %collective-permute-start.17) | collective-permute-done | bytes 360480 | tf_op jit(solution)/shard_map/ppermute | solution.py:48
  108.7 6.2 %collective-permute-start.19 = (f32[192,128]{1,0:T(8,128)S(1)}, f32[192,128]{1,0:T(8,128)S(1)}, u32[]{:S(2)}, u32[]{:S(2)}) collective-permute-start(f32[192,128]{1,0:T(8,128)S(1)} %get-tuple-element.83), channel_id=1, source_target_pairs={{32,64},{64,32},{33,65},{65,33},{34,66},{66,34},{35,67},{67,35},{3... | collective-permute-start | bytes 294920 | tf_op jit(solution)/shard_map/ppermute | solution.py:48
  114.9 1.8 %tile_kernel.7.u_in = f32[2,16,16,16,128]{4,3,2,1,0:T(8,128)S(1)} custom-call(s32[288]{0:T(512)S(1)} %reshape.139.src, s32[1]{0:T(128)} %bitcast.parity, f32[2,16,16,16,128]{4,3,2,1,0:T(8,128)S(1)} %get-tuple-element.77.u_in, f32[704,128]{1,0:T(8,128)S(1)} %collective-permute-done.16.from_a, ...), custom_call_target="tpu_custom_call", output_to_operand_aliasing={{}: (2, {})} | custom-call | flops 2000000 | bytes 2000000 | tf_op jit(solution)/shard_map/tile_kernel/pallas_call | solution.py:369
  116.7 0.5 collective-permute-done.19.from_b
  117.2 3.7 %shard_map.82 = (f32[2,16,16,16,128]{4,3,2,1,0:T(8,128)S(1)}, f32[2,16,16,2048]{3,2,1,0:T(8,128)}) custom-call(s32[288]{0:T(512)S(1)} %reshape.139.src, f32[2,16,16,16,128]{4,3,2,1,0:T(8,128)S(1)} %tile_kernel.7.u_in, f32[192,128]{1,0:T(8,128)S(1)} %collective-permute-done.18.from_a, ...), custom_call_target="tpu_custom_call", output_to_operand_aliasing={{0}: (1, {})} | custom-call | tf_op jit(solution)/shard_map/pallas_call | solution.py:377
  (48 shorter events, 1.1 us)
Async XLA Ops:
  1.4 14.4 %collective-permute-start = (s32[3,32]{1,0:T(4,128)S(1)}, s32[3,32]{1,0:T(4,128)S(1)}, u32[]{:S(2)}, u32[]{:S(2)}) collective-permute-start(s32[3,32]{1,0:T(4,128)S(1)} %get-tuple-element.90), channel_id=1, source_target_pairs={{0,32},{64,96},{32,0},{96,64},{1,33},{65,97},{33,1},{97,65},{2,34}... | collective-permute-start | bytes 1160 | tf_op jit(solution)/shard_map/ppermute | solution.py:49
  2.2 13.7 %collective-permute-start.1 = (s32[3,32]{1,0:T(4,128)S(1)}, s32[3,32]{1,0:T(4,128)S(1)}, u32[]{:S(2)}, u32[]{:S(2)}) collective-permute-start(s32[3,32]{1,0:T(4,128)S(1)} %get-tuple-element.91), channel_id=1, source_target_pairs={{32,64},{64,32},{33,65},{65,33},{34,66},{66,34},{35,67},{67,35},{3... | collective-permute-start | bytes 1160 | tf_op jit(solution)/shard_map/ppermute | solution.py:48
  8.7 9.1 %copy-start = (f32[2,16,16,2048]{3,2,1,0:T(8,128)S(1)}, f32[2,16,16,2048]{3,2,1,0:T(8,128)}, u32[]{:S(2)}) copy-start(f32[2,16,16,2048]{3,2,1,0:T(8,128)} %field_in.1) | copy-start | bytes 12582916
  8.7 1.7 %copy-start.1 = (f32[16,16,2048]{2,1,0:T(8,128)S(1)}, f32[16,16,2048]{2,1,0:T(8,128)}, u32[]{:S(2)}) copy-start(f32[16,16,2048]{2,1,0:T(8,128)} %kr_in.1) | copy-start | bytes 6291460
  10.5 1.7 %copy-start.2 = (f32[16,16,2048]{2,1,0:T(8,128)S(1)}, f32[16,16,2048]{2,1,0:T(8,128)}, u32[]{:S(2)}) copy-start(f32[16,16,2048]{2,1,0:T(8,128)} %kd_in.1) | copy-start | bytes 6291460
  16.1 6.6 %collective-permute-start.2 = (f32[264,128]{1,0:T(8,128)S(1)}, f32[264,128]{1,0:T(8,128)S(1)}, u32[]{:S(2)}, u32[]{:S(2)}) collective-permute-start(f32[264,128]{1,0:T(8,128)S(1)} %get-tuple-element.85), channel_id=1, source_target_pairs={{0,1},{2,3},{4,5},{6,7},{8,9},{10,11},{12,13},{14,15},{16,17},{18,... | collective-permute-start | bytes 405512 | tf_op jit(solution)/shard_map/ppermute | solution.py:49
  18.1 15.1 %copy-start.3 = (f32[128]{0:T(128)S(1)}, f32[128]{0:T(128)}, u32[]{:S(2)}) copy-start(f32[128]{0:T(128)} %param.11) | copy-start | bytes 1540
  18.1 8.8 %collective-permute-start.3 = (f32[264,128]{1,0:T(8,128)S(1)}, f32[264,128]{1,0:T(8,128)S(1)}, u32[]{:S(2)}, u32[]{:S(2)}) collective-permute-start(f32[264,128]{1,0:T(8,128)S(1)} %get-tuple-element.86), channel_id=1, source_target_pairs={{1,2},{3,4},{5,6},{7,8},{9,10},{11,12},{13,14},{15,16},{17,18},{19... | collective-permute-start | bytes 405512 | tf_op jit(solution)/shard_map/ppermute | solution.py:48
  28.6 12.1 %collective-permute-start.4 = (f32[704,128]{1,0:T(8,128)S(1)}, f32[704,128]{1,0:T(8,128)S(1)}, u32[]{:S(2)}, u32[]{:S(2)}) collective-permute-start(f32[704,128]{1,0:T(8,128)S(1)} %get-tuple-element.52), channel_id=1, source_target_pairs={{0,1},{2,3},{4,5},{6,7},{8,9},{10,11},{12,13},{14,15},{16,17},{18,... | collective-permute-start | bytes 1081352 | tf_op jit(solution)/shard_map/ppermute | solution.py:49
  28.7 12.9 %collective-permute-start.5 = (f32[704,128]{1,0:T(8,128)S(1)}, f32[704,128]{1,0:T(8,128)S(1)}, u32[]{:S(2)}, u32[]{:S(2)}) collective-permute-start(f32[704,128]{1,0:T(8,128)S(1)} %get-tuple-element.53), channel_id=1, source_target_pairs={{1,2},{3,4},{5,6},{7,8},{9,10},{11,12},{13,14},{15,16},{17,18},{19... | collective-permute-start | bytes 1081352 | tf_op jit(solution)/shard_map/ppermute | solution.py:48
  41.6 6.6 %collective-permute-start.6 = (f32[192,128]{1,0:T(8,128)S(1)}, f32[192,128]{1,0:T(8,128)S(1)}, u32[]{:S(2)}, u32[]{:S(2)}) collective-permute-start(f32[192,128]{1,0:T(8,128)S(1)} %get-tuple-element.58), channel_id=1, source_target_pairs={{0,32},{64,96},{32,0},{96,64},{1,33},{65,97},{33,1},{97,65},{2,34}... | collective-permute-start | bytes 294920 | tf_op jit(solution)/shard_map/ppermute | solution.py:49
  41.7 7.4 %collective-permute-start.7 = (f32[192,128]{1,0:T(8,128)S(1)}, f32[192,128]{1,0:T(8,128)S(1)}, u32[]{:S(2)}, u32[]{:S(2)}) collective-permute-start(f32[192,128]{1,0:T(8,128)S(1)} %get-tuple-element.59), channel_id=1, source_target_pairs={{32,64},{64,32},{33,65},{65,33},{34,66},{66,34},{35,67},{67,35},{3... | collective-permute-start | bytes 294920 | tf_op jit(solution)/shard_map/ppermute | solution.py:48
  52.0 10.1 %collective-permute-start.8 = (f32[704,128]{1,0:T(8,128)S(1)}, f32[704,128]{1,0:T(8,128)S(1)}, u32[]{:S(2)}, u32[]{:S(2)}) collective-permute-start(f32[704,128]{1,0:T(8,128)S(1)} %get-tuple-element.62), channel_id=1, source_target_pairs={{0,1},{2,3},{4,5},{6,7},{8,9},{10,11},{12,13},{14,15},{16,17},{18,... | collective-permute-start | bytes 1081352 | tf_op jit(solution)/shard_map/ppermute | solution.py:49
  52.1 11.2 %collective-permute-start.9 = (f32[704,128]{1,0:T(8,128)S(1)}, f32[704,128]{1,0:T(8,128)S(1)}, u32[]{:S(2)}, u32[]{:S(2)}) collective-permute-start(f32[704,128]{1,0:T(8,128)S(1)} %get-tuple-element.63), channel_id=1, source_target_pairs={{1,2},{3,4},{5,6},{7,8},{9,10},{11,12},{13,14},{15,16},{17,18},{19... | collective-permute-start | bytes 1081352 | tf_op jit(solution)/shard_map/ppermute | solution.py:48
  63.3 7.8 %collective-permute-start.10 = (f32[192,128]{1,0:T(8,128)S(1)}, f32[192,128]{1,0:T(8,128)S(1)}, u32[]{:S(2)}, u32[]{:S(2)}) collective-permute-start(f32[192,128]{1,0:T(8,128)S(1)} %get-tuple-element.66), channel_id=1, source_target_pairs={{0,32},{64,96},{32,0},{96,64},{1,33},{65,97},{33,1},{97,65},{2,34}... | collective-permute-start | bytes 294920 | tf_op jit(solution)/shard_map/ppermute | solution.py:49
  63.4 8.2 %collective-permute-start.11 = (f32[192,128]{1,0:T(8,128)S(1)}, f32[192,128]{1,0:T(8,128)S(1)}, u32[]{:S(2)}, u32[]{:S(2)}) collective-permute-start(f32[192,128]{1,0:T(8,128)S(1)} %get-tuple-element.67), channel_id=1, source_target_pairs={{32,64},{64,32},{33,65},{65,33},{34,66},{66,34},{35,67},{67,35},{3... | collective-permute-start | bytes 294920 | tf_op jit(solution)/shard_map/ppermute | solution.py:48
  74.4 9.3 %collective-permute-start.12 = (f32[704,128]{1,0:T(8,128)S(1)}, f32[704,128]{1,0:T(8,128)S(1)}, u32[]{:S(2)}, u32[]{:S(2)}) collective-permute-start(f32[704,128]{1,0:T(8,128)S(1)} %get-tuple-element.70), channel_id=1, source_target_pairs={{0,1},{2,3},{4,5},{6,7},{8,9},{10,11},{12,13},{14,15},{16,17},{18,... | collective-permute-start | bytes 1081352 | tf_op jit(solution)/shard_map/ppermute | solution.py:49
  74.5 11.3 %collective-permute-start.13 = (f32[704,128]{1,0:T(8,128)S(1)}, f32[704,128]{1,0:T(8,128)S(1)}, u32[]{:S(2)}, u32[]{:S(2)}) collective-permute-start(f32[704,128]{1,0:T(8,128)S(1)} %get-tuple-element.71), channel_id=1, source_target_pairs={{1,2},{3,4},{5,6},{7,8},{9,10},{11,12},{13,14},{15,16},{17,18},{19... | collective-permute-start | bytes 1081352 | tf_op jit(solution)/shard_map/ppermute | solution.py:48
  85.8 8.1 %collective-permute-start.14 = (f32[192,128]{1,0:T(8,128)S(1)}, f32[192,128]{1,0:T(8,128)S(1)}, u32[]{:S(2)}, u32[]{:S(2)}) collective-permute-start(f32[192,128]{1,0:T(8,128)S(1)} %get-tuple-element.74), channel_id=1, source_target_pairs={{0,32},{64,96},{32,0},{96,64},{1,33},{65,97},{33,1},{97,65},{2,34}... | collective-permute-start | bytes 294920 | tf_op jit(solution)/shard_map/ppermute | solution.py:49
  85.9 8.5 %collective-permute-start.15 = (f32[192,128]{1,0:T(8,128)S(1)}, f32[192,128]{1,0:T(8,128)S(1)}, u32[]{:S(2)}, u32[]{:S(2)}) collective-permute-start(f32[192,128]{1,0:T(8,128)S(1)} %get-tuple-element.75), channel_id=1, source_target_pairs={{32,64},{64,32},{33,65},{65,33},{34,66},{66,34},{35,67},{67,35},{3... | collective-permute-start | bytes 294920 | tf_op jit(solution)/shard_map/ppermute | solution.py:48
  97.2 8.5 %collective-permute-start.16 = (f32[704,128]{1,0:T(8,128)S(1)}, f32[704,128]{1,0:T(8,128)S(1)}, u32[]{:S(2)}, u32[]{:S(2)}) collective-permute-start(f32[704,128]{1,0:T(8,128)S(1)} %get-tuple-element.78), channel_id=1, source_target_pairs={{0,1},{2,3},{4,5},{6,7},{8,9},{10,11},{12,13},{14,15},{16,17},{18,... | collective-permute-start | bytes 1081352 | tf_op jit(solution)/shard_map/ppermute | solution.py:49
  97.3 11.3 %collective-permute-start.17 = (f32[704,128]{1,0:T(8,128)S(1)}, f32[704,128]{1,0:T(8,128)S(1)}, u32[]{:S(2)}, u32[]{:S(2)}) collective-permute-start(f32[704,128]{1,0:T(8,128)S(1)} %get-tuple-element.79), channel_id=1, source_target_pairs={{1,2},{3,4},{5,6},{7,8},{9,10},{11,12},{13,14},{15,16},{17,18},{19... | collective-permute-start | bytes 1081352 | tf_op jit(solution)/shard_map/ppermute | solution.py:48
  108.6 8.1 %collective-permute-start.18 = (f32[192,128]{1,0:T(8,128)S(1)}, f32[192,128]{1,0:T(8,128)S(1)}, u32[]{:S(2)}, u32[]{:S(2)}) collective-permute-start(f32[192,128]{1,0:T(8,128)S(1)} %get-tuple-element.82), channel_id=1, source_target_pairs={{0,32},{64,96},{32,0},{96,64},{1,33},{65,97},{33,1},{97,65},{2,34}... | collective-permute-start | bytes 294920 | tf_op jit(solution)/shard_map/ppermute | solution.py:49
  108.7 8.5 %collective-permute-start.19 = (f32[192,128]{1,0:T(8,128)S(1)}, f32[192,128]{1,0:T(8,128)S(1)}, u32[]{:S(2)}, u32[]{:S(2)}) collective-permute-start(f32[192,128]{1,0:T(8,128)S(1)} %get-tuple-element.83), channel_id=1, source_target_pairs={{32,64},{64,32},{33,65},{65,33},{34,66},{66,34},{35,67},{67,35},{3... | collective-permute-start | bytes 294920 | tf_op jit(solution)/shard_map/ppermute | solution.py:48

commit v2 on v0

v2 whole, which is shorter than its diff:
```python
import jax
import jax.numpy as jnp
from jax import lax
from jax.experimental import pallas as pl
from jax.experimental.pallas import tpu as pltpu
from jax.sharding import PartitionSpec as P

ITERS = 4
SEC = 16
ROW = 16
WID = 2048
LANE = 128
COLS = WID // LANE
CAP = 32
SEG = 3 * CAP
SECTION = COLS * ROW
PART = SEC * SECTION
PAD = 8
FIELD = 2 * PART + 2 * PAD
RIM = SEC * COLS
INNER = SEC - 2
ROW_MSG = 2 * INNER * COLS
EDGE = 2 * SEG
T_MSG = EDGE + 4 * COLS

VM = pl.BlockSpec(memory_space=pltpu.VMEM)
SM = pl.BlockSpec(memory_space=pltpu.SMEM)
HB = pl.BlockSpec(memory_space=pltpu.HBM)


def vmem(*shape):
    return pltpu.VMEM(shape, jnp.float32)


def kernel_call(body, outs, in_specs, aliases=None, scratch=(), cost=0, out_specs=None, limit=4):
    return pl.pallas_call(
        body,
        out_shape=tuple(outs),
        in_specs=in_specs,
        out_specs=out_specs or tuple(VM for _ in outs),
        scratch_shapes=list(scratch),
        input_output_aliases=aliases or {},
        compiler_params=pltpu.CompilerParams(vmem_limit_bytes=limit * 2**20),
        cost_estimate=pl.CostEstimate(flops=cost, bytes_accessed=cost, transcendentals=0),
        name=body.__name__,
    )


def pairing(axis, first):
    secs, tiles = lax.axis_size("sec"), lax.axis_size("tile")
    partner = {}
    for s in range(secs):
        for t in range(tiles):
            at, size = (t, tiles) if axis == "tile" else (s, secs)
            other = at + 1 if (at - first) % 2 == 0 else at - 1
            if axis == "tile":
                to = (s, other) if 0 <= other < size else (s ^ 1, t)
            else:
                to = (other, t) if 0 <= other < size else (s, t ^ 1)
            partner[s * tiles + t] = to[0] * tiles + to[1]
    return list(partner.items())


def exchange(to_a, to_b, axis):
    from_b = lax.ppermute(to_b, ("sec", "tile"), pairing(axis, 1))
    from_a = lax.ppermute(to_a, ("sec", "tile"), pairing(axis, 0))
    return from_a, from_b


def flat(block):
    return (block & 3840) | ((block & 15) << 4) | ((block >> 4) & 15)


def lanes(j):
    return slice(j * LANE, (j + 1) * LANE)


def iota(dim):
    return lax.broadcasted_iota(jnp.int32, (ROW, LANE), dim)


def loop(stop, body, step=1):
    def run(i, carry):
        body(i)
        return carry

    lax.fori_loop(0, stop, run, 0)


def live_slots(count, body):
    def group(i):
        for j in range(4):
            body(i * 4 + j)

    loop((count + 3) // 4, group)


def setup_kernel(
    first, after, keep, u_in, kr_in, kd_in, u_ref, kr_ref, kd_ref, dg_ref, a_ref, b_ref, kr_buf, kd_buf, sems
):
    lane, row = iota(1), iota(0)
    kept = keep[0]
    chunk = 4

    def copies(i):
        part = pl.ds(i * chunk, chunk)
        return (
            pltpu.make_async_copy(kr_in.at[part], kr_buf.at[part], sems.at[0, i]),
            pltpu.make_async_copy(kd_in.at[part], kd_buf.at[part], sems.at[1, i]),
        )

    for i in range(SEC // chunk):
        for copy in copies(i):
            copy.start()
    pack_rows(first, u_ref, a_ref, b_ref)
    kd_ref[pl.ds(0, PAD), :] = jnp.zeros((PAD, LANE), jnp.float32)

    def section(s):
        before = jnp.zeros((ROW, LANE), jnp.float32)
        for j in range(COLS):
            at = pl.multiple_of(s * SECTION + j * ROW, ROW)
            kr = kr_buf[s, :, lanes(j)]
            if j == COLS - 1:
                kr = jnp.where(lane == LANE - 1, 0.0, kr)
            kr_ref[pl.ds(at, ROW), :] = kr
            turned = pltpu.roll(kr, 1, 1)
            left = jnp.where(lane == 0, before, turned)
            before = turned
            kd = kd_buf[s, :, lanes(j)]
            inner = jnp.where(row == ROW - 1, 0.0, kd)
            kd_ref[pl.ds(at + PAD, ROW), :] = inner
            down = jnp.where(row == ROW - 1, kd * kept, kd)
            dg_ref[pl.ds(at, ROW), :] = 1.0 + kr + left + down + pltpu.roll(inner, 1, 0)

    for i in range(SEC // chunk):
        for copy in copies(i):
            copy.wait()
        loop(chunk, lambda s: section(s + i * chunk))


def row_at(m, s, row):
    return pl.ds(PAD + m * PART + s * SECTION + row, COLS, stride=ROW)


def cols_at(m, s):
    return pl.ds(pl.multiple_of((m * INNER + s - 1) * COLS, COLS), COLS)


def edge_at(m, q):
    return pl.ds(EDGE + (m * 2 + q) * COLS, COLS)


def first_row(first):
    return jnp.where(first[1] == 2, ROW - 1, 0)


def pack_rows(first, u_ref, a_ref, b_ref):
    row_a = first_row(first)

    def section(i):
        for m in range(2):
            a_ref[cols_at(m, i + 1), :] = u_ref[row_at(m, i + 1, row_a), :]
            b_ref[cols_at(m, i + 1), :] = u_ref[row_at(m, i + 1, ROW - 1 - row_a), :]

    loop(INNER, section)


def load_kernel(keep, field_in, kd_in, u_ref, rim_ref, buf, rim_buf, sems):
    chunk = 4

    def copies(i):
        part = pl.ds(i * chunk, chunk)
        return [pltpu.make_async_copy(field_in.at[m, part], buf.at[m, part], sems.at[m, i]) for m in range(2)]

    rim_copy = pltpu.make_async_copy(kd_in.at[:, ROW - 1], rim_buf, sems.at[2, 0])
    rim_copy.start()
    for i in range(SEC // chunk):
        for copy in copies(i):
            copy.start()
    zero = jnp.zeros((PAD, LANE), jnp.float32)
    u_ref[pl.ds(0, PAD), :] = zero
    u_ref[pl.ds(FIELD - PAD, PAD), :] = zero
    rim_copy.wait()
    kept = keep[0]
    for j in range(COLS):
        rim_ref[pl.ds(j, SEC, stride=COLS), :] = rim_buf[:, lanes(j)] * kept

    def section(s):
        for m in range(2):
            for j in range(COLS):
                at = pl.multiple_of(PAD + m * PART + s * SECTION + j * ROW, 8)
                u_ref[pl.ds(at, ROW), :] = buf[m, s, :, lanes(j)]

    for i in range(SEC // chunk):
        for copy in copies(i):
            copy.wait()
        loop(chunk, lambda s: section(s + i * chunk))


def diagonal_kernel(src, weight, count, dg_in, u_in, dg_ref, u_ref, cc_ref):
    for a in range(3):
        for e in range(3):
            number = count[0, a, e]

            def slot(k):
                at = pl.ds(src[0, a, e, k], 1)
                dg_ref[at, :] += jnp.where(k < number, weight[0, a, e, k], 0.0)

            live_slots(number, slot)

    def section(s):
        for j in range(COLS):
            at = pl.ds(pl.multiple_of(s * SECTION + j * ROW, ROW), ROW)
            cc_ref[at, :] = 0.8 / dg_ref[at, :]

    loop(SEC, section)


def coefficient_kernel(
    src, weight, count, first, dg_ref, got_a, got_b, rim, cc_in, u_in, cc_ref, u_ref, ca_ref, cb_ref, cw_ref
):
    even = first[1] == 2

    def rims(s):
        own = pl.ds(pl.multiple_of(s * COLS, COLS), COLS)
        top = pl.ds(s * SECTION, COLS, stride=ROW)
        upper = jnp.where(first[2] == 1, jnp.where(even, got_b[own, :], got_a[own, :]), 0.0)
        scale = 0.8 / (dg_ref[top, :] + upper)
        cc_ref[top, :] = scale
        upper = scale * upper
        lower = cc_ref[pl.ds(s * SECTION + ROW - 1, COLS, stride=ROW), :] * rim[own, :]
        ca_ref[own, :] = jnp.where(even, lower, upper)
        cb_ref[own, :] = jnp.where(even, upper, lower)

    loop(SEC, rims)
    for i, a in enumerate((first[0], 1, 2 - first[0])):
        for j, e in enumerate((first[1], 1, 2 - first[1])):
            number = count[0, a, e]

            def slot(k):
                value = cc_ref[pl.ds(src[0, a, e, k], 1), :]
                cw_ref[pl.ds((i * 3 + j) * CAP + k, 1), :] = value * jnp.where(k < number, weight[0, a, e, k], 0.0)

            live_slots(number, slot)


def pack_blocks(wanted, count, u_ref, msg_ref, at, stride):
    def group(i):
        for j in range(8):
            k = i * 8 + j
            block = wanted(k) + PAD
            for m in range(2):
                msg_ref[pl.ds(at + m * stride + k, 1), :] = u_ref[pl.ds(block + m * PART, 1), :]

    loop(count // 8, group)


def pack_messages(wanted, first, u_ref, a_ref, b_ref):
    row_a = first_row(first)
    pack_blocks(lambda k: wanted[k], SEG, u_ref, a_ref, 0, SEG)
    pack_blocks(lambda k: wanted[SEG + k], SEG, u_ref, b_ref, 0, SEG)
    for m in range(2):
        for q, s in enumerate((0, SEC - 1)):
            a_ref[edge_at(m, q), :] = u_ref[row_at(m, s, row_a), :]
            b_ref[edge_at(m, q), :] = u_ref[row_at(m, s, ROW - 1 - row_a), :]


def pack_kernel(wanted, first, u_in, u_ref, a_ref, b_ref):
    pack_messages(wanted, first, u_ref, a_ref, b_ref)


def terms(blocks, fraction, scale):
    return scale * (blocks + fraction * (pltpu.roll(blocks, LANE - 1, 1) - blocks))


def scatter(src, count, a, e, u_ref, term_ref, at, stride):
    def slot(k):
        block = src[0, a, e, k] + PAD
        places = [pl.ds(block + m * PART, 1) for m in range(2)]
        old = [u_ref[place, :] for place in places]
        add = [term_ref[pl.ds(at + m * stride + k, 1), :] for m in range(2)]
        for m in range(2):
            u_ref[places[m], :] = old[m] + add[m]

    live_slots(count[0, a, e], slot)


LOCAL = 4 * CAP


def dense_kernel(src, count, wanted_sec, u_in, kr_ref, kd_ref, cc_ref, cw_ref, frac_ref, u_ref, own_a, own_b, term_ref):
    lane = iota(1)
    zero = jnp.zeros((PAD, LANE), jnp.float32)
    u_ref[pl.ds(0, PAD), :] = zero
    u_ref[pl.ds(FIELD - PAD, PAD), :] = zero

    def section(s):
        def at(m, j, shift=0):
            return pl.ds(PAD + m * PART + s * SECTION + j * ROW + shift, ROW)

        here = [u_in[at(m, 0), :] for m in range(2)]
        here_turned = [pltpu.roll(x, LANE - 1, 1) for x in here]
        before = [jnp.zeros((ROW, LANE), jnp.float32)] * 2
        for j in range(COLS):
            own = pl.ds(s * SECTION + j * ROW, ROW)
            kr = kr_ref[own, :]
            kd = kd_ref[at(0, j), :]
            ku = kd_ref[at(0, j, -1), :]
            cc = cc_ref[own, :]
            for m in range(2):
                x = here[m]
                if j + 1 < COLS:
                    after = u_in[at(m, j + 1), :]
                    after_turned = pltpu.roll(after, LANE - 1, 1)
                    right = jnp.where(lane == LANE - 1, after_turned, here_turned[m])
                else:
                    after, after_turned, right = None, None, here_turned[m]
                turned = pltpu.roll(kr * x, 1, 1)
                total = x + kr * right + jnp.where(lane == 0, before[m], turned)
                total = total + kd * u_in[at(m, j, 1), :] + ku * u_in[at(m, j, -1), :]
                u_ref[at(m, j), :] = 0.2 * x + cc * total
                here[m], here_turned[m], before[m] = after, after_turned, turned

    loop(SEC, section)
    pack_blocks(lambda k: src[1, 1, 1, k], CAP, u_in, term_ref, 0, CAP)
    fraction = frac_ref[...]
    scale = cw_ref[pl.ds(LOCAL, CAP), :]
    for m in range(2):
        at = pl.ds(m * CAP, CAP)
        term_ref[at, :] = terms(term_ref[at, :], fraction, scale)
    scatter(src, count, 1, 1, u_ref, term_ref, 0, CAP)
    pack_blocks(lambda k: wanted_sec[k], CAP, u_in, own_a, 0, CAP)
    pack_blocks(lambda k: wanted_sec[CAP + k], CAP, u_in, own_b, 0, CAP)


def relay_kernel(from_a, from_b, own_a, own_b, a_ref, b_ref):
    for m in range(2):
        for out, own, seg in ((a_ref, own_a, 0), (b_ref, own_b, 2)):
            there = m * SEG + seg * CAP
            out[pl.ds(m * SEG, CAP), :] = from_a[pl.ds(there, CAP), :]
            out[pl.ds(m * SEG + CAP, CAP), :] = own[pl.ds(m * CAP, CAP), :]
            out[pl.ds(m * SEG + 2 * CAP, CAP), :] = from_b[pl.ds(there, CAP), :]


def tile_adds(src, count, first, from_a, from_b, rows_a, rows_b, ca_ref, cb_ref, cw_ref, frac_ref, u_ref, term_ref):
    row_a = first_row(first)

    def add(s, message_a, message_b, at):
        own = pl.ds(s * COLS, COLS)
        for m in range(2):
            u_ref[row_at(m, s, row_a), :] += ca_ref[own, :] * message_a[at(m), :]
            u_ref[row_at(m, s, ROW - 1 - row_a), :] += cb_ref[own, :] * message_b[at(m), :]

    loop(INNER, lambda i: add(i + 1, rows_a, rows_b, lambda m: cols_at(m, i + 1)))
    for q, s in enumerate((0, SEC - 1)):
        add(s, from_a, from_b, lambda m: edge_at(m, q))
    fraction = frac_ref[...]
    for message, start, e in ((from_a, SEG, first[1]), (from_b, SEG + 2 * CAP, 2 - first[1])):
        scale = cw_ref[pl.ds(start, CAP), :]
        for m in range(2):
            blocks = message[pl.ds(m * SEG + CAP, CAP), :]
            term_ref[pl.ds(m * CAP, CAP), :] = terms(blocks, fraction, scale)
        scatter(src, count, 1, e, u_ref, term_ref, 0, CAP)


def tile_kernel(
    src, count, first, u_in, from_a, from_b, rows_a, rows_b, ca_ref, cb_ref, cw_ref, frac_ref, u_ref, a_ref, b_ref, term_ref
):
    tile_adds(src, count, first, from_a, from_b, rows_a, rows_b, ca_ref, cb_ref, cw_ref, frac_ref, u_ref, term_ref)
    pack_rows(first, u_ref, a_ref, b_ref)


def last_tile_kernel(
    src, count, first, u_in, from_a, from_b, rows_a, rows_b, ca_ref, cb_ref, cw_ref, frac_ref, u_ref, term_ref
):
    tile_adds(src, count, first, from_a, from_b, rows_a, rows_b, ca_ref, cb_ref, cw_ref, frac_ref, u_ref, term_ref)


def section_adds(src, count, first, from_a, from_b, cw_ref, frac_ref, u_ref, term_ref):
    fraction = frac_ref[...]
    for message, start, a in ((from_a, 0, first[0]), (from_b, 2 * SEG, 2 - first[0])):
        scale = cw_ref[pl.ds(start, SEG), :]
        for m in range(2):
            at = pl.ds(m * SEG, SEG)
            term_ref[at, :] = terms(message[at, :], fraction, scale)
        for j, e in enumerate((first[1], 1, 2 - first[1])):
            scatter(src, count, a, e, u_ref, term_ref, j * CAP, SEG)


def finish_kernel(src, count, wanted, first, u_in, from_a, from_b, cw_ref, frac_ref, u_ref, a_ref, b_ref, term_ref):
    section_adds(src, count, first, from_a, from_b, cw_ref, frac_ref, u_ref, term_ref)
    pack_messages(wanted, first, u_ref, a_ref, b_ref)


def last_kernel(src, count, first, u_in, from_a, from_b, cw_ref, frac_ref, u_ref, out_ref, term_ref, held_ref, sem):
    section_adds(src, count, first, from_a, from_b, cw_ref, frac_ref, u_ref, term_ref)

    def section(s):
        for m in range(2):
            for j in range(COLS):
                at = pl.ds(pl.multiple_of(PAD + m * PART + s * SECTION + j * ROW, 8), ROW)
                held_ref[m, s, :, lanes(j)] = u_ref[at, :]
            pltpu.make_async_copy(held_ref.at[m, s], out_ref.at[m, s], sem).start()

    loop(SEC, section)
    pltpu.make_async_copy(held_ref, out_ref, sem).wait()


def on_device(
    displacement,
    stiff_right,
    stiff_down,
    bilinear,
    match_source,
    match_target,
    match_count,
    match_weight,
):
    tile_count = lax.axis_size("tile")
    sec, tile = lax.axis_index("sec"), lax.axis_index("tile")
    first = jnp.stack([2 - 2 * (sec % 2), 2 - 2 * (tile % 2), jnp.minimum(tile, 1)]).astype(jnp.int32)
    keep = jnp.where(tile == tile_count - 1, 0.0, 1.0).astype(jnp.float32).reshape(1)
    fraction = jnp.where(jnp.arange(LANE) == LANE - 1, 0.0, bilinear).reshape(1, LANE)

    displacement, stiff_right, stiff_down = (
        pltpu.with_memory_space_constraint(x, pltpu.HBM) for x in (displacement, stiff_right, stiff_down)
    )
    asked_a, asked_b = exchange(match_target, match_target, "sec")
    source = flat(jnp.concatenate([match_source, match_target]))
    asked_a, asked_b = flat(asked_a), flat(asked_b)
    rows = [vmem(ROW_MSG, LANE), vmem(ROW_MSG, LANE)]
    field = vmem(FIELD, LANE)
    u, rim = kernel_call(
        load_kernel,
        [field, vmem(RIM, LANE)],
        [SM, HB, HB],
        scratch=[vmem(2, SEC, ROW, WID), vmem(SEC, WID), pltpu.SemaphoreType.DMA((3, 4))],
        cost=6_000_000,
        limit=8,
    )(keep, displacement, stiff_down)

    def pick(array, a, e):
        return lax.dynamic_slice(array, (0, a, e, 0), (1, 1, 1, CAP)).reshape(CAP)

    def request(e):
        asked = jnp.concatenate([pick(asked_a, 2 - first[0], e), pick(source[1:], 1, e), pick(asked_b, first[0], e)])
        asked = jnp.pad(asked.astype(jnp.float32).reshape(1, SEG), ((0, 7), (0, LANE - SEG)))
        return jnp.concatenate([rim, asked], axis=0)

    got_a, got_b = exchange(request(first[1]), request(2 - first[1]), "tile")
    wanted = jnp.concatenate([got_a[RIM, :SEG], got_b[RIM, :SEG]]).astype(jnp.int32)
    wanted_sec = jnp.concatenate([pick(asked_a, 2 - first[0], 1), pick(asked_b, first[0], 1)])
    u, kr, kd, dg, rows_to_a, rows_to_b = kernel_call(
        setup_kernel,
        [field, vmem(PART, LANE), vmem(PART + 2 * PAD, LANE), vmem(PART, LANE), *rows],
        [SM, SM, SM, VM, HB, HB],
        aliases={3: 0},
        scratch=[vmem(SEC, ROW, WID), vmem(SEC, ROW, WID), pltpu.SemaphoreType.DMA((2, 4))],
        cost=6_000_000,
        limit=8,
    )(first, wanted_sec, keep, u, stiff_right, stiff_down)
    rows_a, rows_b = exchange(rows_to_a, rows_to_b, "tile")
    dg, u, cc = kernel_call(
        diagonal_kernel,
        [vmem(PART, LANE), field, vmem(PART, LANE)],
        [SM, SM, SM, VM, VM],
        aliases={3: 0, 4: 1},
        cost=4_000_000,
    )(source, match_weight, match_count, dg, u)
    messages = [vmem(T_MSG, LANE), vmem(T_MSG, LANE)]
    u, to_a, to_b = kernel_call(pack_kernel, [field, *messages], [SM, SM, VM], aliases={2: 0}, cost=1_000_000)(
        wanted, first, u
    )
    cc, u, ca, cb, cw = kernel_call(
        coefficient_kernel,
        [vmem(PART, LANE), field, vmem(RIM, LANE), vmem(RIM, LANE), vmem(9 * CAP, LANE)],
        [SM] * 4 + [VM] * 6,
        aliases={8: 0, 9: 1},
        cost=1_000_000,
    )(source, match_weight, match_count, first, dg, got_a, got_b, rim, cc, u)

    for step in range(ITERS):
        tile_a, tile_b = exchange(to_a, to_b, "tile")
        v, own_a, own_b = kernel_call(
            dense_kernel,
            [vmem(FIELD, LANE), vmem(2 * CAP, LANE), vmem(2 * CAP, LANE)],
            [SM] * 3 + [VM] * 6,
            scratch=[vmem(2 * CAP, LANE)],
            cost=20_000_000,
        )(source, match_count, wanted_sec, u, kr, kd, cc, cw, fraction)
        sec_to_a, sec_to_b = kernel_call(relay_kernel, [vmem(2 * SEG, LANE)] * 2, [VM] * 4, cost=200_000)(
            tile_a, tile_b, own_a, own_b
        )
        sec_a, sec_b = exchange(sec_to_a, sec_to_b, "sec")
        more = step + 1 < ITERS
        v, *rows_to = kernel_call(
            tile_kernel if more else last_tile_kernel,
            [vmem(FIELD, LANE)] + (rows if more else []),
            [SM] * 3 + [VM] * 9,
            aliases={3: 0},
            scratch=[vmem(2 * CAP, LANE)],
            cost=2_000_000,
        )(source, match_count, first, v, tile_a, tile_b, rows_a, rows_b, ca, cb, cw, fraction)
        if more:
            rows_a, rows_b = exchange(*rows_to, "tile")
        if step + 1 < ITERS:
            u, to_a, to_b = kernel_call(
                finish_kernel,
                [vmem(FIELD, LANE)] + messages,
                [SM] * 4 + [VM] * 5,
                aliases={4: 0},
                scratch=[vmem(2 * SEG, LANE)],
                cost=2_000_000,
            )(source, match_count, wanted, first, v, sec_a, sec_b, cw, fraction)
        else:
            _, out = kernel_call(
                last_kernel,
                [vmem(FIELD, LANE), jax.ShapeDtypeStruct(displacement.shape, jnp.float32)],
                [SM] * 3 + [VM] * 5,
                aliases={3: 0},
                scratch=[vmem(2 * SEG, LANE), vmem(2, SEC, ROW, WID), pltpu.SemaphoreType.DMA],
                cost=2_000_000,
                out_specs=(VM, HB),
                limit=8,
            )(source, match_count, first, v, sec_a, sec_b, cw, fraction)
    return out


def solution(mesh):
    in_specs = (
        P(None, "sec", "tile", None),
        P("sec", "tile", None),
        P("sec", "tile", None),
        P(),
        P(("sec", "tile"), None, None, None),
        P(("sec", "tile"), None, None, None),
        P(("sec", "tile"), None, None),
        P(("sec", "tile"), None, None, None),
    )
    out_specs = P(None, "sec", "tile", None)
    return jax.shard_map(
        on_device, mesh=mesh, in_specs=in_specs, out_specs=out_specs, check_vma=False
    )
```

time: 639 us -> 94.8 us (0.15)
  the two profiles are of different devices: /device:TPU:6 before, /device:TPU:7 now
where the time goes in v2:
time: 94.8 us; the launch traced here: 94.5 us
  Pallas kernels  47.1 us (50%)
  starting transfers between devices  37.7 us (40%)
  waiting for transfers between devices  7.44 us (8%)
  local copies, waits for them, and re-layouts  1.45 us (2%)
    ppermute x14, starting transfers between devices, exchange(): from_b = lax.ppermute(to_b, ('sec', 'tile'), pairing(axis, 1))  32.4 us
    pallas_call x4, Pallas kernels, on_device(): kernel_call(dense_kernel, [vmem(FIELD, LANE), vmem(2 * CAP, LANE), vmem(2...  19.1 us
    ppermute x14, waiting for transfers between devices, exchange(): from_b = lax.ppermute(to_b, ('sec', 'tile'), pairing(axis, 1))  7.4 us
    pallas_call x4, Pallas kernels, on_device(): kernel_call(tile_kernel if more else last_tile_kernel, [vmem(FIELD, LANE)...  7.29 us
    pallas_call x3, Pallas kernels, on_device(): kernel_call(finish_kernel, [vmem(FIELD, LANE)] + messages, [SM] * 4 + [VM...  6.03 us
    ppermute x14, starting transfers between devices, exchange(): from_a = lax.ppermute(to_a, ('sec', 'tile'), pairing(axis, 0))  5.3 us
    pallas_call x1, Pallas kernels, on_device(): kernel_call(last_kernel, [vmem(FIELD, LANE), jax.ShapeDtypeStruct(displac...  3.63 us
    pallas_call x1, Pallas kernels, on_device(): kernel_call(setup_kernel, [field, vmem(PART, LANE), vmem(PART + 2 * PAD,...  3.53 us
  transfers between devices with their start and end apart: 28, of which 6 were waited for; matrix products, arithmetic and copies ran while one was open for 2% of the time, Pallas kernels for 46%

profile of v2, /device:TPU:7, one launch (start us, length us, event | category | flops | bytes accessed | tf_op | source)
XLA Modules:
  0.0 94.5 jit_solution(9484580119983830914)
XLA Ops:
  0.0 0.7 collective-permute-start
  0.7 2.9 %collective-permute-start.1 = (s32[1,3,3,32]{3,0,2,1:T(1,128)}, s32[1,3,3,32]{3,0,2,1:T(1,128)S(1)}, u32[]{:S(2)}, u32[]{:S(2)}) collective-permute-start(s32[1,3,3,32]{3,0,2,1:T(1,128)} %param.13), channel_id=1, source_target_pairs={{0,1},{1,0},{2,3},{3,2},{4,5},{5,4},{6,7},{7,6},{8,9},{9,8},{10,11... | collective-permute-start | bytes 3464 | tf_op jit(solution)/shard_map/ppermute | solution.py:65
  3.6 0.7 constant_dynamic-update-slice_fusion.1
  4.3 0.7 constant_dynamic-update-slice_fusion
  5.0 2.4 %load_kernel.1 = (f32[8208,128]{1,0:T(8,128)S(1)}, f32[256,128]{1,0:T(8,128)S(1)}) custom-call(f32[1]{0:T(128)} %bitcast.5.keep, f32[2,16,16,2048]{3,2,1,0:T(8,128)} %field_in.1, f32[16,16,2048]{2,1,0:T(8,128)} %kd_in.3), custom_call_target="tpu_custom_call" | custom-call | flops 6000000 | bytes 6000000 | tf_op jit(solution)/shard_map/load_kernel/pallas_call | solution.py:433
  7.7 4.2 %collective-permute-start.3 = (f32[264,128]{1,0:T(8,128)S(1)}, f32[264,128]{1,0:T(8,128)S(1)}, u32[]{:S(2)}, u32[]{:S(2)}) collective-permute-start(f32[264,128]{1,0:T(8,128)S(1)} %get-tuple-element.122), channel_id=1, source_target_pairs={{0,32},{1,2},{2,1},{3,4},{4,3},{5,6},{6,5},{7,8},{8,7},{9,10},{10,... | collective-permute-start | bytes 405512 | tf_op jit(solution)/shard_map/ppermute | solution.py:65
  12.0 0.1 collective-permute-start.2
  12.1 3.5 %setup_kernel.1 = (f32[8208,128]{1,0:T(8,128)S(1)}, f32[4096,128]{1,0:T(8,128)S(1)}, f32[4112,128]{1,0:T(8,128)S(1)}, f32[4096,128]{1,0:T(8,128)S(1)}, f32[448,128]{1,0:T(8,128)S(1)}, /*index=5*/f32[448,128]{1,0:T(8,128)S(1)}) custom-call(s32[3]{0:T(128)S(1)} %pad_add_fusion.first, ...), custom_call_target="tpu_custom_call", output_to_operand_aliasing={{0}: (3, {})} | custom-call | flops 6000000 | bytes 6000000 | tf_op jit(solution)/shard_map/setup_kernel/pallas_call | solution.py:453
  15.7 1.5 %collective-permute-start.6 = (f32[448,128]{1,0:T(8,128)S(1)}, f32[448,128]{1,0:T(8,128)S(1)}, u32[]{:S(2)}, u32[]{:S(2)}) collective-permute-start(f32[448,128]{1,0:T(8,128)S(1)} %get-tuple-element.79), channel_id=1, source_target_pairs={{0,1},{1,0},{2,3},{3,2},{4,5},{5,4},{6,7},{7,6},{8,9},{9,8},{10,11... | collective-permute-start | bytes 688136 | tf_op jit(solution)/shard_map/ppermute | solution.py:66
  17.2 0.3 collective-permute-start.7
  17.6 2.1 %diagonal_kernel.1 = (f32[4096,128]{1,0:T(8,128)S(1)}, f32[8208,128]{1,0:T(8,128)S(1)}, f32[4096,128]{1,0:T(8,128)S(1)}) custom-call(s32[2,3,3,32]{3,2,1,0:T(4,128)S(1)} %and_or_fusion.src, f32[1,3,3,32]{3,2,1,0:T(4,128)S(1)} %copy.27.weight, s32[1,3,3]{2,1,0:T(4,128)S(1)} %copy.40.count, ...), custom_call_target="tpu_custom_call", output_to_operand_aliasing={{0}: (3, {}), {1}: (4, {})} | custom-call | flops 4000000 | bytes 4000000 | tf_op jit(solution)/shard_map/diagonal_kernel/pallas_call | solution.py:463
  19.8 0.9 pack_kernel.1
  20.8 4.4 %collective-permute-start.5 = (f32[256,128]{1,0:T(8,128)S(1)}, f32[256,128]{1,0:T(8,128)S(1)}, u32[]{:S(2)}, u32[]{:S(2)}) collective-permute-start(f32[256,128]{1,0:T(8,128)S(1)} %get-tuple-element.78), channel_id=1, source_target_pairs={{0,32},{1,2},{2,1},{3,4},{4,3},{5,6},{6,5},{7,8},{8,7},{9,10},{10,... | collective-permute-start | bytes 393224 | tf_op jit(solution)/shard_map/ppermute | solution.py:65
  25.2 2.0 %coefficient_kernel.1 = (f32[4096,128]{1,0:T(8,128)S(1)}, f32[8208,128]{1,0:T(8,128)S(1)}, f32[256,128]{1,0:T(8,128)S(1)}, f32[256,128]{1,0:T(8,128)S(1)}, f32[288,128]{1,0:T(8,128)S(1)}) custom-call(s32[2,3,3,32]{3,2,1,0:T(4,128)S(1)} %and_or_fusion.src, f32[1,3,3,32]{3,2,1,0:T(4,128)S(1)} %copy.27.weight, ...), custom_call_target="tpu_custom_call", output_to_operand_aliasing={{0}: (8, {}), {1}: (9, {})} | custom-call | flops 1000000 | bytes 1000000 | tf_op jit(solution)/shard_map/coefficient_kernel/pallas_call | solution.py:474
  27.2 4.8 %dense_kernel.4 = (f32[8208,128]{1,0:T(8,128)S(1)}, f32[64,128]{1,0:T(8,128)S(1)}, f32[64,128]{1,0:T(8,128)S(1)}) custom-call(s32[2,3,3,32]{3,2,1,0:T(4,128)S(1)} %and_or_fusion.src, s32[1,3,3]{2,1,0:T(4,128)S(1)} %copy.40.count, s32[64]{0:T(128)S(1)} %pad_add_fusion.1.after.wanted_sec, f32[8208,128]{1,0:T(8,128)S(1)} %get-tuple-element.71.u_in, ...), custom_call_target="tpu_custom_call" | custom-call | flops 20000000 | bytes 20000000 | tf_op jit(solution)/shard_map/dense_kernel/pallas_call | solution.py:484
  32.1 3.2 %collective-permute-start.9 = (f32[192,128]{1,0:T(8,128)S(1)}, f32[192,128]{1,0:T(8,128)S(1)}, u32[]{:S(2)}, u32[]{:S(2)}) collective-permute-start(f32[192,128]{1,0:T(8,128)S(1)} %get-tuple-element.87), channel_id=1, source_target_pairs={{0,1},{1,0},{2,3},{3,2},{4,5},{5,4},{6,7},{7,6},{8,9},{9,8},{10,11... | collective-permute-start | bytes 294920 | tf_op jit(solution)/shard_map/ppermute | solution.py:65
  35.3 1.9 %tile_kernel.3 = (f32[8208,128]{1,0:T(8,128)S(1)}, f32[448,128]{1,0:T(8,128)S(1)}, f32[448,128]{1,0:T(8,128)S(1)}) custom-call(s32[2,3,3,32]{3,2,1,0:T(4,128)S(1)} %and_or_fusion.src, s32[1,3,3]{2,1,0:T(4,128)S(1)} %copy.40.count, s32[3]{0:T(128)S(1)} %pad_add_fusion.first, f32[8208,128]{1,0:T(8,128)S(1)} %get-tuple-element.76.u_in, ...), custom_call_target="tpu_custom_call", output_to_operand_aliasing={{0}: (3, {})} | custom-call | flops 2000000 | bytes 2000000 | tf_op jit(solution)/shard_map/tile_kernel/pallas_call | solution.py:496
  37.2 0.1 collective-permute-start.12
  37.3 0.6 collective-permute-start.13
  37.9 2.0 %finish_kernel.3 = (f32[8208,128]{1,0:T(8,128)S(1)}, f32[256,128]{1,0:T(8,128)S(1)}, f32[256,128]{1,0:T(8,128)S(1)}) custom-call(s32[2,3,3,32]{3,2,1,0:T(4,128)S(1)} %and_or_fusion.src, s32[1,3,3]{2,1,0:T(4,128)S(1)} %copy.40.count, s32[192]{0:T(256)S(1)} %maximum_convert_fusion.wanted, s32[3]{0:T(128)S(1)} %pad_add_fusion.first, ...), custom_call_target="tpu_custom_call", output_to_operand_aliasing={{0}: (4, {})} | custom-call | flops 2000000 | bytes 2000000 | tf_op jit(solution)/shard_map/finish_kernel/pallas_call | solution.py:507
  39.9 0.7 collective-permute-start.10
  40.7 3.4 %collective-permute-start.11 = (f32[256,128]{1,0:T(8,128)S(1)}, f32[256,128]{1,0:T(8,128)S(1)}, u32[]{:S(2)}, u32[]{:S(2)}) collective-permute-start(f32[256,128]{1,0:T(8,128)S(1)} %get-tuple-element.91), channel_id=1, source_target_pairs={{0,32},{1,2},{2,1},{3,4},{4,3},{5,6},{6,5},{7,8},{8,7},{9,10},{10,... | collective-permute-start | bytes 393224 | tf_op jit(solution)/shard_map/ppermute | solution.py:65
  44.1 4.8 %dense_kernel.5 = (f32[8208,128]{1,0:T(8,128)S(1)}, f32[64,128]{1,0:T(8,128)S(1)}, f32[64,128]{1,0:T(8,128)S(1)}) custom-call(s32[2,3,3,32]{3,2,1,0:T(4,128)S(1)} %and_or_fusion.src, s32[1,3,3]{2,1,0:T(4,128)S(1)} %copy.40.count, s32[64]{0:T(128)S(1)} %pad_add_fusion.1.after.wanted_sec, f32[8208,128]{1,0:T(8,128)S(1)} %get-tuple-element.88.u_in, ...), custom_call_target="tpu_custom_call" | custom-call | flops 20000000 | bytes 20000000 | tf_op jit(solution)/shard_map/dense_kernel/pallas_call | solution.py:484
  48.8 1.4 %collective-permute-done.11.from_b = f32[256,128]{1,0:T(8,128)S(1)} collective-permute-done((f32[256,128]{1,0:T(8,128)S(1)}, f32[256,128]{1,0:T(8,128)S(1)}, u32[]{:S(2)}, u32[]{:S(2)}) %collective-permute-start.11) | collective-permute-done | bytes 131104 | tf_op jit(solution)/shard_map/ppermute | solution.py:65
  50.3 0.4 collective-permute-start.14
  50.7 1.4 %collective-permute-start.15 = (f32[192,128]{1,0:T(8,128)S(1)}, f32[192,128]{1,0:T(8,128)S(1)}, u32[]{:S(2)}, u32[]{:S(2)}) collective-permute-start(f32[192,128]{1,0:T(8,128)S(1)} %get-tuple-element.98), channel_id=1, source_target_pairs={{0,1},{1,0},{2,3},{3,2},{4,5},{5,4},{6,7},{7,6},{8,9},{9,8},{10,11... | collective-permute-start | bytes 294920 | tf_op jit(solution)/shard_map/ppermute | solution.py:65
  52.1 1.9 %tile_kernel.4 = (f32[8208,128]{1,0:T(8,128)S(1)}, f32[448,128]{1,0:T(8,128)S(1)}, f32[448,128]{1,0:T(8,128)S(1)}) custom-call(s32[2,3,3,32]{3,2,1,0:T(4,128)S(1)} %and_or_fusion.src, s32[1,3,3]{2,1,0:T(4,128)S(1)} %copy.40.count, s32[3]{0:T(128)S(1)} %pad_add_fusion.first, f32[8208,128]{1,0:T(8,128)S(1)} %get-tuple-element.89.u_in, ...), custom_call_target="tpu_custom_call", output_to_operand_aliasing={{0}: (3, {})} | custom-call | flops 2000000 | bytes 2000000 | tf_op jit(solution)/shard_map/tile_kernel/pallas_call | solution.py:496
  54.1 1.2 %collective-permute-start.19 = (f32[448,128]{1,0:T(8,128)S(1)}, f32[448,128]{1,0:T(8,128)S(1)}, u32[]{:S(2)}, u32[]{:S(2)}) collective-permute-start(f32[448,128]{1,0:T(8,128)S(1)} %get-tuple-element.104), channel_id=1, source_target_pairs={{0,32},{1,2},{2,1},{3,4},{4,3},{5,6},{6,5},{7,8},{8,7},{9,10},{10,... | collective-permute-start | bytes 688136 | tf_op jit(solution)/shard_map/ppermute | solution.py:65
  55.3 0.9 collective-permute-done.15.from_b
  56.2 2.0 %finish_kernel.4 = (f32[8208,128]{1,0:T(8,128)S(1)}, f32[256,128]{1,0:T(8,128)S(1)}, f32[256,128]{1,0:T(8,128)S(1)}) custom-call(s32[2,3,3,32]{3,2,1,0:T(4,128)S(1)} %and_or_fusion.src, s32[1,3,3]{2,1,0:T(4,128)S(1)} %copy.40.count, s32[192]{0:T(256)S(1)} %maximum_convert_fusion.wanted, s32[3]{0:T(128)S(1)} %pad_add_fusion.first, ...), custom_call_target="tpu_custom_call", output_to_operand_aliasing={{0}: (4, {})} | custom-call | flops 2000000 | bytes 2000000 | tf_op jit(solution)/shard_map/finish_kernel/pallas_call | solution.py:507
  58.2 0.1 collective-permute-start.16
  58.3 2.5 %collective-permute-start.17 = (f32[256,128]{1,0:T(8,128)S(1)}, f32[256,128]{1,0:T(8,128)S(1)}, u32[]{:S(2)}, u32[]{:S(2)}) collective-permute-start(f32[256,128]{1,0:T(8,128)S(1)} %get-tuple-element.102), channel_id=1, source_target_pairs={{0,32},{1,2},{2,1},{3,4},{4,3},{5,6},{6,5},{7,8},{8,7},{9,10},{10,... | collective-permute-start | bytes 393224 | tf_op jit(solution)/shard_map/ppermute | solution.py:65
  60.8 4.8 %dense_kernel.6 = (f32[8208,128]{1,0:T(8,128)S(1)}, f32[64,128]{1,0:T(8,128)S(1)}, f32[64,128]{1,0:T(8,128)S(1)}) custom-call(s32[2,3,3,32]{3,2,1,0:T(4,128)S(1)} %and_or_fusion.src, s32[1,3,3]{2,1,0:T(4,128)S(1)} %copy.40.count, s32[64]{0:T(128)S(1)} %pad_add_fusion.1.after.wanted_sec, f32[8208,128]{1,0:T(8,128)S(1)} %get-tuple-element.99.u_in, ...), custom_call_target="tpu_custom_call" | custom-call | flops 20000000 | bytes 20000000 | tf_op jit(solution)/shard_map/dense_kernel/pallas_call | solution.py:484
  65.7 1.3 %collective-permute-done.17.from_b = f32[256,128]{1,0:T(8,128)S(1)} collective-permute-done((f32[256,128]{1,0:T(8,128)S(1)}, f32[256,128]{1,0:T(8,128)S(1)}, u32[]{:S(2)}, u32[]{:S(2)}) %collective-permute-start.17) | collective-permute-done | bytes 131104 | tf_op jit(solution)/shard_map/ppermute | solution.py:65
  66.9 1.2 %collective-permute-start.20 = (f32[192,128]{1,0:T(8,128)S(1)}, f32[192,128]{1,0:T(8,128)S(1)}, u32[]{:S(2)}, u32[]{:S(2)}) collective-permute-start(f32[192,128]{1,0:T(8,128)S(1)} %get-tuple-element.108), channel_id=1, source_target_pairs={{0,32},{1,33},{2,34},{3,35},{4,36},{5,37},{6,38},{7,39},{8,40},{9,... | collective-permute-start | bytes 294920 | tf_op jit(solution)/shard_map/ppermute | solution.py:66
  68.2 1.4 %collective-permute-start.21 = (f32[192,128]{1,0:T(8,128)S(1)}, f32[192,128]{1,0:T(8,128)S(1)}, u32[]{:S(2)}, u32[]{:S(2)}) collective-permute-start(f32[192,128]{1,0:T(8,128)S(1)} %get-tuple-element.109), channel_id=1, source_target_pairs={{0,1},{1,0},{2,3},{3,2},{4,5},{5,4},{6,7},{7,6},{8,9},{9,8},{10,11... | collective-permute-start | bytes 294920 | tf_op jit(solution)/shard_map/ppermute | solution.py:65
  69.6 1.9 %tile_kernel.5 = (f32[8208,128]{1,0:T(8,128)S(1)}, f32[448,128]{1,0:T(8,128)S(1)}, f32[448,128]{1,0:T(8,128)S(1)}) custom-call(s32[2,3,3,32]{3,2,1,0:T(4,128)S(1)} %and_or_fusion.src, s32[1,3,3]{2,1,0:T(4,128)S(1)} %copy.40.count, s32[3]{0:T(128)S(1)} %pad_add_fusion.first, ...), custom_call_target="tpu_custom_call", output_to_operand_aliasing={{0}: (3, {})} | custom-call | flops 2000000 | bytes 2000000 | tf_op jit(solution)/shard_map/tile_kernel/pallas_call | solution.py:496
  71.5 0.1 collective-permute-start.24
  71.6 2.1 %collective-permute-done.21.from_b = f32[192,128]{1,0:T(8,128)S(1)} collective-permute-done((f32[192,128]{1,0:T(8,128)S(1)}, f32[192,128]{1,0:T(8,128)S(1)}, u32[]{:S(2)}, u32[]{:S(2)}) %collective-permute-start.21) | collective-permute-done | bytes 98336 | tf_op jit(solution)/shard_map/ppermute | solution.py:65
  73.7 2.0 %finish_kernel.5 = (f32[8208,128]{1,0:T(8,128)S(1)}, f32[256,128]{1,0:T(8,128)S(1)}, f32[256,128]{1,0:T(8,128)S(1)}) custom-call(s32[2,3,3,32]{3,2,1,0:T(4,128)S(1)} %and_or_fusion.src, s32[1,3,3]{2,1,0:T(4,128)S(1)} %copy.40.count, s32[192]{0:T(256)S(1)} %maximum_convert_fusion.wanted, s32[3]{0:T(128)S(1)} %pad_add_fusion.first, ...), custom_call_target="tpu_custom_call", output_to_operand_aliasing={{0}: (4, {})} | custom-call | flops 2000000 | bytes 2000000 | tf_op jit(solution)/shard_map/finish_kernel/pallas_call | solution.py:507
  75.8 1.7 %collective-permute-start.23 = (f32[256,128]{1,0:T(8,128)S(1)}, f32[256,128]{1,0:T(8,128)S(1)}, u32[]{:S(2)}, u32[]{:S(2)}) collective-permute-start(f32[256,128]{1,0:T(8,128)S(1)} %get-tuple-element.113), channel_id=1, source_target_pairs={{0,32},{1,2},{2,1},{3,4},{4,3},{5,6},{6,5},{7,8},{8,7},{9,10},{10,... | collective-permute-start | bytes 393224 | tf_op jit(solution)/shard_map/ppermute | solution.py:65
  77.6 2.8 %collective-permute-start.25 = (f32[448,128]{1,0:T(8,128)S(1)}, f32[448,128]{1,0:T(8,128)S(1)}, u32[]{:S(2)}, u32[]{:S(2)}) collective-permute-start(f32[448,128]{1,0:T(8,128)S(1)} %get-tuple-element.115), channel_id=1, source_target_pairs={{0,32},{1,2},{2,1},{3,4},{4,3},{5,6},{6,5},{7,8},{8,7},{9,10},{10,... | collective-permute-start | bytes 688136 | tf_op jit(solution)/shard_map/ppermute | solution.py:65
  80.4 4.8 %dense_kernel.7 = (f32[8208,128]{1,0:T(8,128)S(1)}, f32[64,128]{1,0:T(8,128)S(1)}, f32[64,128]{1,0:T(8,128)S(1)}) custom-call(s32[2,3,3,32]{3,2,1,0:T(4,128)S(1)} %and_or_fusion.src, s32[1,3,3]{2,1,0:T(4,128)S(1)} %copy.40.count, s32[64]{0:T(128)S(1)} %pad_add_fusion.1.after.wanted_sec, f32[8208,128]{1,0:T(8,128)S(1)} %get-tuple-element.110.u_in, ...), custom_call_target="tpu_custom_call" | custom-call | flops 20000000 | bytes 20000000 | tf_op jit(solution)/shard_map/dense_kernel/pallas_call | solution.py:484
  85.3 2.3 %collective-permute-start.27 = (f32[192,128]{1,0:T(8,128)S(1)}, f32[192,128]{1,0:T(8,128)S(1)}, u32[]{:S(2)}, u32[]{:S(2)}) collective-permute-start(f32[192,128]{1,0:T(8,128)S(1)} %get-tuple-element.119), channel_id=1, source_target_pairs={{0,1},{1,0},{2,3},{3,2},{4,5},{5,4},{6,7},{7,6},{8,9},{9,8},{10,11... | collective-permute-start | bytes 294920 | tf_op jit(solution)/shard_map/ppermute | solution.py:65
  87.6 0.8 collective-permute-done.25.rows_b
  88.4 1.6 %last_tile_kernel.1.u_in = f32[8208,128]{1,0:T(8,128)S(1)} custom-call(s32[2,3,3,32]{3,2,1,0:T(4,128)S(1)} %and_or_fusion.src, s32[1,3,3]{2,1,0:T(4,128)S(1)} %copy.40.count, s32[3]{0:T(128)S(1)} %pad_add_fusion.first, f32[8208,128]{1,0:T(8,128)S(1)} %get-tuple-element.111.u_in, ...), custom_call_target="tpu_custom_call", output_to_operand_aliasing={{}: (3, {})} | custom-call | flops 2000000 | bytes 2000000 | tf_op jit(solution)/shard_map/last_tile_kernel/pallas_call | solution.py:496
  90.0 0.9 collective-permute-done.27.from_b
  90.9 3.6 %last_kernel.1 = (f32[8208,128]{1,0:T(8,128)S(1)}, f32[2,16,16,2048]{3,2,1,0:T(8,128)}) custom-call(s32[2,3,3,32]{3,2,1,0:T(4,128)S(1)} %and_or_fusion.src, s32[1,3,3]{2,1,0:T(4,128)S(1)} %copy.40.count, s32[3]{0:T(128)S(1)} %pad_add_fusion.first, f32[8208,128]{1,0:T(8,128)S(1)} %last_tile_kernel.1.u_in, ...), custom_call_target="tpu_custom_call", output_to_operand_aliasing={{0}: (3, {})} | custom-call | flops 2000000 | bytes 2000000 | tf_op jit(solution)/shard_map/last_kernel/pallas_call | solution.py:516
  (54 shorter events, 1.0 us)
Async XLA Ops:
  0.0 12.0 %copy-start.1 = (s32[1,3,3]{2,0,1:T(1,128)S(1)}, s32[1,3,3]{2,0,1:T(1,128)}, u32[]{:S(2)}) copy-start(s32[1,3,3]{2,0,1:T(1,128)} %param.14) | copy-start | bytes 112
  0.0 12.0 %copy-start = (f32[1,3,3,32]{3,0,2,1:T(1,128)S(1)}, f32[1,3,3,32]{3,0,2,1:T(1,128)}, u32[]{:S(2)}) copy-start(f32[1,3,3,32]{3,0,2,1:T(1,128)} %param.15) | copy-start | bytes 3460
  0.0 7.4 %collective-permute-start = (s32[1,3,3,32]{3,0,2,1:T(1,128)}, s32[1,3,3,32]{3,0,2,1:T(1,128)S(1)}, u32[]{:S(2)}, u32[]{:S(2)}) collective-permute-start(s32[1,3,3,32]{3,0,2,1:T(1,128)} %param.13), channel_id=1, source_target_pairs={{0,32},{1,33},{2,34},{3,35},{4,36},{5,37},{6,38},{7,39},{8,40},{9,... | collective-permute-start | bytes 3464 | tf_op jit(solution)/shard_map/ppermute | solution.py:66
  0.7 6.8 %collective-permute-start.1 = (s32[1,3,3,32]{3,0,2,1:T(1,128)}, s32[1,3,3,32]{3,0,2,1:T(1,128)S(1)}, u32[]{:S(2)}, u32[]{:S(2)}) collective-permute-start(s32[1,3,3,32]{3,0,2,1:T(1,128)} %param.13), channel_id=1, source_target_pairs={{0,1},{1,0},{2,3},{3,2},{4,5},{5,4},{6,7},{7,6},{8,9},{9,8},{10,11... | collective-permute-start | bytes 3464 | tf_op jit(solution)/shard_map/ppermute | solution.py:65
  7.7 12.0 %collective-permute-start.3 = (f32[264,128]{1,0:T(8,128)S(1)}, f32[264,128]{1,0:T(8,128)S(1)}, u32[]{:S(2)}, u32[]{:S(2)}) collective-permute-start(f32[264,128]{1,0:T(8,128)S(1)} %get-tuple-element.122), channel_id=1, source_target_pairs={{0,32},{1,2},{2,1},{3,4},{4,3},{5,6},{6,5},{7,8},{8,7},{9,10},{10,... | collective-permute-start | bytes 405512 | tf_op jit(solution)/shard_map/ppermute | solution.py:65
  12.0 7.8 %collective-permute-start.2 = (f32[264,128]{1,0:T(8,128)S(1)}, f32[264,128]{1,0:T(8,128)S(1)}, u32[]{:S(2)}, u32[]{:S(2)}) collective-permute-start(f32[264,128]{1,0:T(8,128)S(1)} %get-tuple-element.121), channel_id=1, source_target_pairs={{0,1},{1,0},{2,3},{3,2},{4,5},{5,4},{6,7},{7,6},{8,9},{9,8},{10,11... | collective-permute-start | bytes 405512 | tf_op jit(solution)/shard_map/ppermute | solution.py:66
  15.7 19.6 %collective-permute-start.6 = (f32[448,128]{1,0:T(8,128)S(1)}, f32[448,128]{1,0:T(8,128)S(1)}, u32[]{:S(2)}, u32[]{:S(2)}) collective-permute-start(f32[448,128]{1,0:T(8,128)S(1)} %get-tuple-element.79), channel_id=1, source_target_pairs={{0,1},{1,0},{2,3},{3,2},{4,5},{5,4},{6,7},{7,6},{8,9},{9,8},{10,11... | collective-permute-start | bytes 688136 | tf_op jit(solution)/shard_map/ppermute | solution.py:66
  17.2 18.1 %collective-permute-start.7 = (f32[448,128]{1,0:T(8,128)S(1)}, f32[448,128]{1,0:T(8,128)S(1)}, u32[]{:S(2)}, u32[]{:S(2)}) collective-permute-start(f32[448,128]{1,0:T(8,128)S(1)} %get-tuple-element.80), channel_id=1, source_target_pairs={{0,32},{1,2},{2,1},{3,4},{4,3},{5,6},{6,5},{7,8},{8,7},{9,10},{10,... | collective-permute-start | bytes 688136 | tf_op jit(solution)/shard_map/ppermute | solution.py:65
  17.6 7.6 %copy-start.2 = (f32[128]{0:T(128)S(1)}, f32[128]{0:T(128)}, u32[]{:S(2)}) copy-start(f32[128]{0:T(128)} %param.11) | copy-start | bytes 1540
  20.7 11.2 %collective-permute-start.4 = (f32[256,128]{1,0:T(8,128)S(1)}, f32[256,128]{1,0:T(8,128)S(1)}, u32[]{:S(2)}, u32[]{:S(2)}) collective-permute-start(f32[256,128]{1,0:T(8,128)S(1)} %get-tuple-element.77), channel_id=1, source_target_pairs={{0,1},{1,0},{2,3},{3,2},{4,5},{5,4},{6,7},{7,6},{8,9},{9,8},{10,11... | collective-permute-start | bytes 393224 | tf_op jit(solution)/shard_map/ppermute | solution.py:66
  20.8 11.2 %collective-permute-start.5 = (f32[256,128]{1,0:T(8,128)S(1)}, f32[256,128]{1,0:T(8,128)S(1)}, u32[]{:S(2)}, u32[]{:S(2)}) collective-permute-start(f32[256,128]{1,0:T(8,128)S(1)} %get-tuple-element.78), channel_id=1, source_target_pairs={{0,32},{1,2},{2,1},{3,4},{4,3},{5,6},{6,5},{7,8},{8,7},{9,10},{10,... | collective-permute-start | bytes 393224 | tf_op jit(solution)/shard_map/ppermute | solution.py:65
  32.0 5.9 %collective-permute-start.8 = (f32[192,128]{1,0:T(8,128)S(1)}, f32[192,128]{1,0:T(8,128)S(1)}, u32[]{:S(2)}, u32[]{:S(2)}) collective-permute-start(f32[192,128]{1,0:T(8,128)S(1)} %get-tuple-element.86), channel_id=1, source_target_pairs={{0,32},{1,33},{2,34},{3,35},{4,36},{5,37},{6,38},{7,39},{8,40},{9,... | collective-permute-start | bytes 294920 | tf_op jit(solution)/shard_map/ppermute | solution.py:66
  32.1 5.8 %collective-permute-start.9 = (f32[192,128]{1,0:T(8,128)S(1)}, f32[192,128]{1,0:T(8,128)S(1)}, u32[]{:S(2)}, u32[]{:S(2)}) collective-permute-start(f32[192,128]{1,0:T(8,128)S(1)} %get-tuple-element.87), channel_id=1, source_target_pairs={{0,1},{1,0},{2,3},{3,2},{4,5},{5,4},{6,7},{7,6},{8,9},{9,8},{10,11... | collective-permute-start | bytes 294920 | tf_op jit(solution)/shard_map/ppermute | solution.py:65
  37.2 14.9 %collective-permute-start.12 = (f32[448,128]{1,0:T(8,128)S(1)}, f32[448,128]{1,0:T(8,128)S(1)}, u32[]{:S(2)}, u32[]{:S(2)}) collective-permute-start(f32[448,128]{1,0:T(8,128)S(1)} %get-tuple-element.92), channel_id=1, source_target_pairs={{0,1},{1,0},{2,3},{3,2},{4,5},{5,4},{6,7},{7,6},{8,9},{9,8},{10,11... | collective-permute-start | bytes 688136 | tf_op jit(solution)/shard_map/ppermute | solution.py:66
  37.3 14.8 %collective-permute-start.13 = (f32[448,128]{1,0:T(8,128)S(1)}, f32[448,128]{1,0:T(8,128)S(1)}, u32[]{:S(2)}, u32[]{:S(2)}) collective-permute-start(f32[448,128]{1,0:T(8,128)S(1)} %get-tuple-element.93), channel_id=1, source_target_pairs={{0,32},{1,2},{2,1},{3,4},{4,3},{5,6},{6,5},{7,8},{8,7},{9,10},{10,... | collective-permute-start | bytes 688136 | tf_op jit(solution)/shard_map/ppermute | solution.py:65
  39.9 8.9 %collective-permute-start.10 = (f32[256,128]{1,0:T(8,128)S(1)}, f32[256,128]{1,0:T(8,128)S(1)}, u32[]{:S(2)}, u32[]{:S(2)}) collective-permute-start(f32[256,128]{1,0:T(8,128)S(1)} %get-tuple-element.90), channel_id=1, source_target_pairs={{0,1},{1,0},{2,3},{3,2},{4,5},{5,4},{6,7},{7,6},{8,9},{9,8},{10,11... | collective-permute-start | bytes 393224 | tf_op jit(solution)/shard_map/ppermute | solution.py:66
  40.7 9.6 %collective-permute-start.11 = (f32[256,128]{1,0:T(8,128)S(1)}, f32[256,128]{1,0:T(8,128)S(1)}, u32[]{:S(2)}, u32[]{:S(2)}) collective-permute-start(f32[256,128]{1,0:T(8,128)S(1)} %get-tuple-element.91), channel_id=1, source_target_pairs={{0,32},{1,2},{2,1},{3,4},{4,3},{5,6},{6,5},{7,8},{8,7},{9,10},{10,... | collective-permute-start | bytes 393224 | tf_op jit(solution)/shard_map/ppermute | solution.py:65
  50.3 5.0 %collective-permute-start.14 = (f32[192,128]{1,0:T(8,128)S(1)}, f32[192,128]{1,0:T(8,128)S(1)}, u32[]{:S(2)}, u32[]{:S(2)}) collective-permute-start(f32[192,128]{1,0:T(8,128)S(1)} %get-tuple-element.97), channel_id=1, source_target_pairs={{0,32},{1,33},{2,34},{3,35},{4,36},{5,37},{6,38},{7,39},{8,40},{9,... | collective-permute-start | bytes 294920 | tf_op jit(solution)/shard_map/ppermute | solution.py:66
  50.7 5.5 %collective-permute-start.15 = (f32[192,128]{1,0:T(8,128)S(1)}, f32[192,128]{1,0:T(8,128)S(1)}, u32[]{:S(2)}, u32[]{:S(2)}) collective-permute-start(f32[192,128]{1,0:T(8,128)S(1)} %get-tuple-element.98), channel_id=1, source_target_pairs={{0,1},{1,0},{2,3},{3,2},{4,5},{5,4},{6,7},{7,6},{8,9},{9,8},{10,11... | collective-permute-start | bytes 294920 | tf_op jit(solution)/shard_map/ppermute | solution.py:65
  54.0 15.6 %collective-permute-start.18 = (f32[448,128]{1,0:T(8,128)S(1)}, f32[448,128]{1,0:T(8,128)S(1)}, u32[]{:S(2)}, u32[]{:S(2)}) collective-permute-start(f32[448,128]{1,0:T(8,128)S(1)} %get-tuple-element.103), channel_id=1, source_target_pairs={{0,1},{1,0},{2,3},{3,2},{4,5},{5,4},{6,7},{7,6},{8,9},{9,8},{10,11... | collective-permute-start | bytes 688136 | tf_op jit(solution)/shard_map/ppermute | solution.py:66
  54.1 15.5 %collective-permute-start.19 = (f32[448,128]{1,0:T(8,128)S(1)}, f32[448,128]{1,0:T(8,128)S(1)}, u32[]{:S(2)}, u32[]{:S(2)}) collective-permute-start(f32[448,128]{1,0:T(8,128)S(1)} %get-tuple-element.104), channel_id=1, source_target_pairs={{0,32},{1,2},{2,1},{3,4},{4,3},{5,6},{6,5},{7,8},{8,7},{9,10},{10,... | collective-permute-start | bytes 688136 | tf_op jit(solution)/shard_map/ppermute | solution.py:65
  58.2 7.4 %collective-permute-start.16 = (f32[256,128]{1,0:T(8,128)S(1)}, f32[256,128]{1,0:T(8,128)S(1)}, u32[]{:S(2)}, u32[]{:S(2)}) collective-permute-start(f32[256,128]{1,0:T(8,128)S(1)} %get-tuple-element.101), channel_id=1, source_target_pairs={{0,1},{1,0},{2,3},{3,2},{4,5},{5,4},{6,7},{7,6},{8,9},{9,8},{10,11... | collective-permute-start | bytes 393224 | tf_op jit(solution)/shard_map/ppermute | solution.py:66
  58.3 8.6 %collective-permute-start.17 = (f32[256,128]{1,0:T(8,128)S(1)}, f32[256,128]{1,0:T(8,128)S(1)}, u32[]{:S(2)}, u32[]{:S(2)}) collective-permute-start(f32[256,128]{1,0:T(8,128)S(1)} %get-tuple-element.102), channel_id=1, source_target_pairs={{0,32},{1,2},{2,1},{3,4},{4,3},{5,6},{6,5},{7,8},{8,7},{9,10},{10,... | collective-permute-start | bytes 393224 | tf_op jit(solution)/shard_map/ppermute | solution.py:65
  66.9 4.7 %collective-permute-start.20 = (f32[192,128]{1,0:T(8,128)S(1)}, f32[192,128]{1,0:T(8,128)S(1)}, u32[]{:S(2)}, u32[]{:S(2)}) collective-permute-start(f32[192,128]{1,0:T(8,128)S(1)} %get-tuple-element.108), channel_id=1, source_target_pairs={{0,32},{1,33},{2,34},{3,35},{4,36},{5,37},{6,38},{7,39},{8,40},{9,... | collective-permute-start | bytes 294920 | tf_op jit(solution)/shard_map/ppermute | solution.py:66
  68.2 5.5 %collective-permute-start.21 = (f32[192,128]{1,0:T(8,128)S(1)}, f32[192,128]{1,0:T(8,128)S(1)}, u32[]{:S(2)}, u32[]{:S(2)}) collective-permute-start(f32[192,128]{1,0:T(8,128)S(1)} %get-tuple-element.109), channel_id=1, source_target_pairs={{0,1},{1,0},{2,3},{3,2},{4,5},{5,4},{6,7},{7,6},{8,9},{9,8},{10,11... | collective-permute-start | bytes 294920 | tf_op jit(solution)/shard_map/ppermute | solution.py:65
  71.5 16.1 %collective-permute-start.24 = (f32[448,128]{1,0:T(8,128)S(1)}, f32[448,128]{1,0:T(8,128)S(1)}, u32[]{:S(2)}, u32[]{:S(2)}) collective-permute-start(f32[448,128]{1,0:T(8,128)S(1)} %get-tuple-element.114), channel_id=1, source_target_pairs={{0,1},{1,0},{2,3},{3,2},{4,5},{5,4},{6,7},{7,6},{8,9},{9,8},{10,11... | collective-permute-start | bytes 688136 | tf_op jit(solution)/shard_map/ppermute | solution.py:66
  75.7 9.4 %collective-permute-start.22 = (f32[256,128]{1,0:T(8,128)S(1)}, f32[256,128]{1,0:T(8,128)S(1)}, u32[]{:S(2)}, u32[]{:S(2)}) collective-permute-start(f32[256,128]{1,0:T(8,128)S(1)} %get-tuple-element.112), channel_id=1, source_target_pairs={{0,1},{1,0},{2,3},{3,2},{4,5},{5,4},{6,7},{7,6},{8,9},{9,8},{10,11... | collective-permute-start | bytes 393224 | tf_op jit(solution)/shard_map/ppermute | solution.py:66
  75.8 9.3 %collective-permute-start.23 = (f32[256,128]{1,0:T(8,128)S(1)}, f32[256,128]{1,0:T(8,128)S(1)}, u32[]{:S(2)}, u32[]{:S(2)}) collective-permute-start(f32[256,128]{1,0:T(8,128)S(1)} %get-tuple-element.113), channel_id=1, source_target_pairs={{0,32},{1,2},{2,1},{3,4},{4,3},{5,6},{6,5},{7,8},{8,7},{9,10},{10,... | collective-permute-start | bytes 393224 | tf_op jit(solution)/shard_map/ppermute | solution.py:65
  77.6 10.8 %collective-permute-start.25 = (f32[448,128]{1,0:T(8,128)S(1)}, f32[448,128]{1,0:T(8,128)S(1)}, u32[]{:S(2)}, u32[]{:S(2)}) collective-permute-start(f32[448,128]{1,0:T(8,128)S(1)} %get-tuple-element.115), channel_id=1, source_target_pairs={{0,32},{1,2},{2,1},{3,4},{4,3},{5,6},{6,5},{7,8},{8,7},{9,10},{10,... | collective-permute-start | bytes 688136 | tf_op jit(solution)/shard_map/ppermute | solution.py:65
  85.2 4.8 %collective-permute-start.26 = (f32[192,128]{1,0:T(8,128)S(1)}, f32[192,128]{1,0:T(8,128)S(1)}, u32[]{:S(2)}, u32[]{:S(2)}) collective-permute-start(f32[192,128]{1,0:T(8,128)S(1)} %get-tuple-element.118), channel_id=1, source_target_pairs={{0,32},{1,33},{2,34},{3,35},{4,36},{5,37},{6,38},{7,39},{8,40},{9,... | collective-permute-start | bytes 294920 | tf_op jit(solution)/shard_map/ppermute | solution.py:66
  85.3 5.6 %collective-permute-start.27 = (f32[192,128]{1,0:T(8,128)S(1)}, f32[192,128]{1,0:T(8,128)S(1)}, u32[]{:S(2)}, u32[]{:S(2)}) collective-permute-start(f32[192,128]{1,0:T(8,128)S(1)} %get-tuple-element.119), channel_id=1, source_target_pairs={{0,1},{1,0},{2,3},{3,2},{4,5},{5,4},{6,7},{7,6},{8,9},{9,8},{10,11... | collective-permute-start | bytes 294920 | tf_op jit(solution)/shard_map/ppermute | solution.py:65

commit v3 on v2

--- a/solution.py
+++ b/solution.py
@@ -42,7 +42,6 @@
         input_output_aliases=aliases or {},
         compiler_params=pltpu.CompilerParams(vmem_limit_bytes=limit * 2**20),
         cost_estimate=pl.CostEstimate(flops=cost, bytes_accessed=cost, transcendentals=0),
-        name=body.__name__,
     )
 
 
@@ -79,7 +78,7 @@
     return lax.broadcasted_iota(jnp.int32, (ROW, LANE), dim)
 
 
-def loop(stop, body, step=1):
+def loop(stop, body):
     def run(i, carry):
         body(i)
         return carry
@@ -342,18 +341,10 @@
             out[pl.ds(m * SEG + 2 * CAP, CAP), :] = from_b[pl.ds(there, CAP), :]
 
 
-def tile_adds(src, count, first, from_a, from_b, rows_a, rows_b, ca_ref, cb_ref, cw_ref, frac_ref, u_ref, term_ref):
+def tile_adds(
+    src, count, first, from_a, from_b, rows_a, rows_b, ca_ref, cb_ref, cw_ref, frac_ref, u_ref, term_ref, a_ref=None, b_ref=None
+):
     row_a = first_row(first)
-
-    def add(s, message_a, message_b, at):
-        own = pl.ds(s * COLS, COLS)
-        for m in range(2):
-            u_ref[row_at(m, s, row_a), :] += ca_ref[own, :] * message_a[at(m), :]
-            u_ref[row_at(m, s, ROW - 1 - row_a), :] += cb_ref[own, :] * message_b[at(m), :]
-
-    loop(INNER, lambda i: add(i + 1, rows_a, rows_b, lambda m: cols_at(m, i + 1)))
-    for q, s in enumerate((0, SEC - 1)):
-        add(s, from_a, from_b, lambda m: edge_at(m, q))
     fraction = frac_ref[...]
     for message, start, e in ((from_a, SEG, first[1]), (from_b, SEG + 2 * CAP, 2 - first[1])):
         scale = cw_ref[pl.ds(start, CAP), :]
@@ -362,18 +353,43 @@
             term_ref[pl.ds(m * CAP, CAP), :] = terms(blocks, fraction, scale)
         scatter(src, count, 1, e, u_ref, term_ref, 0, CAP)
 
+    def add(s, message_a, message_b, at, to_a, to_b):
+        own = pl.ds(s * COLS, COLS)
+        for m in range(2):
+            for row, scale, message, to in ((row_a, ca_ref, message_a, to_a), (ROW - 1 - row_a, cb_ref, message_b, to_b)):
+                value = u_ref[row_at(m, s, row), :] + scale[own, :] * message[at(m), :]
+                u_ref[row_at(m, s, row), :] = value
+                if to is not None:
+                    to[at(m), :] = value
+
+    loop(INNER, lambda i: add(i + 1, rows_a, rows_b, lambda m: cols_at(m, i + 1), a_ref, b_ref))
+    for q, s in enumerate((0, SEC - 1)):
+        add(s, from_a, from_b, lambda m: edge_at(m, q), None, None)
+
 
 def tile_kernel(
     src, count, first, u_in, from_a, from_b, rows_a, rows_b, ca_ref, cb_ref, cw_ref, frac_ref, u_ref, a_ref, b_ref, term_ref
 ):
-    tile_adds(src, count, first, from_a, from_b, rows_a, rows_b, ca_ref, cb_ref, cw_ref, frac_ref, u_ref, term_ref)
-    pack_rows(first, u_ref, a_ref, b_ref)
+    tile_adds(
+        src, count, first, from_a, from_b, rows_a, rows_b, ca_ref, cb_ref, cw_ref, frac_ref, u_ref, term_ref, a_ref, b_ref
+    )
+
+
+def write_section(s, u_ref, held_ref, out_ref, sem):
+    for m in range(2):
+        for j in range(COLS):
+            at = pl.ds(pl.multiple_of(PAD + m * PART + s * SECTION + j * ROW, 8), ROW)
+            held_ref[m, s, :, lanes(j)] = u_ref[at, :]
+        pltpu.make_async_copy(held_ref.at[m, s], out_ref.at[m, s], sem).start()
 
 
 def last_tile_kernel(
-    src, count, first, u_in, from_a, from_b, rows_a, rows_b, ca_ref, cb_ref, cw_ref, frac_ref, u_ref, term_ref
+    src, count, first, u_in, from_a, from_b, rows_a, rows_b, ca_ref, cb_ref, cw_ref, frac_ref, u_ref, out_ref, term_ref, held_ref, sem
 ):
     tile_adds(src, count, first, from_a, from_b, rows_a, rows_b, ca_ref, cb_ref, cw_ref, frac_ref, u_ref, term_ref)
+    loop(INNER, lambda i: write_section(i + 1, u_ref, held_ref, out_ref, sem))
+    inner = (slice(None), pl.ds(1, INNER))
+    pltpu.make_async_copy(held_ref.at[inner], out_ref.at[inner], sem).wait()
 
 
 def section_adds(src, count, first, from_a, from_b, cw_ref, frac_ref, u_ref, term_ref):
@@ -392,18 +408,16 @@
     pack_messages(wanted, first, u_ref, a_ref, b_ref)
 
 
-def last_kernel(src, count, first, u_in, from_a, from_b, cw_ref, frac_ref, u_ref, out_ref, term_ref, held_ref, sem):
+def last_kernel(src, count, first, u_in, out_in, from_a, from_b, cw_ref, frac_ref, u_ref, out_ref, term_ref, held_ref, sem):
     section_adds(src, count, first, from_a, from_b, cw_ref, frac_ref, u_ref, term_ref)
-
-    def section(s):
+    for q, s in enumerate((0, SEC - 1)):
         for m in range(2):
             for j in range(COLS):
-                at = pl.ds(pl.multiple_of(PAD + m * PART + s * SECTION + j * ROW, 8), ROW)
-                held_ref[m, s, :, lanes(j)] = u_ref[at, :]
-            pltpu.make_async_copy(held_ref.at[m, s], out_ref.at[m, s], sem).start()
-
-    loop(SEC, section)
-    pltpu.make_async_copy(held_ref, out_ref, sem).wait()
+                held_ref[q, m, :, lanes(j)] = u_ref[pl.ds(PAD + m * PART + s * SECTION + j * ROW, ROW), :]
+            pltpu.make_async_copy(held_ref.at[q, m], out_ref.at[m, s], sem.at[q, m]).start()
+    for q, s in enumerate((0, SEC - 1)):
+        for m in range(2):
+            pltpu.make_async_copy(held_ref.at[q, m], out_ref.at[m, s], sem.at[q, m]).wait()
 
 
 def on_device(
@@ -479,11 +493,12 @@
         cost=1_000_000,
     )(source, match_weight, match_count, first, dg, got_a, got_b, rim, cc, u)
 
+    whole = jax.ShapeDtypeStruct(displacement.shape, jnp.float32)
     for step in range(ITERS):
         tile_a, tile_b = exchange(to_a, to_b, "tile")
         v, own_a, own_b = kernel_call(
             dense_kernel,
-            [vmem(FIELD, LANE), vmem(2 * CAP, LANE), vmem(2 * CAP, LANE)],
+            [field, vmem(2 * CAP, LANE), vmem(2 * CAP, LANE)],
             [SM] * 3 + [VM] * 6,
             scratch=[vmem(2 * CAP, LANE)],
             cost=20_000_000,
@@ -492,37 +507,45 @@
             tile_a, tile_b, own_a, own_b
         )
         sec_a, sec_b = exchange(sec_to_a, sec_to_b, "sec")
-        more = step + 1 < ITERS
-        v, *rows_to = kernel_call(
-            tile_kernel if more else last_tile_kernel,
-            [vmem(FIELD, LANE)] + (rows if more else []),
-            [SM] * 3 + [VM] * 9,
-            aliases={3: 0},
-            scratch=[vmem(2 * CAP, LANE)],
-            cost=2_000_000,
-        )(source, match_count, first, v, tile_a, tile_b, rows_a, rows_b, ca, cb, cw, fraction)
-        if more:
+        received = (tile_a, tile_b, rows_a, rows_b, ca, cb, cw, fraction)
+        if step + 1 < ITERS:
+            v, *rows_to = kernel_call(
+                tile_kernel,
+                [field] + rows,
+                [SM] * 3 + [VM] * 9,
+                aliases={3: 0},
+                scratch=[vmem(2 * CAP, LANE)],
+                cost=2_000_000,
+            )(source, match_count, first, v, *received)
             rows_a, rows_b = exchange(*rows_to, "tile")
-        if step + 1 < ITERS:
             u, to_a, to_b = kernel_call(
                 finish_kernel,
-                [vmem(FIELD, LANE)] + messages,
+                [field] + messages,
                 [SM] * 4 + [VM] * 5,
                 aliases={4: 0},
                 scratch=[vmem(2 * SEG, LANE)],
                 cost=2_000_000,
             )(source, match_count, wanted, first, v, sec_a, sec_b, cw, fraction)
         else:
+            v, out = kernel_call(
+                last_tile_kernel,
+                [field, whole],
+                [SM] * 3 + [VM] * 9,
+                aliases={3: 0},
+                scratch=[vmem(2 * CAP, LANE), vmem(2, SEC, ROW, WID), pltpu.SemaphoreType.DMA],
+                cost=4_000_000,
+                out_specs=(VM, HB),
+                limit=8,
+            )(source, match_count, first, v, *received)
             _, out = kernel_call(
                 last_kernel,
-                [vmem(FIELD, LANE), jax.ShapeDtypeStruct(displacement.shape, jnp.float32)],
-                [SM] * 3 + [VM] * 5,
-                aliases={3: 0},
-                scratch=[vmem(2 * SEG, LANE), vmem(2, SEC, ROW, WID), pltpu.SemaphoreType.DMA],
+                [field, whole],
+                [SM] * 3 + [VM, HB] + [VM] * 4,
+                aliases={3: 0, 4: 1},
+                scratch=[vmem(2 * SEG, LANE), vmem(2, 2, ROW, WID), pltpu.SemaphoreType.DMA((2, 2))],
                 cost=2_000_000,
                 out_specs=(VM, HB),
-                limit=8,
-            )(source, match_count, first, v, sec_a, sec_b, cw, fraction)
+            )(source, match_count, first, v, out, sec_a, sec_b, cw, fraction)
     return out
 
 

time: 94.8 us -> 93.1 us (0.982)
  Pallas kernels: 47.1 us -> 45.9 us
    ppermute x14, starting transfers between devices: 5.3 us -> 6.77 us  [exchange(): from_a = lax.ppermute(to_a, ('sec', 'tile'), pairing(axis, 0))]
    ppermute x14, starting transfers between devices: 32.4 us -> 31.2 us  [exchange(): from_b = lax.ppermute(to_b, ('sec', 'tile'), pairing(axis, 1))]
  transfers between devices with their start and end apart: 28 -> 28, of which waited for: 6 -> 6; matrix products, arithmetic and copies ran while one was open for 2% -> 2% of each run, Pallas kernels for 46% -> 47%
where the time goes in v3:
time: 93.1 us; the launch traced here: 92.9 us
  Pallas kernels  45.9 us (49%)
  starting transfers between devices  37.9 us (41%)
  waiting for transfers between devices  6.81 us (7%)
  local copies, waits for them, and re-layouts  1.45 us (2%)
    ppermute x14, starting transfers between devices, exchange(): from_b = lax.ppermute(to_b, ('sec', 'tile'), pairing(axis, 1))  31.2 us
    pallas_call x4, Pallas kernels, on_device(): kernel_call(dense_kernel, [field, vmem(2 * CAP, LANE), vmem(2 * CAP, LANE...  19 us
    ppermute x14, waiting for transfers between devices, exchange(): from_b = lax.ppermute(to_b, ('sec', 'tile'), pairing(axis, 1))  6.77 us
    ppermute x14, starting transfers between devices, exchange(): from_a = lax.ppermute(to_a, ('sec', 'tile'), pairing(axis, 0))  6.77 us
    pallas_call x3, Pallas kernels, on_device(): kernel_call(finish_kernel, [field] + messages, [SM] * 4 + [VM] * 5, alias...  5.31 us
    pallas_call x3, Pallas kernels, on_device(): kernel_call(tile_kernel, [field] + rows, [SM] * 3 + [VM] * 9, aliases={3:...  5.15 us
    pallas_call x1, Pallas kernels, on_device(): kernel_call(setup_kernel, [field, vmem(PART, LANE), vmem(PART + 2 * PAD,...  3.53 us
    pallas_call x1, Pallas kernels, on_device(): kernel_call(last_tile_kernel, [field, whole], [SM] * 3 + [VM] * 9, aliase...  3.51 us
  transfers between devices with their start and end apart: 28, of which 6 were waited for; matrix products, arithmetic and copies ran while one was open for 2% of the time, Pallas kernels for 47%

profile of v3, /device:TPU:7, one launch (start us, length us, event | category | flops | bytes accessed | tf_op | source)
XLA Modules:
  0.0 92.9 jit_solution(9621538224405003540)
XLA Ops:
  0.0 0.7 collective-permute-start
  0.7 2.9 %collective-permute-start.1 = (s32[1,3,3,32]{3,0,2,1:T(1,128)}, s32[1,3,3,32]{3,0,2,1:T(1,128)S(1)}, u32[]{:S(2)}, u32[]{:S(2)}) collective-permute-start(s32[1,3,3,32]{3,0,2,1:T(1,128)} %param.13), channel_id=1, source_target_pairs={{0,1},{1,0},{2,3},{3,2},{4,5},{5,4},{6,7},{7,6},{8,9},{9,8},{10,11... | collective-permute-start | bytes 3464 | tf_op jit(solution)/shard_map/ppermute | solution.py:64
  3.6 0.7 constant_dynamic-update-slice_fusion.1
  4.3 0.7 constant_dynamic-update-slice_fusion
  5.0 2.4 %shard_map.82 = (f32[8208,128]{1,0:T(8,128)S(1)}, f32[256,128]{1,0:T(8,128)S(1)}) custom-call(f32[1]{0:T(128)} %bitcast.5.keep, f32[2,16,16,2048]{3,2,1,0:T(8,128)} %field_in.1, f32[16,16,2048]{2,1,0:T(8,128)} %kd_in.3), custom_call_target="tpu_custom_call" | custom-call | flops 6000000 | bytes 6000000 | tf_op jit(solution)/shard_map/pallas_call | solution.py:447
  7.7 4.2 %collective-permute-start.3 = (f32[264,128]{1,0:T(8,128)S(1)}, f32[264,128]{1,0:T(8,128)S(1)}, u32[]{:S(2)}, u32[]{:S(2)}) collective-permute-start(f32[264,128]{1,0:T(8,128)S(1)} %get-tuple-element.126), channel_id=1, source_target_pairs={{0,32},{1,2},{2,1},{3,4},{4,3},{5,6},{6,5},{7,8},{8,7},{9,10},{10,... | collective-permute-start | bytes 405512 | tf_op jit(solution)/shard_map/ppermute | solution.py:64
  12.1 3.5 %shard_map.83 = (f32[8208,128]{1,0:T(8,128)S(1)}, f32[4096,128]{1,0:T(8,128)S(1)}, f32[4112,128]{1,0:T(8,128)S(1)}, f32[4096,128]{1,0:T(8,128)S(1)}, f32[448,128]{1,0:T(8,128)S(1)}, /*index=5*/f32[448,128]{1,0:T(8,128)S(1)}) custom-call(s32[3]{0:T(128)S(1)} %pad_add_fusion.first, ...), custom_call_target="tpu_custom_call", output_to_operand_aliasing={{0}: (3, {})} | custom-call | flops 6000000 | bytes 6000000 | tf_op jit(solution)/shard_map/pallas_call | solution.py:467
  15.7 1.5 %collective-permute-start.6 = (f32[448,128]{1,0:T(8,128)S(1)}, f32[448,128]{1,0:T(8,128)S(1)}, u32[]{:S(2)}, u32[]{:S(2)}) collective-permute-start(f32[448,128]{1,0:T(8,128)S(1)} %get-tuple-element.81), channel_id=1, source_target_pairs={{0,1},{1,0},{2,3},{3,2},{4,5},{5,4},{6,7},{7,6},{8,9},{9,8},{10,11... | collective-permute-start | bytes 688136 | tf_op jit(solution)/shard_map/ppermute | solution.py:65
  17.2 0.3 collective-permute-start.7
  17.6 2.0 %shard_map.84 = (f32[4096,128]{1,0:T(8,128)S(1)}, f32[8208,128]{1,0:T(8,128)S(1)}, f32[4096,128]{1,0:T(8,128)S(1)}) custom-call(s32[2,3,3,32]{3,2,1,0:T(4,128)S(1)} %and_or_fusion.src, f32[1,3,3,32]{3,2,1,0:T(4,128)S(1)} %copy.28.weight, s32[1,3,3]{2,1,0:T(4,128)S(1)} %copy.41.count, ...), custom_call_target="tpu_custom_call", output_to_operand_aliasing={{0}: (3, {}), {1}: (4, {})} | custom-call | flops 4000000 | bytes 4000000 | tf_op jit(solution)/shard_map/pallas_call | solution.py:477
  19.6 0.9 shard_map.85
  20.6 4.7 %collective-permute-start.5 = (f32[256,128]{1,0:T(8,128)S(1)}, f32[256,128]{1,0:T(8,128)S(1)}, u32[]{:S(2)}, u32[]{:S(2)}) collective-permute-start(f32[256,128]{1,0:T(8,128)S(1)} %get-tuple-element.80), channel_id=1, source_target_pairs={{0,32},{1,2},{2,1},{3,4},{4,3},{5,6},{6,5},{7,8},{8,7},{9,10},{10,... | collective-permute-start | bytes 393224 | tf_op jit(solution)/shard_map/ppermute | solution.py:64
  25.3 1.8 %shard_map.86 = (f32[4096,128]{1,0:T(8,128)S(1)}, f32[8208,128]{1,0:T(8,128)S(1)}, f32[256,128]{1,0:T(8,128)S(1)}, f32[256,128]{1,0:T(8,128)S(1)}, f32[288,128]{1,0:T(8,128)S(1)}) custom-call(s32[2,3,3,32]{3,2,1,0:T(4,128)S(1)} %and_or_fusion.src, f32[1,3,3,32]{3,2,1,0:T(4,128)S(1)} %copy.28.weight, ...), custom_call_target="tpu_custom_call", output_to_operand_aliasing={{0}: (8, {}), {1}: (9, {})} | custom-call | flops 1000000 | bytes 1000000 | tf_op jit(solution)/shard_map/pallas_call | solution.py:488
  27.2 4.7 %shard_map.87 = (f32[8208,128]{1,0:T(8,128)S(1)}, f32[64,128]{1,0:T(8,128)S(1)}, f32[64,128]{1,0:T(8,128)S(1)}) custom-call(s32[2,3,3,32]{3,2,1,0:T(4,128)S(1)} %and_or_fusion.src, s32[1,3,3]{2,1,0:T(4,128)S(1)} %copy.41.count, s32[64]{0:T(128)S(1)} %pad_add_fusion.1.after.wanted_sec, f32[8208,128]{1,0:T(8,128)S(1)} %get-tuple-element.73.u_in, ...), custom_call_target="tpu_custom_call" | custom-call | flops 20000000 | bytes 20000000 | tf_op jit(solution)/shard_map/pallas_call | solution.py:499
  32.0 3.4 %collective-permute-start.9 = (f32[192,128]{1,0:T(8,128)S(1)}, f32[192,128]{1,0:T(8,128)S(1)}, u32[]{:S(2)}, u32[]{:S(2)}) collective-permute-start(f32[192,128]{1,0:T(8,128)S(1)} %get-tuple-element.89), channel_id=1, source_target_pairs={{0,1},{1,0},{2,3},{3,2},{4,5},{5,4},{6,7},{7,6},{8,9},{9,8},{10,11... | collective-permute-start | bytes 294920 | tf_op jit(solution)/shard_map/ppermute | solution.py:64
  35.5 1.7 %shard_map.88 = (f32[8208,128]{1,0:T(8,128)S(1)}, f32[448,128]{1,0:T(8,128)S(1)}, f32[448,128]{1,0:T(8,128)S(1)}) custom-call(s32[2,3,3,32]{3,2,1,0:T(4,128)S(1)} %and_or_fusion.src, s32[1,3,3]{2,1,0:T(4,128)S(1)} %copy.41.count, s32[3]{0:T(128)S(1)} %pad_add_fusion.first, f32[8208,128]{1,0:T(8,128)S(1)} %get-tuple-element.78.u_in, ...), custom_call_target="tpu_custom_call", output_to_operand_aliasing={{0}: (3, {})} | custom-call | flops 2000000 | bytes 2000000 | tf_op jit(solution)/shard_map/pallas_call | solution.py:512
  37.2 0.1 collective-permute-start.12
  37.3 0.4 collective-permute-start.13
  37.8 1.8 %shard_map.90 = (f32[8208,128]{1,0:T(8,128)S(1)}, f32[256,128]{1,0:T(8,128)S(1)}, f32[256,128]{1,0:T(8,128)S(1)}) custom-call(s32[2,3,3,32]{3,2,1,0:T(4,128)S(1)} %and_or_fusion.src, s32[1,3,3]{2,1,0:T(4,128)S(1)} %copy.41.count, s32[192]{0:T(256)S(1)} %maximum_convert_fusion.wanted, s32[3]{0:T(128)S(1)} %pad_add_fusion.first, ...), custom_call_target="tpu_custom_call", output_to_operand_aliasing={{0}: (4, {})} | custom-call | flops 2000000 | bytes 2000000 | tf_op jit(solution)/shard_map/pallas_call | solution.py:521
  39.5 1.1 %collective-permute-start.10 = (f32[256,128]{1,0:T(8,128)S(1)}, f32[256,128]{1,0:T(8,128)S(1)}, u32[]{:S(2)}, u32[]{:S(2)}) collective-permute-start(f32[256,128]{1,0:T(8,128)S(1)} %get-tuple-element.92), channel_id=1, source_target_pairs={{0,1},{1,0},{2,3},{3,2},{4,5},{5,4},{6,7},{7,6},{8,9},{9,8},{10,11... | collective-permute-start | bytes 393224 | tf_op jit(solution)/shard_map/ppermute | solution.py:65
  40.6 3.5 %collective-permute-start.11 = (f32[256,128]{1,0:T(8,128)S(1)}, f32[256,128]{1,0:T(8,128)S(1)}, u32[]{:S(2)}, u32[]{:S(2)}) collective-permute-start(f32[256,128]{1,0:T(8,128)S(1)} %get-tuple-element.93), channel_id=1, source_target_pairs={{0,32},{1,2},{2,1},{3,4},{4,3},{5,6},{6,5},{7,8},{8,7},{9,10},{10,... | collective-permute-start | bytes 393224 | tf_op jit(solution)/shard_map/ppermute | solution.py:64
  44.1 4.7 %shard_map.91 = (f32[8208,128]{1,0:T(8,128)S(1)}, f32[64,128]{1,0:T(8,128)S(1)}, f32[64,128]{1,0:T(8,128)S(1)}) custom-call(s32[2,3,3,32]{3,2,1,0:T(4,128)S(1)} %and_or_fusion.src, s32[1,3,3]{2,1,0:T(4,128)S(1)} %copy.41.count, s32[64]{0:T(128)S(1)} %pad_add_fusion.1.after.wanted_sec, f32[8208,128]{1,0:T(8,128)S(1)} %get-tuple-element.90.u_in, ...), custom_call_target="tpu_custom_call" | custom-call | flops 20000000 | bytes 20000000 | tf_op jit(solution)/shard_map/pallas_call | solution.py:499
  48.8 1.4 %collective-permute-done.11.from_b = f32[256,128]{1,0:T(8,128)S(1)} collective-permute-done((f32[256,128]{1,0:T(8,128)S(1)}, f32[256,128]{1,0:T(8,128)S(1)}, u32[]{:S(2)}, u32[]{:S(2)}) %collective-permute-start.11) | collective-permute-done | bytes 131104 | tf_op jit(solution)/shard_map/ppermute | solution.py:64
  50.2 0.4 collective-permute-start.14
  50.6 1.3 %collective-permute-start.15 = (f32[192,128]{1,0:T(8,128)S(1)}, f32[192,128]{1,0:T(8,128)S(1)}, u32[]{:S(2)}, u32[]{:S(2)}) collective-permute-start(f32[192,128]{1,0:T(8,128)S(1)} %get-tuple-element.100), channel_id=1, source_target_pairs={{0,1},{1,0},{2,3},{3,2},{4,5},{5,4},{6,7},{7,6},{8,9},{9,8},{10,11... | collective-permute-start | bytes 294920 | tf_op jit(solution)/shard_map/ppermute | solution.py:64
  51.9 1.7 %shard_map.92 = (f32[8208,128]{1,0:T(8,128)S(1)}, f32[448,128]{1,0:T(8,128)S(1)}, f32[448,128]{1,0:T(8,128)S(1)}) custom-call(s32[2,3,3,32]{3,2,1,0:T(4,128)S(1)} %and_or_fusion.src, s32[1,3,3]{2,1,0:T(4,128)S(1)} %copy.41.count, s32[3]{0:T(128)S(1)} %pad_add_fusion.first, f32[8208,128]{1,0:T(8,128)S(1)} %get-tuple-element.91.u_in, ...), custom_call_target="tpu_custom_call", output_to_operand_aliasing={{0}: (3, {})} | custom-call | flops 2000000 | bytes 2000000 | tf_op jit(solution)/shard_map/pallas_call | solution.py:512
  53.6 0.1 collective-permute-start.18
  53.7 1.3 %collective-permute-start.19 = (f32[448,128]{1,0:T(8,128)S(1)}, f32[448,128]{1,0:T(8,128)S(1)}, u32[]{:S(2)}, u32[]{:S(2)}) collective-permute-start(f32[448,128]{1,0:T(8,128)S(1)} %get-tuple-element.106), channel_id=1, source_target_pairs={{0,32},{1,2},{2,1},{3,4},{4,3},{5,6},{6,5},{7,8},{8,7},{9,10},{10,... | collective-permute-start | bytes 688136 | tf_op jit(solution)/shard_map/ppermute | solution.py:64
  55.0 1.1 %collective-permute-done.15.from_b = f32[192,128]{1,0:T(8,128)S(1)} collective-permute-done((f32[192,128]{1,0:T(8,128)S(1)}, f32[192,128]{1,0:T(8,128)S(1)}, u32[]{:S(2)}, u32[]{:S(2)}) %collective-permute-start.15) | collective-permute-done | bytes 98336 | tf_op jit(solution)/shard_map/ppermute | solution.py:64
  56.1 1.8 %shard_map.94 = (f32[8208,128]{1,0:T(8,128)S(1)}, f32[256,128]{1,0:T(8,128)S(1)}, f32[256,128]{1,0:T(8,128)S(1)}) custom-call(s32[2,3,3,32]{3,2,1,0:T(4,128)S(1)} %and_or_fusion.src, s32[1,3,3]{2,1,0:T(4,128)S(1)} %copy.41.count, s32[192]{0:T(256)S(1)} %maximum_convert_fusion.wanted, s32[3]{0:T(128)S(1)} %pad_add_fusion.first, ...), custom_call_target="tpu_custom_call", output_to_operand_aliasing={{0}: (4, {})} | custom-call | flops 2000000 | bytes 2000000 | tf_op jit(solution)/shard_map/pallas_call | solution.py:521
  58.0 2.5 %collective-permute-start.17 = (f32[256,128]{1,0:T(8,128)S(1)}, f32[256,128]{1,0:T(8,128)S(1)}, u32[]{:S(2)}, u32[]{:S(2)}) collective-permute-start(f32[256,128]{1,0:T(8,128)S(1)} %get-tuple-element.104), channel_id=1, source_target_pairs={{0,32},{1,2},{2,1},{3,4},{4,3},{5,6},{6,5},{7,8},{8,7},{9,10},{10,... | collective-permute-start | bytes 393224 | tf_op jit(solution)/shard_map/ppermute | solution.py:64
  60.5 4.8 %shard_map.95 = (f32[8208,128]{1,0:T(8,128)S(1)}, f32[64,128]{1,0:T(8,128)S(1)}, f32[64,128]{1,0:T(8,128)S(1)}) custom-call(s32[2,3,3,32]{3,2,1,0:T(4,128)S(1)} %and_or_fusion.src, s32[1,3,3]{2,1,0:T(4,128)S(1)} %copy.41.count, s32[64]{0:T(128)S(1)} %pad_add_fusion.1.after.wanted_sec, f32[8208,128]{1,0:T(8,128)S(1)} %get-tuple-element.101.u_in, ...), custom_call_target="tpu_custom_call" | custom-call | flops 20000000 | bytes 20000000 | tf_op jit(solution)/shard_map/pallas_call | solution.py:499
  65.3 1.3 %collective-permute-done.17.from_b = f32[256,128]{1,0:T(8,128)S(1)} collective-permute-done((f32[256,128]{1,0:T(8,128)S(1)}, f32[256,128]{1,0:T(8,128)S(1)}, u32[]{:S(2)}, u32[]{:S(2)}) %collective-permute-start.17) | collective-permute-done | bytes 131104 | tf_op jit(solution)/shard_map/ppermute | solution.py:64
  66.6 1.1 %collective-permute-start.20 = (f32[192,128]{1,0:T(8,128)S(1)}, f32[192,128]{1,0:T(8,128)S(1)}, u32[]{:S(2)}, u32[]{:S(2)}) collective-permute-start(f32[192,128]{1,0:T(8,128)S(1)} %get-tuple-element.110), channel_id=1, source_target_pairs={{0,32},{1,33},{2,34},{3,35},{4,36},{5,37},{6,38},{7,39},{8,40},{9,... | collective-permute-start | bytes 294920 | tf_op jit(solution)/shard_map/ppermute | solution.py:65
  67.8 1.4 %collective-permute-start.21 = (f32[192,128]{1,0:T(8,128)S(1)}, f32[192,128]{1,0:T(8,128)S(1)}, u32[]{:S(2)}, u32[]{:S(2)}) collective-permute-start(f32[192,128]{1,0:T(8,128)S(1)} %get-tuple-element.111), channel_id=1, source_target_pairs={{0,1},{1,0},{2,3},{3,2},{4,5},{5,4},{6,7},{7,6},{8,9},{9,8},{10,11... | collective-permute-start | bytes 294920 | tf_op jit(solution)/shard_map/ppermute | solution.py:64
  69.2 1.7 %shard_map.96 = (f32[8208,128]{1,0:T(8,128)S(1)}, f32[448,128]{1,0:T(8,128)S(1)}, f32[448,128]{1,0:T(8,128)S(1)}) custom-call(s32[2,3,3,32]{3,2,1,0:T(4,128)S(1)} %and_or_fusion.src, s32[1,3,3]{2,1,0:T(4,128)S(1)} %copy.41.count, s32[3]{0:T(128)S(1)} %pad_add_fusion.first, f32[8208,128]{1,0:T(8,128)S(1)} %get-tuple-element.102.u_in, ...), custom_call_target="tpu_custom_call", output_to_operand_aliasing={{0}: (3, {})} | custom-call | flops 2000000 | bytes 2000000 | tf_op jit(solution)/shard_map/pallas_call | solution.py:512
  71.0 1.3 %collective-permute-start.25 = (f32[448,128]{1,0:T(8,128)S(1)}, f32[448,128]{1,0:T(8,128)S(1)}, u32[]{:S(2)}, u32[]{:S(2)}) collective-permute-start(f32[448,128]{1,0:T(8,128)S(1)} %get-tuple-element.117), channel_id=1, source_target_pairs={{0,32},{1,2},{2,1},{3,4},{4,3},{5,6},{6,5},{7,8},{8,7},{9,10},{10,... | collective-permute-start | bytes 688136 | tf_op jit(solution)/shard_map/ppermute | solution.py:64
  72.3 1.0 %collective-permute-done.21.from_b = f32[192,128]{1,0:T(8,128)S(1)} collective-permute-done((f32[192,128]{1,0:T(8,128)S(1)}, f32[192,128]{1,0:T(8,128)S(1)}, u32[]{:S(2)}, u32[]{:S(2)}) %collective-permute-start.21) | collective-permute-done | bytes 98336 | tf_op jit(solution)/shard_map/ppermute | solution.py:64
  73.3 1.8 %shard_map.98 = (f32[8208,128]{1,0:T(8,128)S(1)}, f32[256,128]{1,0:T(8,128)S(1)}, f32[256,128]{1,0:T(8,128)S(1)}) custom-call(s32[2,3,3,32]{3,2,1,0:T(4,128)S(1)} %and_or_fusion.src, s32[1,3,3]{2,1,0:T(4,128)S(1)} %copy.41.count, s32[192]{0:T(256)S(1)} %maximum_convert_fusion.wanted, s32[3]{0:T(128)S(1)} %pad_add_fusion.first, ...), custom_call_target="tpu_custom_call", output_to_operand_aliasing={{0}: (4, {})} | custom-call | flops 2000000 | bytes 2000000 | tf_op jit(solution)/shard_map/pallas_call | solution.py:521
  75.1 0.1 collective-permute-start.22
  75.2 2.6 %collective-permute-start.23 = (f32[256,128]{1,0:T(8,128)S(1)}, f32[256,128]{1,0:T(8,128)S(1)}, u32[]{:S(2)}, u32[]{:S(2)}) collective-permute-start(f32[256,128]{1,0:T(8,128)S(1)} %get-tuple-element.115), channel_id=1, source_target_pairs={{0,32},{1,2},{2,1},{3,4},{4,3},{5,6},{6,5},{7,8},{8,7},{9,10},{10,... | collective-permute-start | bytes 393224 | tf_op jit(solution)/shard_map/ppermute | solution.py:64
  77.8 4.7 %shard_map.99 = (f32[8208,128]{1,0:T(8,128)S(1)}, f32[64,128]{1,0:T(8,128)S(1)}, f32[64,128]{1,0:T(8,128)S(1)}) custom-call(s32[2,3,3,32]{3,2,1,0:T(4,128)S(1)} %and_or_fusion.src, s32[1,3,3]{2,1,0:T(4,128)S(1)} %copy.41.count, s32[64]{0:T(128)S(1)} %pad_add_fusion.1.after.wanted_sec, f32[8208,128]{1,0:T(8,128)S(1)} %get-tuple-element.112.u_in, ...), custom_call_target="tpu_custom_call" | custom-call | flops 20000000 | bytes 20000000 | tf_op jit(solution)/shard_map/pallas_call | solution.py:499
  82.6 1.2 %collective-permute-done.23.from_b = f32[256,128]{1,0:T(8,128)S(1)} collective-permute-done((f32[256,128]{1,0:T(8,128)S(1)}, f32[256,128]{1,0:T(8,128)S(1)}, u32[]{:S(2)}, u32[]{:S(2)}) %collective-permute-start.23) | collective-permute-done | bytes 131104 | tf_op jit(solution)/shard_map/ppermute | solution.py:64
  83.8 1.3 %collective-permute-start.26 = (f32[192,128]{1,0:T(8,128)S(1)}, f32[192,128]{1,0:T(8,128)S(1)}, u32[]{:S(2)}, u32[]{:S(2)}) collective-permute-start(f32[192,128]{1,0:T(8,128)S(1)} %get-tuple-element.122), channel_id=1, source_target_pairs={{0,32},{1,33},{2,34},{3,35},{4,36},{5,37},{6,38},{7,39},{8,40},{9,... | collective-permute-start | bytes 294920 | tf_op jit(solution)/shard_map/ppermute | solution.py:65
  85.1 1.4 %collective-permute-start.27 = (f32[192,128]{1,0:T(8,128)S(1)}, f32[192,128]{1,0:T(8,128)S(1)}, u32[]{:S(2)}, u32[]{:S(2)}) collective-permute-start(f32[192,128]{1,0:T(8,128)S(1)} %get-tuple-element.123), channel_id=1, source_target_pairs={{0,1},{1,0},{2,3},{3,2},{4,5},{5,4},{6,7},{7,6},{8,9},{9,8},{10,11... | collective-permute-start | bytes 294920 | tf_op jit(solution)/shard_map/ppermute | solution.py:64
  86.5 3.5 %shard_map.100 = (f32[8208,128]{1,0:T(8,128)S(1)}, f32[2,16,16,2048]{3,2,1,0:T(8,128)}) custom-call(s32[2,3,3,32]{3,2,1,0:T(4,128)S(1)} %and_or_fusion.src, s32[1,3,3]{2,1,0:T(4,128)S(1)} %copy.41.count, s32[3]{0:T(128)S(1)} %pad_add_fusion.first, f32[8208,128]{1,0:T(8,128)S(1)} %get-tuple-element.113.u_in, ...), custom_call_target="tpu_custom_call", output_to_operand_aliasing={{0}: (3, {})} | custom-call | flops 4000000 | bytes 4000000 | tf_op jit(solution)/shard_map/pallas_call | solution.py:530
  90.0 0.7 collective-permute-done.27.from_b
  90.7 2.2 %shard_map.102 = (f32[8208,128]{1,0:T(8,128)S(1)}, f32[2,16,16,2048]{3,2,1,0:T(8,128)}) custom-call(s32[2,3,3,32]{3,2,1,0:T(4,128)S(1)} %and_or_fusion.src, s32[1,3,3]{2,1,0:T(4,128)S(1)} %copy.41.count, s32[3]{0:T(128)S(1)} %pad_add_fusion.first, f32[8208,128]{1,0:T(8,128)S(1)} %get-tuple-element.118.u_in, ...), custom_call_target="tpu_custom_call", output_to_operand_aliasing={{0}: (3, {}), {1}: (4, {})} | custom-call | flops 2000000 | bytes 2000000 | tf_op jit(solution)/shard_map/pallas_call | solution.py:540
  (54 shorter events, 1.0 us)
Async XLA Ops:
  0.0 12.0 %copy-start.1 = (s32[1,3,3]{2,0,1:T(1,128)S(1)}, s32[1,3,3]{2,0,1:T(1,128)}, u32[]{:S(2)}) copy-start(s32[1,3,3]{2,0,1:T(1,128)} %param.14) | copy-start | bytes 112
  0.0 12.0 %copy-start = (f32[1,3,3,32]{3,0,2,1:T(1,128)S(1)}, f32[1,3,3,32]{3,0,2,1:T(1,128)}, u32[]{:S(2)}) copy-start(f32[1,3,3,32]{3,0,2,1:T(1,128)} %param.15) | copy-start | bytes 3460
  0.0 7.4 %collective-permute-start = (s32[1,3,3,32]{3,0,2,1:T(1,128)}, s32[1,3,3,32]{3,0,2,1:T(1,128)S(1)}, u32[]{:S(2)}, u32[]{:S(2)}) collective-permute-start(s32[1,3,3,32]{3,0,2,1:T(1,128)} %param.13), channel_id=1, source_target_pairs={{0,32},{1,33},{2,34},{3,35},{4,36},{5,37},{6,38},{7,39},{8,40},{9,... | collective-permute-start | bytes 3464 | tf_op jit(solution)/shard_map/ppermute | solution.py:65
  0.7 6.8 %collective-permute-start.1 = (s32[1,3,3,32]{3,0,2,1:T(1,128)}, s32[1,3,3,32]{3,0,2,1:T(1,128)S(1)}, u32[]{:S(2)}, u32[]{:S(2)}) collective-permute-start(s32[1,3,3,32]{3,0,2,1:T(1,128)} %param.13), channel_id=1, source_target_pairs={{0,1},{1,0},{2,3},{3,2},{4,5},{5,4},{6,7},{7,6},{8,9},{9,8},{10,11... | collective-permute-start | bytes 3464 | tf_op jit(solution)/shard_map/ppermute | solution.py:64
  7.7 11.9 %collective-permute-start.3 = (f32[264,128]{1,0:T(8,128)S(1)}, f32[264,128]{1,0:T(8,128)S(1)}, u32[]{:S(2)}, u32[]{:S(2)}) collective-permute-start(f32[264,128]{1,0:T(8,128)S(1)} %get-tuple-element.126), channel_id=1, source_target_pairs={{0,32},{1,2},{2,1},{3,4},{4,3},{5,6},{6,5},{7,8},{8,7},{9,10},{10,... | collective-permute-start | bytes 405512 | tf_op jit(solution)/shard_map/ppermute | solution.py:64
  12.0 7.6 %collective-permute-start.2 = (f32[264,128]{1,0:T(8,128)S(1)}, f32[264,128]{1,0:T(8,128)S(1)}, u32[]{:S(2)}, u32[]{:S(2)}) collective-permute-start(f32[264,128]{1,0:T(8,128)S(1)} %get-tuple-element.125), channel_id=1, source_target_pairs={{0,1},{1,0},{2,3},{3,2},{4,5},{5,4},{6,7},{7,6},{8,9},{9,8},{10,11... | collective-permute-start | bytes 405512 | tf_op jit(solution)/shard_map/ppermute | solution.py:65
  15.7 19.8 %collective-permute-start.6 = (f32[448,128]{1,0:T(8,128)S(1)}, f32[448,128]{1,0:T(8,128)S(1)}, u32[]{:S(2)}, u32[]{:S(2)}) collective-permute-start(f32[448,128]{1,0:T(8,128)S(1)} %get-tuple-element.81), channel_id=1, source_target_pairs={{0,1},{1,0},{2,3},{3,2},{4,5},{5,4},{6,7},{7,6},{8,9},{9,8},{10,11... | collective-permute-start | bytes 688136 | tf_op jit(solution)/shard_map/ppermute | solution.py:65
  17.2 18.2 %collective-permute-start.7 = (f32[448,128]{1,0:T(8,128)S(1)}, f32[448,128]{1,0:T(8,128)S(1)}, u32[]{:S(2)}, u32[]{:S(2)}) collective-permute-start(f32[448,128]{1,0:T(8,128)S(1)} %get-tuple-element.82), channel_id=1, source_target_pairs={{0,32},{1,2},{2,1},{3,4},{4,3},{5,6},{6,5},{7,8},{8,7},{9,10},{10,... | collective-permute-start | bytes 688136 | tf_op jit(solution)/shard_map/ppermute | solution.py:64
  17.6 7.8 %copy-start.2 = (f32[128]{0:T(128)S(1)}, f32[128]{0:T(128)}, u32[]{:S(2)}) copy-start(f32[128]{0:T(128)} %param.11) | copy-start | bytes 1540
  20.6 11.4 %collective-permute-start.4 = (f32[256,128]{1,0:T(8,128)S(1)}, f32[256,128]{1,0:T(8,128)S(1)}, u32[]{:S(2)}, u32[]{:S(2)}) collective-permute-start(f32[256,128]{1,0:T(8,128)S(1)} %get-tuple-element.79), channel_id=1, source_target_pairs={{0,1},{1,0},{2,3},{3,2},{4,5},{5,4},{6,7},{7,6},{8,9},{9,8},{10,11... | collective-permute-start | bytes 393224 | tf_op jit(solution)/shard_map/ppermute | solution.py:65
  20.6 11.3 %collective-permute-start.5 = (f32[256,128]{1,0:T(8,128)S(1)}, f32[256,128]{1,0:T(8,128)S(1)}, u32[]{:S(2)}, u32[]{:S(2)}) collective-permute-start(f32[256,128]{1,0:T(8,128)S(1)} %get-tuple-element.80), channel_id=1, source_target_pairs={{0,32},{1,2},{2,1},{3,4},{4,3},{5,6},{6,5},{7,8},{8,7},{9,10},{10,... | collective-permute-start | bytes 393224 | tf_op jit(solution)/shard_map/ppermute | solution.py:64
  32.0 5.8 %collective-permute-start.8 = (f32[192,128]{1,0:T(8,128)S(1)}, f32[192,128]{1,0:T(8,128)S(1)}, u32[]{:S(2)}, u32[]{:S(2)}) collective-permute-start(f32[192,128]{1,0:T(8,128)S(1)} %get-tuple-element.88), channel_id=1, source_target_pairs={{0,32},{1,33},{2,34},{3,35},{4,36},{5,37},{6,38},{7,39},{8,40},{9,... | collective-permute-start | bytes 294920 | tf_op jit(solution)/shard_map/ppermute | solution.py:65
  32.0 5.7 %collective-permute-start.9 = (f32[192,128]{1,0:T(8,128)S(1)}, f32[192,128]{1,0:T(8,128)S(1)}, u32[]{:S(2)}, u32[]{:S(2)}) collective-permute-start(f32[192,128]{1,0:T(8,128)S(1)} %get-tuple-element.89), channel_id=1, source_target_pairs={{0,1},{1,0},{2,3},{3,2},{4,5},{5,4},{6,7},{7,6},{8,9},{9,8},{10,11... | collective-permute-start | bytes 294920 | tf_op jit(solution)/shard_map/ppermute | solution.py:64
  37.2 14.7 %collective-permute-start.12 = (f32[448,128]{1,0:T(8,128)S(1)}, f32[448,128]{1,0:T(8,128)S(1)}, u32[]{:S(2)}, u32[]{:S(2)}) collective-permute-start(f32[448,128]{1,0:T(8,128)S(1)} %get-tuple-element.94), channel_id=1, source_target_pairs={{0,1},{1,0},{2,3},{3,2},{4,5},{5,4},{6,7},{7,6},{8,9},{9,8},{10,11... | collective-permute-start | bytes 688136 | tf_op jit(solution)/shard_map/ppermute | solution.py:65
  37.3 14.6 %collective-permute-start.13 = (f32[448,128]{1,0:T(8,128)S(1)}, f32[448,128]{1,0:T(8,128)S(1)}, u32[]{:S(2)}, u32[]{:S(2)}) collective-permute-start(f32[448,128]{1,0:T(8,128)S(1)} %get-tuple-element.95), channel_id=1, source_target_pairs={{0,32},{1,2},{2,1},{3,4},{4,3},{5,6},{6,5},{7,8},{8,7},{9,10},{10,... | collective-permute-start | bytes 688136 | tf_op jit(solution)/shard_map/ppermute | solution.py:64
  39.5 9.3 %collective-permute-start.10 = (f32[256,128]{1,0:T(8,128)S(1)}, f32[256,128]{1,0:T(8,128)S(1)}, u32[]{:S(2)}, u32[]{:S(2)}) collective-permute-start(f32[256,128]{1,0:T(8,128)S(1)} %get-tuple-element.92), channel_id=1, source_target_pairs={{0,1},{1,0},{2,3},{3,2},{4,5},{5,4},{6,7},{7,6},{8,9},{9,8},{10,11... | collective-permute-start | bytes 393224 | tf_op jit(solution)/shard_map/ppermute | solution.py:65
  40.6 9.6 %collective-permute-start.11 = (f32[256,128]{1,0:T(8,128)S(1)}, f32[256,128]{1,0:T(8,128)S(1)}, u32[]{:S(2)}, u32[]{:S(2)}) collective-permute-start(f32[256,128]{1,0:T(8,128)S(1)} %get-tuple-element.93), channel_id=1, source_target_pairs={{0,32},{1,2},{2,1},{3,4},{4,3},{5,6},{6,5},{7,8},{8,7},{9,10},{10,... | collective-permute-start | bytes 393224 | tf_op jit(solution)/shard_map/ppermute | solution.py:64
  50.2 4.8 %collective-permute-start.14 = (f32[192,128]{1,0:T(8,128)S(1)}, f32[192,128]{1,0:T(8,128)S(1)}, u32[]{:S(2)}, u32[]{:S(2)}) collective-permute-start(f32[192,128]{1,0:T(8,128)S(1)} %get-tuple-element.99), channel_id=1, source_target_pairs={{0,32},{1,33},{2,34},{3,35},{4,36},{5,37},{6,38},{7,39},{8,40},{9,... | collective-permute-start | bytes 294920 | tf_op jit(solution)/shard_map/ppermute | solution.py:65
  50.6 5.5 %collective-permute-start.15 = (f32[192,128]{1,0:T(8,128)S(1)}, f32[192,128]{1,0:T(8,128)S(1)}, u32[]{:S(2)}, u32[]{:S(2)}) collective-permute-start(f32[192,128]{1,0:T(8,128)S(1)} %get-tuple-element.100), channel_id=1, source_target_pairs={{0,1},{1,0},{2,3},{3,2},{4,5},{5,4},{6,7},{7,6},{8,9},{9,8},{10,11... | collective-permute-start | bytes 294920 | tf_op jit(solution)/shard_map/ppermute | solution.py:64
  53.6 15.6 %collective-permute-start.18 = (f32[448,128]{1,0:T(8,128)S(1)}, f32[448,128]{1,0:T(8,128)S(1)}, u32[]{:S(2)}, u32[]{:S(2)}) collective-permute-start(f32[448,128]{1,0:T(8,128)S(1)} %get-tuple-element.105), channel_id=1, source_target_pairs={{0,1},{1,0},{2,3},{3,2},{4,5},{5,4},{6,7},{7,6},{8,9},{9,8},{10,11... | collective-permute-start | bytes 688136 | tf_op jit(solution)/shard_map/ppermute | solution.py:65
  53.7 15.5 %collective-permute-start.19 = (f32[448,128]{1,0:T(8,128)S(1)}, f32[448,128]{1,0:T(8,128)S(1)}, u32[]{:S(2)}, u32[]{:S(2)}) collective-permute-start(f32[448,128]{1,0:T(8,128)S(1)} %get-tuple-element.106), channel_id=1, source_target_pairs={{0,32},{1,2},{2,1},{3,4},{4,3},{5,6},{6,5},{7,8},{8,7},{9,10},{10,... | collective-permute-start | bytes 688136 | tf_op jit(solution)/shard_map/ppermute | solution.py:64
  57.9 7.4 %collective-permute-start.16 = (f32[256,128]{1,0:T(8,128)S(1)}, f32[256,128]{1,0:T(8,128)S(1)}, u32[]{:S(2)}, u32[]{:S(2)}) collective-permute-start(f32[256,128]{1,0:T(8,128)S(1)} %get-tuple-element.103), channel_id=1, source_target_pairs={{0,1},{1,0},{2,3},{3,2},{4,5},{5,4},{6,7},{7,6},{8,9},{9,8},{10,11... | collective-permute-start | bytes 393224 | tf_op jit(solution)/shard_map/ppermute | solution.py:65
  58.0 8.6 %collective-permute-start.17 = (f32[256,128]{1,0:T(8,128)S(1)}, f32[256,128]{1,0:T(8,128)S(1)}, u32[]{:S(2)}, u32[]{:S(2)}) collective-permute-start(f32[256,128]{1,0:T(8,128)S(1)} %get-tuple-element.104), channel_id=1, source_target_pairs={{0,32},{1,2},{2,1},{3,4},{4,3},{5,6},{6,5},{7,8},{8,7},{9,10},{10,... | collective-permute-start | bytes 393224 | tf_op jit(solution)/shard_map/ppermute | solution.py:64
  66.6 5.6 %collective-permute-start.20 = (f32[192,128]{1,0:T(8,128)S(1)}, f32[192,128]{1,0:T(8,128)S(1)}, u32[]{:S(2)}, u32[]{:S(2)}) collective-permute-start(f32[192,128]{1,0:T(8,128)S(1)} %get-tuple-element.110), channel_id=1, source_target_pairs={{0,32},{1,33},{2,34},{3,35},{4,36},{5,37},{6,38},{7,39},{8,40},{9,... | collective-permute-start | bytes 294920 | tf_op jit(solution)/shard_map/ppermute | solution.py:65
  67.8 5.5 %collective-permute-start.21 = (f32[192,128]{1,0:T(8,128)S(1)}, f32[192,128]{1,0:T(8,128)S(1)}, u32[]{:S(2)}, u32[]{:S(2)}) collective-permute-start(f32[192,128]{1,0:T(8,128)S(1)} %get-tuple-element.111), channel_id=1, source_target_pairs={{0,1},{1,0},{2,3},{3,2},{4,5},{5,4},{6,7},{7,6},{8,9},{9,8},{10,11... | collective-permute-start | bytes 294920 | tf_op jit(solution)/shard_map/ppermute | solution.py:64
  70.9 15.6 %collective-permute-start.24 = (f32[448,128]{1,0:T(8,128)S(1)}, f32[448,128]{1,0:T(8,128)S(1)}, u32[]{:S(2)}, u32[]{:S(2)}) collective-permute-start(f32[448,128]{1,0:T(8,128)S(1)} %get-tuple-element.116), channel_id=1, source_target_pairs={{0,1},{1,0},{2,3},{3,2},{4,5},{5,4},{6,7},{7,6},{8,9},{9,8},{10,11... | collective-permute-start | bytes 688136 | tf_op jit(solution)/shard_map/ppermute | solution.py:65
  71.0 15.5 %collective-permute-start.25 = (f32[448,128]{1,0:T(8,128)S(1)}, f32[448,128]{1,0:T(8,128)S(1)}, u32[]{:S(2)}, u32[]{:S(2)}) collective-permute-start(f32[448,128]{1,0:T(8,128)S(1)} %get-tuple-element.117), channel_id=1, source_target_pairs={{0,32},{1,2},{2,1},{3,4},{4,3},{5,6},{6,5},{7,8},{8,7},{9,10},{10,... | collective-permute-start | bytes 688136 | tf_op jit(solution)/shard_map/ppermute | solution.py:64
  75.1 7.5 %collective-permute-start.22 = (f32[256,128]{1,0:T(8,128)S(1)}, f32[256,128]{1,0:T(8,128)S(1)}, u32[]{:S(2)}, u32[]{:S(2)}) collective-permute-start(f32[256,128]{1,0:T(8,128)S(1)} %get-tuple-element.114), channel_id=1, source_target_pairs={{0,1},{1,0},{2,3},{3,2},{4,5},{5,4},{6,7},{7,6},{8,9},{9,8},{10,11... | collective-permute-start | bytes 393224 | tf_op jit(solution)/shard_map/ppermute | solution.py:65
  75.2 8.6 %collective-permute-start.23 = (f32[256,128]{1,0:T(8,128)S(1)}, f32[256,128]{1,0:T(8,128)S(1)}, u32[]{:S(2)}, u32[]{:S(2)}) collective-permute-start(f32[256,128]{1,0:T(8,128)S(1)} %get-tuple-element.115), channel_id=1, source_target_pairs={{0,32},{1,2},{2,1},{3,4},{4,3},{5,6},{6,5},{7,8},{8,7},{9,10},{10,... | collective-permute-start | bytes 393224 | tf_op jit(solution)/shard_map/ppermute | solution.py:64
  83.8 6.2 %collective-permute-start.26 = (f32[192,128]{1,0:T(8,128)S(1)}, f32[192,128]{1,0:T(8,128)S(1)}, u32[]{:S(2)}, u32[]{:S(2)}) collective-permute-start(f32[192,128]{1,0:T(8,128)S(1)} %get-tuple-element.122), channel_id=1, source_target_pairs={{0,32},{1,33},{2,34},{3,35},{4,36},{5,37},{6,38},{7,39},{8,40},{9,... | collective-permute-start | bytes 294920 | tf_op jit(solution)/shard_map/ppermute | solution.py:65
  85.1 5.5 %collective-permute-start.27 = (f32[192,128]{1,0:T(8,128)S(1)}, f32[192,128]{1,0:T(8,128)S(1)}, u32[]{:S(2)}, u32[]{:S(2)}) collective-permute-start(f32[192,128]{1,0:T(8,128)S(1)} %get-tuple-element.123), channel_id=1, source_target_pairs={{0,1},{1,0},{2,3},{3,2},{4,5},{5,4},{6,7},{7,6},{8,9},{9,8},{10,11... | collective-permute-start | bytes 294920 | tf_op jit(solution)/shard_map/ppermute | solution.py:64

commit v4 on v3

--- a/solution.py
+++ b/solution.py
@@ -26,6 +26,7 @@
 VM = pl.BlockSpec(memory_space=pltpu.VMEM)
 SM = pl.BlockSpec(memory_space=pltpu.SMEM)
 HB = pl.BlockSpec(memory_space=pltpu.HBM)
+ANY = pl.BlockSpec(memory_space=pl.ANY)
 
 
 def vmem(*shape):
@@ -88,10 +89,28 @@
 
 def live_slots(count, body):
     def group(i):
-        for j in range(4):
-            body(i * 4 + j)
-
-    loop((count + 3) // 4, group)
+        for j in range(8):
+            body(i * 8 + j)
+
+    loop((count + 7) // 8, group)
+
+
+def slots_at(a, e):
+    return (a * 3 + e) * CAP
+
+
+GROUP = 8
+
+
+def grouped_adds(block, count, term, ref, parts):
+    def group(i):
+        for j in range(GROUP):
+            place = block(i * GROUP + j)
+            old = [ref[pl.ds(place + part, 1), :] for part in parts]
+            for m, part in enumerate(parts):
+                ref[pl.ds(place + part, 1), :] = old[m] + term(i * GROUP + j, m)
+
+    loop((count + GROUP - 1) // GROUP, group)
 
 
 def setup_kernel(
@@ -164,7 +183,7 @@
     loop(INNER, section)
 
 
-def load_kernel(keep, field_in, kd_in, u_ref, rim_ref, buf, rim_buf, sems):
+def load_kernel(keep, src, weight, field_in, kd_in, u_ref, rim_ref, buf, rim_buf, sems):
     chunk = 4
 
     def copies(i):
@@ -199,13 +218,12 @@
 def diagonal_kernel(src, weight, count, dg_in, u_in, dg_ref, u_ref, cc_ref):
     for a in range(3):
         for e in range(3):
-            number = count[0, a, e]
-
-            def slot(k):
-                at = pl.ds(src[0, a, e, k], 1)
-                dg_ref[at, :] += jnp.where(k < number, weight[0, a, e, k], 0.0)
-
-            live_slots(number, slot)
+            number, base = count[0, a, e], slots_at(a, e)
+
+            def term(k, m):
+                return jnp.full((1, LANE), jnp.where(k < number, weight[base + k], 0.0), jnp.float32)
+
+            grouped_adds(lambda k: src[base + k], number, term, dg_ref, (0,))
 
     def section(s):
         for j in range(COLS):
@@ -234,11 +252,11 @@
     loop(SEC, rims)
     for i, a in enumerate((first[0], 1, 2 - first[0])):
         for j, e in enumerate((first[1], 1, 2 - first[1])):
-            number = count[0, a, e]
+            number, base = count[0, a, e], slots_at(a, e)
 
             def slot(k):
-                value = cc_ref[pl.ds(src[0, a, e, k], 1), :]
-                cw_ref[pl.ds((i * 3 + j) * CAP + k, 1), :] = value * jnp.where(k < number, weight[0, a, e, k], 0.0)
+                value = cc_ref[pl.ds(src[base + k], 1), :]
+                cw_ref[pl.ds((i * 3 + j) * CAP + k, 1), :] = value * jnp.where(k < number, weight[base + k], 0.0)
 
             live_slots(number, slot)
 
@@ -273,15 +291,11 @@
 
 
 def scatter(src, count, a, e, u_ref, term_ref, at, stride):
-    def slot(k):
-        block = src[0, a, e, k] + PAD
-        places = [pl.ds(block + m * PART, 1) for m in range(2)]
-        old = [u_ref[place, :] for place in places]
-        add = [term_ref[pl.ds(at + m * stride + k, 1), :] for m in range(2)]
-        for m in range(2):
-            u_ref[places[m], :] = old[m] + add[m]
-
-    live_slots(count[0, a, e], slot)
+    def term(k, m):
+        return term_ref[pl.ds(at + m * stride + k, 1), :]
+
+    base = slots_at(a, e)
+    grouped_adds(lambda k: src[base + k] + PAD, count[0, a, e], term, u_ref, (0, PART))
 
 
 LOCAL = 4 * CAP
@@ -321,7 +335,7 @@
                 here[m], here_turned[m], before[m] = after, after_turned, turned
 
     loop(SEC, section)
-    pack_blocks(lambda k: src[1, 1, 1, k], CAP, u_in, term_ref, 0, CAP)
+    pack_blocks(lambda k: src[(9 + 4) * CAP + k], CAP, u_in, term_ref, 0, CAP)
     fraction = frac_ref[...]
     scale = cw_ref[pl.ds(LOCAL, CAP), :]
     for m in range(2):
@@ -440,24 +454,26 @@
         pltpu.with_memory_space_constraint(x, pltpu.HBM) for x in (displacement, stiff_right, stiff_down)
     )
     asked_a, asked_b = exchange(match_target, match_target, "sec")
-    source = flat(jnp.concatenate([match_source, match_target]))
+    which = lax.broadcasted_iota(jnp.int32, (2,) + match_source.shape[1:], 0)
+    ids = flat(jnp.where(which == 0, match_source, match_target))
+    source, weight = ids.reshape(-1), match_weight.reshape(-1)
     asked_a, asked_b = flat(asked_a), flat(asked_b)
     rows = [vmem(ROW_MSG, LANE), vmem(ROW_MSG, LANE)]
     field = vmem(FIELD, LANE)
     u, rim = kernel_call(
         load_kernel,
         [field, vmem(RIM, LANE)],
-        [SM, HB, HB],
+        [SM, ANY, ANY, HB, HB],
         scratch=[vmem(2, SEC, ROW, WID), vmem(SEC, WID), pltpu.SemaphoreType.DMA((3, 4))],
         cost=6_000_000,
         limit=8,
-    )(keep, displacement, stiff_down)
+    )(keep, source, weight, displacement, stiff_down)
 
     def pick(array, a, e):
         return lax.dynamic_slice(array, (0, a, e, 0), (1, 1, 1, CAP)).reshape(CAP)
 
     def request(e):
-        asked = jnp.concatenate([pick(asked_a, 2 - first[0], e), pick(source[1:], 1, e), pick(asked_b, first[0], e)])
+        asked = jnp.concatenate([pick(asked_a, 2 - first[0], e), pick(ids[1:], 1, e), pick(asked_b, first[0], e)])
         asked = jnp.pad(asked.astype(jnp.float32).reshape(1, SEG), ((0, 7), (0, LANE - SEG)))
         return jnp.concatenate([rim, asked], axis=0)
 
@@ -480,7 +496,7 @@
         [SM, SM, SM, VM, VM],
         aliases={3: 0, 4: 1},
         cost=4_000_000,
-    )(source, match_weight, match_count, dg, u)
+    )(source, weight, match_count, dg, u)
     messages = [vmem(T_MSG, LANE), vmem(T_MSG, LANE)]
     u, to_a, to_b = kernel_call(pack_kernel, [field, *messages], [SM, SM, VM], aliases={2: 0}, cost=1_000_000)(
         wanted, first, u
@@ -491,7 +507,7 @@
         [SM] * 4 + [VM] * 6,
         aliases={8: 0, 9: 1},
         cost=1_000_000,
-    )(source, match_weight, match_count, first, dg, got_a, got_b, rim, cc, u)
+    )(source, weight, match_count, first, dg, got_a, got_b, rim, cc, u)
 
     whole = jax.ShapeDtypeStruct(displacement.shape, jnp.float32)
     for step in range(ITERS):

time: 93.1 us -> 92.1 us (0.989)
  Pallas kernels: 45.9 us -> 42.7 us
  starting transfers between devices: 37.9 us -> 38.9 us
    ppermute x14, starting transfers between devices: 31.2 us -> 32.7 us  [exchange(): from_b = lax.ppermute(to_b, ('sec', 'tile'), pairing(axis, 1))]
  transfers between devices with their start and end apart: 28 -> 28, of which waited for: 6 -> 6; matrix products, arithmetic and copies ran while one was open for 2% -> 3% of each run, Pallas kernels for 47% -> 44%
where the time goes in v4:
time: 92.1 us; the launch traced here: 91.9 us
  Pallas kernels  42.7 us (46%)
  starting transfers between devices  38.9 us (42%)
  waiting for transfers between devices  7.14 us (8%)
  local copies, waits for them, and re-layouts  1.63 us (2%)
  other arithmetic  1.16 us (1%)
    ppermute x14, starting transfers between devices, exchange(): from_b = lax.ppermute(to_b, ('sec', 'tile'), pairing(axis, 1))  32.7 us
    pallas_call x4, Pallas kernels, on_device(): kernel_call(dense_kernel, [field, vmem(2 * CAP, LANE), vmem(2 * CAP, LANE...  18.2 us
    ppermute x14, waiting for transfers between devices, exchange(): from_b = lax.ppermute(to_b, ('sec', 'tile'), pairing(axis, 1))  7.1 us
    ppermute x14, starting transfers between devices, exchange(): from_a = lax.ppermute(to_a, ('sec', 'tile'), pairing(axis, 0))  6.23 us
    pallas_call x3, Pallas kernels, on_device(): kernel_call(finish_kernel, [field] + messages, [SM] * 4 + [VM] * 5, alias...  4.68 us
    pallas_call x3, Pallas kernels, on_device(): kernel_call(tile_kernel, [field] + rows, [SM] * 3 + [VM] * 9, aliases={3:...  4.6 us
    pallas_call x1, Pallas kernels, on_device(): kernel_call(setup_kernel, [field, vmem(PART, LANE), vmem(PART + 2 * PAD,...  3.53 us
    pallas_call x1, Pallas kernels, on_device(): kernel_call(last_tile_kernel, [field, whole], [SM] * 3 + [VM] * 9, aliase...  3.36 us
  transfers between devices with their start and end apart: 28, of which 6 were waited for; matrix products, arithmetic and copies ran while one was open for 3% of the time, Pallas kernels for 44%

profile of v4, /device:TPU:7, one launch (start us, length us, event | category | flops | bytes accessed | tf_op | source)
XLA Modules:
  0.0 91.9 jit_solution(4529667733225109787)
XLA Ops:
  0.0 0.7 collective-permute-start
  0.7 2.9 %collective-permute-start.1 = (s32[1,3,3,32]{3,0,2,1:T(1,128)}, s32[1,3,3,32]{3,0,2,1:T(1,128)S(1)}, u32[]{:S(2)}, u32[]{:S(2)}) collective-permute-start(s32[1,3,3,32]{3,0,2,1:T(1,128)} %param.13), channel_id=1, source_target_pairs={{0,1},{1,0},{2,3},{3,2},{4,5},{5,4},{6,7},{7,6},{8,9},{9,8},{10,11... | collective-permute-start | bytes 3464 | tf_op jit(solution)/shard_map/ppermute | solution.py:65
  3.6 0.7 copy.56
  4.3 0.7 copy.57
  5.2 0.7 reduce
  5.9 0.1 reshape.132.weight
  6.0 2.4 %shard_map.82 = (f32[8208,128]{1,0:T(8,128)S(1)}, f32[256,128]{1,0:T(8,128)S(1)}) custom-call(f32[1]{0:T(128)} %bitcast.5.keep, s32[576]{0:T(1024)S(1)} %reshape.134.src, f32[288]{0:T(512)S(1)} %reshape.132.weight, f32[2,16,16,2048]{3,2,1,0:T(8,128)} %field_in.1, f32[16,16,2048]{2,1,0:T(8,128)} %kd_in.3), custom_call_target="tpu_custom_call" | custom-call | flops 6000000 | bytes 6000000 | tf_op jit(solution)/shard_map/pallas_call | solution.py:463
  8.6 4.2 %collective-permute-start.3 = (f32[264,128]{1,0:T(8,128)S(1)}, f32[264,128]{1,0:T(8,128)S(1)}, u32[]{:S(2)}, u32[]{:S(2)}) collective-permute-start(f32[264,128]{1,0:T(8,128)S(1)} %get-tuple-element.126), channel_id=1, source_target_pairs={{0,32},{1,2},{2,1},{3,4},{4,3},{5,6},{6,5},{7,8},{8,7},{9,10},{10,... | collective-permute-start | bytes 405512 | tf_op jit(solution)/shard_map/ppermute | solution.py:65
  13.0 3.5 %shard_map.83 = (f32[8208,128]{1,0:T(8,128)S(1)}, f32[4096,128]{1,0:T(8,128)S(1)}, f32[4112,128]{1,0:T(8,128)S(1)}, f32[4096,128]{1,0:T(8,128)S(1)}, f32[448,128]{1,0:T(8,128)S(1)}, /*index=5*/f32[448,128]{1,0:T(8,128)S(1)}) custom-call(s32[3]{0:T(128)S(1)} %pad_add_fusion.first, ...), custom_call_target="tpu_custom_call", output_to_operand_aliasing={{0}: (3, {})} | custom-call | flops 6000000 | bytes 6000000 | tf_op jit(solution)/shard_map/pallas_call | solution.py:483
  16.5 1.5 %collective-permute-start.6 = (f32[448,128]{1,0:T(8,128)S(1)}, f32[448,128]{1,0:T(8,128)S(1)}, u32[]{:S(2)}, u32[]{:S(2)}) collective-permute-start(f32[448,128]{1,0:T(8,128)S(1)} %get-tuple-element.81), channel_id=1, source_target_pairs={{0,1},{1,0},{2,3},{3,2},{4,5},{5,4},{6,7},{7,6},{8,9},{9,8},{10,11... | collective-permute-start | bytes 688136 | tf_op jit(solution)/shard_map/ppermute | solution.py:66
  18.1 0.3 collective-permute-start.7
  18.4 1.6 %shard_map.84 = (f32[4096,128]{1,0:T(8,128)S(1)}, f32[8208,128]{1,0:T(8,128)S(1)}, f32[4096,128]{1,0:T(8,128)S(1)}) custom-call(s32[576]{0:T(1024)S(1)} %reshape.134.src, f32[288]{0:T(512)S(1)} %reshape.132.weight, s32[1,3,3]{2,1,0:T(4,128)S(1)} %copy.51.count, ...), custom_call_target="tpu_custom_call", output_to_operand_aliasing={{0}: (3, {}), {1}: (4, {})} | custom-call | flops 4000000 | bytes 4000000 | tf_op jit(solution)/shard_map/pallas_call | solution.py:493
  20.1 0.9 shard_map.85
  21.1 0.1 collective-permute-start.4
  21.2 4.5 %collective-permute-start.5 = (f32[256,128]{1,0:T(8,128)S(1)}, f32[256,128]{1,0:T(8,128)S(1)}, u32[]{:S(2)}, u32[]{:S(2)}) collective-permute-start(f32[256,128]{1,0:T(8,128)S(1)} %get-tuple-element.80), channel_id=1, source_target_pairs={{0,32},{1,2},{2,1},{3,4},{4,3},{5,6},{6,5},{7,8},{8,7},{9,10},{10,... | collective-permute-start | bytes 393224 | tf_op jit(solution)/shard_map/ppermute | solution.py:65
  25.7 1.4 %shard_map.86 = (f32[4096,128]{1,0:T(8,128)S(1)}, f32[8208,128]{1,0:T(8,128)S(1)}, f32[256,128]{1,0:T(8,128)S(1)}, f32[256,128]{1,0:T(8,128)S(1)}, f32[288,128]{1,0:T(8,128)S(1)}) custom-call(s32[576]{0:T(1024)S(1)} %reshape.134.src, f32[288]{0:T(512)S(1)} %reshape.132.weight, ...), custom_call_target="tpu_custom_call", output_to_operand_aliasing={{0}: (8, {}), {1}: (9, {})} | custom-call | flops 1000000 | bytes 1000000 | tf_op jit(solution)/shard_map/pallas_call | solution.py:504
  27.0 4.5 %shard_map.87 = (f32[8208,128]{1,0:T(8,128)S(1)}, f32[64,128]{1,0:T(8,128)S(1)}, f32[64,128]{1,0:T(8,128)S(1)}) custom-call(s32[576]{0:T(1024)S(1)} %reshape.134.src, s32[1,3,3]{2,1,0:T(4,128)S(1)} %copy.51.count, s32[64]{0:T(128)S(1)} %pad_add_fusion.1.after.wanted_sec, f32[8208,128]{1,0:T(8,128)S(1)} %get-tuple-element.73.u_in, ...), custom_call_target="tpu_custom_call" | custom-call | flops 20000000 | bytes 20000000 | tf_op jit(solution)/shard_map/pallas_call | solution.py:515
  31.7 3.5 %collective-permute-start.9 = (f32[192,128]{1,0:T(8,128)S(1)}, f32[192,128]{1,0:T(8,128)S(1)}, u32[]{:S(2)}, u32[]{:S(2)}) collective-permute-start(f32[192,128]{1,0:T(8,128)S(1)} %get-tuple-element.89), channel_id=1, source_target_pairs={{0,1},{1,0},{2,3},{3,2},{4,5},{5,4},{6,7},{7,6},{8,9},{9,8},{10,11... | collective-permute-start | bytes 294920 | tf_op jit(solution)/shard_map/ppermute | solution.py:65
  35.2 1.5 %shard_map.88 = (f32[8208,128]{1,0:T(8,128)S(1)}, f32[448,128]{1,0:T(8,128)S(1)}, f32[448,128]{1,0:T(8,128)S(1)}) custom-call(s32[576]{0:T(1024)S(1)} %reshape.134.src, s32[1,3,3]{2,1,0:T(4,128)S(1)} %copy.51.count, s32[3]{0:T(128)S(1)} %pad_add_fusion.first, f32[8208,128]{1,0:T(8,128)S(1)} %get-tuple-element.78.u_in, ...), custom_call_target="tpu_custom_call", output_to_operand_aliasing={{0}: (3, {})} | custom-call | flops 2000000 | bytes 2000000 | tf_op jit(solution)/shard_map/pallas_call | solution.py:528
  36.8 1.2 %collective-permute-start.13 = (f32[448,128]{1,0:T(8,128)S(1)}, f32[448,128]{1,0:T(8,128)S(1)}, u32[]{:S(2)}, u32[]{:S(2)}) collective-permute-start(f32[448,128]{1,0:T(8,128)S(1)} %get-tuple-element.95), channel_id=1, source_target_pairs={{0,32},{1,2},{2,1},{3,4},{4,3},{5,6},{6,5},{7,8},{8,7},{9,10},{10,... | collective-permute-start | bytes 688136 | tf_op jit(solution)/shard_map/ppermute | solution.py:65
  38.0 1.6 %shard_map.90 = (f32[8208,128]{1,0:T(8,128)S(1)}, f32[256,128]{1,0:T(8,128)S(1)}, f32[256,128]{1,0:T(8,128)S(1)}) custom-call(s32[576]{0:T(1024)S(1)} %reshape.134.src, s32[1,3,3]{2,1,0:T(4,128)S(1)} %copy.51.count, s32[192]{0:T(256)S(1)} %maximum_convert_fusion.wanted, s32[3]{0:T(128)S(1)} %pad_add_fusion.first, ...), custom_call_target="tpu_custom_call", output_to_operand_aliasing={{0}: (4, {})} | custom-call | flops 2000000 | bytes 2000000 | tf_op jit(solution)/shard_map/pallas_call | solution.py:537
  39.5 0.4 collective-permute-start.10
  39.9 3.4 %collective-permute-start.11 = (f32[256,128]{1,0:T(8,128)S(1)}, f32[256,128]{1,0:T(8,128)S(1)}, u32[]{:S(2)}, u32[]{:S(2)}) collective-permute-start(f32[256,128]{1,0:T(8,128)S(1)} %get-tuple-element.93), channel_id=1, source_target_pairs={{0,32},{1,2},{2,1},{3,4},{4,3},{5,6},{6,5},{7,8},{8,7},{9,10},{10,... | collective-permute-start | bytes 393224 | tf_op jit(solution)/shard_map/ppermute | solution.py:65
  43.3 4.5 %shard_map.91 = (f32[8208,128]{1,0:T(8,128)S(1)}, f32[64,128]{1,0:T(8,128)S(1)}, f32[64,128]{1,0:T(8,128)S(1)}) custom-call(s32[576]{0:T(1024)S(1)} %reshape.134.src, s32[1,3,3]{2,1,0:T(4,128)S(1)} %copy.51.count, s32[64]{0:T(128)S(1)} %pad_add_fusion.1.after.wanted_sec, f32[8208,128]{1,0:T(8,128)S(1)} %get-tuple-element.90.u_in, ...), custom_call_target="tpu_custom_call" | custom-call | flops 20000000 | bytes 20000000 | tf_op jit(solution)/shard_map/pallas_call | solution.py:515
  47.9 1.8 %collective-permute-done.11.from_b = f32[256,128]{1,0:T(8,128)S(1)} collective-permute-done((f32[256,128]{1,0:T(8,128)S(1)}, f32[256,128]{1,0:T(8,128)S(1)}, u32[]{:S(2)}, u32[]{:S(2)}) %collective-permute-start.11) | collective-permute-done | bytes 131104 | tf_op jit(solution)/shard_map/ppermute | solution.py:65
  49.7 0.3 collective-permute-start.14
  50.0 1.5 %collective-permute-start.15 = (f32[192,128]{1,0:T(8,128)S(1)}, f32[192,128]{1,0:T(8,128)S(1)}, u32[]{:S(2)}, u32[]{:S(2)}) collective-permute-start(f32[192,128]{1,0:T(8,128)S(1)} %get-tuple-element.100), channel_id=1, source_target_pairs={{0,1},{1,0},{2,3},{3,2},{4,5},{5,4},{6,7},{7,6},{8,9},{9,8},{10,11... | collective-permute-start | bytes 294920 | tf_op jit(solution)/shard_map/ppermute | solution.py:65
  51.5 1.5 %shard_map.92 = (f32[8208,128]{1,0:T(8,128)S(1)}, f32[448,128]{1,0:T(8,128)S(1)}, f32[448,128]{1,0:T(8,128)S(1)}) custom-call(s32[576]{0:T(1024)S(1)} %reshape.134.src, s32[1,3,3]{2,1,0:T(4,128)S(1)} %copy.51.count, s32[3]{0:T(128)S(1)} %pad_add_fusion.first, f32[8208,128]{1,0:T(8,128)S(1)} %get-tuple-element.91.u_in, ...), custom_call_target="tpu_custom_call", output_to_operand_aliasing={{0}: (3, {})} | custom-call | flops 2000000 | bytes 2000000 | tf_op jit(solution)/shard_map/pallas_call | solution.py:528
  53.1 1.9 %collective-permute-start.19 = (f32[448,128]{1,0:T(8,128)S(1)}, f32[448,128]{1,0:T(8,128)S(1)}, u32[]{:S(2)}, u32[]{:S(2)}) collective-permute-start(f32[448,128]{1,0:T(8,128)S(1)} %get-tuple-element.106), channel_id=1, source_target_pairs={{0,32},{1,2},{2,1},{3,4},{4,3},{5,6},{6,5},{7,8},{8,7},{9,10},{10,... | collective-permute-start | bytes 688136 | tf_op jit(solution)/shard_map/ppermute | solution.py:65
  55.0 0.5 collective-permute-done.15.from_b
  55.5 1.6 %shard_map.94 = (f32[8208,128]{1,0:T(8,128)S(1)}, f32[256,128]{1,0:T(8,128)S(1)}, f32[256,128]{1,0:T(8,128)S(1)}) custom-call(s32[576]{0:T(1024)S(1)} %reshape.134.src, s32[1,3,3]{2,1,0:T(4,128)S(1)} %copy.51.count, s32[192]{0:T(256)S(1)} %maximum_convert_fusion.wanted, s32[3]{0:T(128)S(1)} %pad_add_fusion.first, ...), custom_call_target="tpu_custom_call", output_to_operand_aliasing={{0}: (4, {})} | custom-call | flops 2000000 | bytes 2000000 | tf_op jit(solution)/shard_map/pallas_call | solution.py:537
  57.2 2.4 %collective-permute-start.17 = (f32[256,128]{1,0:T(8,128)S(1)}, f32[256,128]{1,0:T(8,128)S(1)}, u32[]{:S(2)}, u32[]{:S(2)}) collective-permute-start(f32[256,128]{1,0:T(8,128)S(1)} %get-tuple-element.104), channel_id=1, source_target_pairs={{0,32},{1,2},{2,1},{3,4},{4,3},{5,6},{6,5},{7,8},{8,7},{9,10},{10,... | collective-permute-start | bytes 393224 | tf_op jit(solution)/shard_map/ppermute | solution.py:65
  59.6 4.6 %shard_map.95 = (f32[8208,128]{1,0:T(8,128)S(1)}, f32[64,128]{1,0:T(8,128)S(1)}, f32[64,128]{1,0:T(8,128)S(1)}) custom-call(s32[576]{0:T(1024)S(1)} %reshape.134.src, s32[1,3,3]{2,1,0:T(4,128)S(1)} %copy.51.count, s32[64]{0:T(128)S(1)} %pad_add_fusion.1.after.wanted_sec, f32[8208,128]{1,0:T(8,128)S(1)} %get-tuple-element.101.u_in, ...), custom_call_target="tpu_custom_call" | custom-call | flops 20000000 | bytes 20000000 | tf_op jit(solution)/shard_map/pallas_call | solution.py:515
  64.3 1.5 %collective-permute-done.17.from_b = f32[256,128]{1,0:T(8,128)S(1)} collective-permute-done((f32[256,128]{1,0:T(8,128)S(1)}, f32[256,128]{1,0:T(8,128)S(1)}, u32[]{:S(2)}, u32[]{:S(2)}) %collective-permute-start.17) | collective-permute-done | bytes 131104 | tf_op jit(solution)/shard_map/ppermute | solution.py:65
  65.8 1.4 %collective-permute-start.20 = (f32[192,128]{1,0:T(8,128)S(1)}, f32[192,128]{1,0:T(8,128)S(1)}, u32[]{:S(2)}, u32[]{:S(2)}) collective-permute-start(f32[192,128]{1,0:T(8,128)S(1)} %get-tuple-element.110), channel_id=1, source_target_pairs={{0,32},{1,33},{2,34},{3,35},{4,36},{5,37},{6,38},{7,39},{8,40},{9,... | collective-permute-start | bytes 294920 | tf_op jit(solution)/shard_map/ppermute | solution.py:66
  67.2 1.4 %collective-permute-start.21 = (f32[192,128]{1,0:T(8,128)S(1)}, f32[192,128]{1,0:T(8,128)S(1)}, u32[]{:S(2)}, u32[]{:S(2)}) collective-permute-start(f32[192,128]{1,0:T(8,128)S(1)} %get-tuple-element.111), channel_id=1, source_target_pairs={{0,1},{1,0},{2,3},{3,2},{4,5},{5,4},{6,7},{7,6},{8,9},{9,8},{10,11... | collective-permute-start | bytes 294920 | tf_op jit(solution)/shard_map/ppermute | solution.py:65
  68.6 1.5 %shard_map.96 = (f32[8208,128]{1,0:T(8,128)S(1)}, f32[448,128]{1,0:T(8,128)S(1)}, f32[448,128]{1,0:T(8,128)S(1)}) custom-call(s32[576]{0:T(1024)S(1)} %reshape.134.src, s32[1,3,3]{2,1,0:T(4,128)S(1)} %copy.51.count, s32[3]{0:T(128)S(1)} %pad_add_fusion.first, f32[8208,128]{1,0:T(8,128)S(1)} %get-tuple-element.102.u_in, ...), custom_call_target="tpu_custom_call", output_to_operand_aliasing={{0}: (3, {})} | custom-call | flops 2000000 | bytes 2000000 | tf_op jit(solution)/shard_map/pallas_call | solution.py:528
  70.3 1.7 %collective-permute-start.25 = (f32[448,128]{1,0:T(8,128)S(1)}, f32[448,128]{1,0:T(8,128)S(1)}, u32[]{:S(2)}, u32[]{:S(2)}) collective-permute-start(f32[448,128]{1,0:T(8,128)S(1)} %get-tuple-element.117), channel_id=1, source_target_pairs={{0,32},{1,2},{2,1},{3,4},{4,3},{5,6},{6,5},{7,8},{8,7},{9,10},{10,... | collective-permute-start | bytes 688136 | tf_op jit(solution)/shard_map/ppermute | solution.py:65
  72.0 0.8 collective-permute-done.21.from_b
  72.8 1.6 %shard_map.98 = (f32[8208,128]{1,0:T(8,128)S(1)}, f32[256,128]{1,0:T(8,128)S(1)}, f32[256,128]{1,0:T(8,128)S(1)}) custom-call(s32[576]{0:T(1024)S(1)} %reshape.134.src, s32[1,3,3]{2,1,0:T(4,128)S(1)} %copy.51.count, s32[192]{0:T(256)S(1)} %maximum_convert_fusion.wanted, s32[3]{0:T(128)S(1)} %pad_add_fusion.first, ...), custom_call_target="tpu_custom_call", output_to_operand_aliasing={{0}: (4, {})} | custom-call | flops 2000000 | bytes 2000000 | tf_op jit(solution)/shard_map/pallas_call | solution.py:537
  74.4 2.4 %collective-permute-start.23 = (f32[256,128]{1,0:T(8,128)S(1)}, f32[256,128]{1,0:T(8,128)S(1)}, u32[]{:S(2)}, u32[]{:S(2)}) collective-permute-start(f32[256,128]{1,0:T(8,128)S(1)} %get-tuple-element.115), channel_id=1, source_target_pairs={{0,32},{1,2},{2,1},{3,4},{4,3},{5,6},{6,5},{7,8},{8,7},{9,10},{10,... | collective-permute-start | bytes 393224 | tf_op jit(solution)/shard_map/ppermute | solution.py:65
  76.8 4.5 %shard_map.99 = (f32[8208,128]{1,0:T(8,128)S(1)}, f32[64,128]{1,0:T(8,128)S(1)}, f32[64,128]{1,0:T(8,128)S(1)}) custom-call(s32[576]{0:T(1024)S(1)} %reshape.134.src, s32[1,3,3]{2,1,0:T(4,128)S(1)} %copy.51.count, s32[64]{0:T(128)S(1)} %pad_add_fusion.1.after.wanted_sec, f32[8208,128]{1,0:T(8,128)S(1)} %get-tuple-element.112.u_in, ...), custom_call_target="tpu_custom_call" | custom-call | flops 20000000 | bytes 20000000 | tf_op jit(solution)/shard_map/pallas_call | solution.py:515
  81.3 1.7 %collective-permute-done.23.from_b = f32[256,128]{1,0:T(8,128)S(1)} collective-permute-done((f32[256,128]{1,0:T(8,128)S(1)}, f32[256,128]{1,0:T(8,128)S(1)}, u32[]{:S(2)}, u32[]{:S(2)}) %collective-permute-start.23) | collective-permute-done | bytes 131104 | tf_op jit(solution)/shard_map/ppermute | solution.py:65
  83.0 1.3 %collective-permute-start.26 = (f32[192,128]{1,0:T(8,128)S(1)}, f32[192,128]{1,0:T(8,128)S(1)}, u32[]{:S(2)}, u32[]{:S(2)}) collective-permute-start(f32[192,128]{1,0:T(8,128)S(1)} %get-tuple-element.122), channel_id=1, source_target_pairs={{0,32},{1,33},{2,34},{3,35},{4,36},{5,37},{6,38},{7,39},{8,40},{9,... | collective-permute-start | bytes 294920 | tf_op jit(solution)/shard_map/ppermute | solution.py:66
  84.4 1.4 %collective-permute-start.27 = (f32[192,128]{1,0:T(8,128)S(1)}, f32[192,128]{1,0:T(8,128)S(1)}, u32[]{:S(2)}, u32[]{:S(2)}) collective-permute-start(f32[192,128]{1,0:T(8,128)S(1)} %get-tuple-element.123), channel_id=1, source_target_pairs={{0,1},{1,0},{2,3},{3,2},{4,5},{5,4},{6,7},{7,6},{8,9},{9,8},{10,11... | collective-permute-start | bytes 294920 | tf_op jit(solution)/shard_map/ppermute | solution.py:65
  85.8 3.4 %shard_map.100 = (f32[8208,128]{1,0:T(8,128)S(1)}, f32[2,16,16,2048]{3,2,1,0:T(8,128)}) custom-call(s32[576]{0:T(1024)S(1)} %reshape.134.src, s32[1,3,3]{2,1,0:T(4,128)S(1)} %copy.51.count, s32[3]{0:T(128)S(1)} %pad_add_fusion.first, f32[8208,128]{1,0:T(8,128)S(1)} %get-tuple-element.113.u_in, ...), custom_call_target="tpu_custom_call", output_to_operand_aliasing={{0}: (3, {})} | custom-call | flops 4000000 | bytes 4000000 | tf_op jit(solution)/shard_map/pallas_call | solution.py:546
  89.2 0.8 collective-permute-done.27.from_b
  89.9 2.0 %shard_map.102 = (f32[8208,128]{1,0:T(8,128)S(1)}, f32[2,16,16,2048]{3,2,1,0:T(8,128)}) custom-call(s32[576]{0:T(1024)S(1)} %reshape.134.src, s32[1,3,3]{2,1,0:T(4,128)S(1)} %copy.51.count, s32[3]{0:T(128)S(1)} %pad_add_fusion.first, f32[8208,128]{1,0:T(8,128)S(1)} %get-tuple-element.118.u_in, ...), custom_call_target="tpu_custom_call", output_to_operand_aliasing={{0}: (3, {}), {1}: (4, {})} | custom-call | flops 2000000 | bytes 2000000 | tf_op jit(solution)/shard_map/pallas_call | solution.py:556
  (55 shorter events, 1.2 us)
Async XLA Ops:
  0.0 12.9 %copy-start = (s32[1,3,3]{2,0,1:T(1,128)S(1)}, s32[1,3,3]{2,0,1:T(1,128)}, u32[]{:S(2)}) copy-start(s32[1,3,3]{2,0,1:T(1,128)} %param.14) | copy-start | bytes 112
  0.0 8.4 %collective-permute-start = (s32[1,3,3,32]{3,0,2,1:T(1,128)}, s32[1,3,3,32]{3,0,2,1:T(1,128)S(1)}, u32[]{:S(2)}, u32[]{:S(2)}) collective-permute-start(s32[1,3,3,32]{3,0,2,1:T(1,128)} %param.13), channel_id=1, source_target_pairs={{0,32},{1,33},{2,34},{3,35},{4,36},{5,37},{6,38},{7,39},{8,40},{9,... | collective-permute-start | bytes 3464 | tf_op jit(solution)/shard_map/ppermute | solution.py:66
  0.7 7.7 %collective-permute-start.1 = (s32[1,3,3,32]{3,0,2,1:T(1,128)}, s32[1,3,3,32]{3,0,2,1:T(1,128)S(1)}, u32[]{:S(2)}, u32[]{:S(2)}) collective-permute-start(s32[1,3,3,32]{3,0,2,1:T(1,128)} %param.13), channel_id=1, source_target_pairs={{0,1},{1,0},{2,3},{3,2},{4,5},{5,4},{6,7},{7,6},{8,9},{9,8},{10,11... | collective-permute-start | bytes 3464 | tf_op jit(solution)/shard_map/ppermute | solution.py:65
  8.6 11.4 %collective-permute-start.3 = (f32[264,128]{1,0:T(8,128)S(1)}, f32[264,128]{1,0:T(8,128)S(1)}, u32[]{:S(2)}, u32[]{:S(2)}) collective-permute-start(f32[264,128]{1,0:T(8,128)S(1)} %get-tuple-element.126), channel_id=1, source_target_pairs={{0,32},{1,2},{2,1},{3,4},{4,3},{5,6},{6,5},{7,8},{8,7},{9,10},{10,... | collective-permute-start | bytes 405512 | tf_op jit(solution)/shard_map/ppermute | solution.py:65
  12.9 7.2 %collective-permute-start.2 = (f32[264,128]{1,0:T(8,128)S(1)}, f32[264,128]{1,0:T(8,128)S(1)}, u32[]{:S(2)}, u32[]{:S(2)}) collective-permute-start(f32[264,128]{1,0:T(8,128)S(1)} %get-tuple-element.125), channel_id=1, source_target_pairs={{0,1},{1,0},{2,3},{3,2},{4,5},{5,4},{6,7},{7,6},{8,9},{9,8},{10,11... | collective-permute-start | bytes 405512 | tf_op jit(solution)/shard_map/ppermute | solution.py:66
  16.5 18.6 %collective-permute-start.6 = (f32[448,128]{1,0:T(8,128)S(1)}, f32[448,128]{1,0:T(8,128)S(1)}, u32[]{:S(2)}, u32[]{:S(2)}) collective-permute-start(f32[448,128]{1,0:T(8,128)S(1)} %get-tuple-element.81), channel_id=1, source_target_pairs={{0,1},{1,0},{2,3},{3,2},{4,5},{5,4},{6,7},{7,6},{8,9},{9,8},{10,11... | collective-permute-start | bytes 688136 | tf_op jit(solution)/shard_map/ppermute | solution.py:66
  18.1 17.1 %collective-permute-start.7 = (f32[448,128]{1,0:T(8,128)S(1)}, f32[448,128]{1,0:T(8,128)S(1)}, u32[]{:S(2)}, u32[]{:S(2)}) collective-permute-start(f32[448,128]{1,0:T(8,128)S(1)} %get-tuple-element.82), channel_id=1, source_target_pairs={{0,32},{1,2},{2,1},{3,4},{4,3},{5,6},{6,5},{7,8},{8,7},{9,10},{10,... | collective-permute-start | bytes 688136 | tf_op jit(solution)/shard_map/ppermute | solution.py:65
  18.4 7.3 %copy-start.1 = (f32[128]{0:T(128)S(1)}, f32[128]{0:T(128)}, u32[]{:S(2)}) copy-start(f32[128]{0:T(128)} %param.11) | copy-start | bytes 1540
  21.1 10.5 %collective-permute-start.4 = (f32[256,128]{1,0:T(8,128)S(1)}, f32[256,128]{1,0:T(8,128)S(1)}, u32[]{:S(2)}, u32[]{:S(2)}) collective-permute-start(f32[256,128]{1,0:T(8,128)S(1)} %get-tuple-element.79), channel_id=1, source_target_pairs={{0,1},{1,0},{2,3},{3,2},{4,5},{5,4},{6,7},{7,6},{8,9},{9,8},{10,11... | collective-permute-start | bytes 393224 | tf_op jit(solution)/shard_map/ppermute | solution.py:66
  21.2 10.4 %collective-permute-start.5 = (f32[256,128]{1,0:T(8,128)S(1)}, f32[256,128]{1,0:T(8,128)S(1)}, u32[]{:S(2)}, u32[]{:S(2)}) collective-permute-start(f32[256,128]{1,0:T(8,128)S(1)} %get-tuple-element.80), channel_id=1, source_target_pairs={{0,32},{1,2},{2,1},{3,4},{4,3},{5,6},{6,5},{7,8},{8,7},{9,10},{10,... | collective-permute-start | bytes 393224 | tf_op jit(solution)/shard_map/ppermute | solution.py:65
  31.6 6.4 %collective-permute-start.8 = (f32[192,128]{1,0:T(8,128)S(1)}, f32[192,128]{1,0:T(8,128)S(1)}, u32[]{:S(2)}, u32[]{:S(2)}) collective-permute-start(f32[192,128]{1,0:T(8,128)S(1)} %get-tuple-element.88), channel_id=1, source_target_pairs={{0,32},{1,33},{2,34},{3,35},{4,36},{5,37},{6,38},{7,39},{8,40},{9,... | collective-permute-start | bytes 294920 | tf_op jit(solution)/shard_map/ppermute | solution.py:66
  31.7 6.3 %collective-permute-start.9 = (f32[192,128]{1,0:T(8,128)S(1)}, f32[192,128]{1,0:T(8,128)S(1)}, u32[]{:S(2)}, u32[]{:S(2)}) collective-permute-start(f32[192,128]{1,0:T(8,128)S(1)} %get-tuple-element.89), channel_id=1, source_target_pairs={{0,1},{1,0},{2,3},{3,2},{4,5},{5,4},{6,7},{7,6},{8,9},{9,8},{10,11... | collective-permute-start | bytes 294920 | tf_op jit(solution)/shard_map/ppermute | solution.py:65
  36.7 14.7 %collective-permute-start.12 = (f32[448,128]{1,0:T(8,128)S(1)}, f32[448,128]{1,0:T(8,128)S(1)}, u32[]{:S(2)}, u32[]{:S(2)}) collective-permute-start(f32[448,128]{1,0:T(8,128)S(1)} %get-tuple-element.94), channel_id=1, source_target_pairs={{0,1},{1,0},{2,3},{3,2},{4,5},{5,4},{6,7},{7,6},{8,9},{9,8},{10,11... | collective-permute-start | bytes 688136 | tf_op jit(solution)/shard_map/ppermute | solution.py:66
  36.8 14.7 %collective-permute-start.13 = (f32[448,128]{1,0:T(8,128)S(1)}, f32[448,128]{1,0:T(8,128)S(1)}, u32[]{:S(2)}, u32[]{:S(2)}) collective-permute-start(f32[448,128]{1,0:T(8,128)S(1)} %get-tuple-element.95), channel_id=1, source_target_pairs={{0,32},{1,2},{2,1},{3,4},{4,3},{5,6},{6,5},{7,8},{8,7},{9,10},{10,... | collective-permute-start | bytes 688136 | tf_op jit(solution)/shard_map/ppermute | solution.py:65
  39.5 8.3 %collective-permute-start.10 = (f32[256,128]{1,0:T(8,128)S(1)}, f32[256,128]{1,0:T(8,128)S(1)}, u32[]{:S(2)}, u32[]{:S(2)}) collective-permute-start(f32[256,128]{1,0:T(8,128)S(1)} %get-tuple-element.92), channel_id=1, source_target_pairs={{0,1},{1,0},{2,3},{3,2},{4,5},{5,4},{6,7},{7,6},{8,9},{9,8},{10,11... | collective-permute-start | bytes 393224 | tf_op jit(solution)/shard_map/ppermute | solution.py:66
  39.9 9.8 %collective-permute-start.11 = (f32[256,128]{1,0:T(8,128)S(1)}, f32[256,128]{1,0:T(8,128)S(1)}, u32[]{:S(2)}, u32[]{:S(2)}) collective-permute-start(f32[256,128]{1,0:T(8,128)S(1)} %get-tuple-element.93), channel_id=1, source_target_pairs={{0,32},{1,2},{2,1},{3,4},{4,3},{5,6},{6,5},{7,8},{8,7},{9,10},{10,... | collective-permute-start | bytes 393224 | tf_op jit(solution)/shard_map/ppermute | solution.py:65
  49.7 5.3 %collective-permute-start.14 = (f32[192,128]{1,0:T(8,128)S(1)}, f32[192,128]{1,0:T(8,128)S(1)}, u32[]{:S(2)}, u32[]{:S(2)}) collective-permute-start(f32[192,128]{1,0:T(8,128)S(1)} %get-tuple-element.99), channel_id=1, source_target_pairs={{0,32},{1,33},{2,34},{3,35},{4,36},{5,37},{6,38},{7,39},{8,40},{9,... | collective-permute-start | bytes 294920 | tf_op jit(solution)/shard_map/ppermute | solution.py:66
  50.0 5.5 %collective-permute-start.15 = (f32[192,128]{1,0:T(8,128)S(1)}, f32[192,128]{1,0:T(8,128)S(1)}, u32[]{:S(2)}, u32[]{:S(2)}) collective-permute-start(f32[192,128]{1,0:T(8,128)S(1)} %get-tuple-element.100), channel_id=1, source_target_pairs={{0,1},{1,0},{2,3},{3,2},{4,5},{5,4},{6,7},{7,6},{8,9},{9,8},{10,11... | collective-permute-start | bytes 294920 | tf_op jit(solution)/shard_map/ppermute | solution.py:65
  53.0 15.6 %collective-permute-start.18 = (f32[448,128]{1,0:T(8,128)S(1)}, f32[448,128]{1,0:T(8,128)S(1)}, u32[]{:S(2)}, u32[]{:S(2)}) collective-permute-start(f32[448,128]{1,0:T(8,128)S(1)} %get-tuple-element.105), channel_id=1, source_target_pairs={{0,1},{1,0},{2,3},{3,2},{4,5},{5,4},{6,7},{7,6},{8,9},{9,8},{10,11... | collective-permute-start | bytes 688136 | tf_op jit(solution)/shard_map/ppermute | solution.py:66
  53.1 15.5 %collective-permute-start.19 = (f32[448,128]{1,0:T(8,128)S(1)}, f32[448,128]{1,0:T(8,128)S(1)}, u32[]{:S(2)}, u32[]{:S(2)}) collective-permute-start(f32[448,128]{1,0:T(8,128)S(1)} %get-tuple-element.106), channel_id=1, source_target_pairs={{0,32},{1,2},{2,1},{3,4},{4,3},{5,6},{6,5},{7,8},{8,7},{9,10},{10,... | collective-permute-start | bytes 688136 | tf_op jit(solution)/shard_map/ppermute | solution.py:65
  57.1 7.2 %collective-permute-start.16 = (f32[256,128]{1,0:T(8,128)S(1)}, f32[256,128]{1,0:T(8,128)S(1)}, u32[]{:S(2)}, u32[]{:S(2)}) collective-permute-start(f32[256,128]{1,0:T(8,128)S(1)} %get-tuple-element.103), channel_id=1, source_target_pairs={{0,1},{1,0},{2,3},{3,2},{4,5},{5,4},{6,7},{7,6},{8,9},{9,8},{10,11... | collective-permute-start | bytes 393224 | tf_op jit(solution)/shard_map/ppermute | solution.py:66
  57.2 8.6 %collective-permute-start.17 = (f32[256,128]{1,0:T(8,128)S(1)}, f32[256,128]{1,0:T(8,128)S(1)}, u32[]{:S(2)}, u32[]{:S(2)}) collective-permute-start(f32[256,128]{1,0:T(8,128)S(1)} %get-tuple-element.104), channel_id=1, source_target_pairs={{0,32},{1,2},{2,1},{3,4},{4,3},{5,6},{6,5},{7,8},{8,7},{9,10},{10,... | collective-permute-start | bytes 393224 | tf_op jit(solution)/shard_map/ppermute | solution.py:65
  65.8 6.2 %collective-permute-start.20 = (f32[192,128]{1,0:T(8,128)S(1)}, f32[192,128]{1,0:T(8,128)S(1)}, u32[]{:S(2)}, u32[]{:S(2)}) collective-permute-start(f32[192,128]{1,0:T(8,128)S(1)} %get-tuple-element.110), channel_id=1, source_target_pairs={{0,32},{1,33},{2,34},{3,35},{4,36},{5,37},{6,38},{7,39},{8,40},{9,... | collective-permute-start | bytes 294920 | tf_op jit(solution)/shard_map/ppermute | solution.py:66
  67.2 5.5 %collective-permute-start.21 = (f32[192,128]{1,0:T(8,128)S(1)}, f32[192,128]{1,0:T(8,128)S(1)}, u32[]{:S(2)}, u32[]{:S(2)}) collective-permute-start(f32[192,128]{1,0:T(8,128)S(1)} %get-tuple-element.111), channel_id=1, source_target_pairs={{0,1},{1,0},{2,3},{3,2},{4,5},{5,4},{6,7},{7,6},{8,9},{9,8},{10,11... | collective-permute-start | bytes 294920 | tf_op jit(solution)/shard_map/ppermute | solution.py:65
  70.2 15.6 %collective-permute-start.24 = (f32[448,128]{1,0:T(8,128)S(1)}, f32[448,128]{1,0:T(8,128)S(1)}, u32[]{:S(2)}, u32[]{:S(2)}) collective-permute-start(f32[448,128]{1,0:T(8,128)S(1)} %get-tuple-element.116), channel_id=1, source_target_pairs={{0,1},{1,0},{2,3},{3,2},{4,5},{5,4},{6,7},{7,6},{8,9},{9,8},{10,11... | collective-permute-start | bytes 688136 | tf_op jit(solution)/shard_map/ppermute | solution.py:66
  70.3 15.5 %collective-permute-start.25 = (f32[448,128]{1,0:T(8,128)S(1)}, f32[448,128]{1,0:T(8,128)S(1)}, u32[]{:S(2)}, u32[]{:S(2)}) collective-permute-start(f32[448,128]{1,0:T(8,128)S(1)} %get-tuple-element.117), channel_id=1, source_target_pairs={{0,32},{1,2},{2,1},{3,4},{4,3},{5,6},{6,5},{7,8},{8,7},{9,10},{10,... | collective-permute-start | bytes 688136 | tf_op jit(solution)/shard_map/ppermute | solution.py:65
  74.3 7.0 %collective-permute-start.22 = (f32[256,128]{1,0:T(8,128)S(1)}, f32[256,128]{1,0:T(8,128)S(1)}, u32[]{:S(2)}, u32[]{:S(2)}) collective-permute-start(f32[256,128]{1,0:T(8,128)S(1)} %get-tuple-element.114), channel_id=1, source_target_pairs={{0,1},{1,0},{2,3},{3,2},{4,5},{5,4},{6,7},{7,6},{8,9},{9,8},{10,11... | collective-permute-start | bytes 393224 | tf_op jit(solution)/shard_map/ppermute | solution.py:66
  74.4 8.6 %collective-permute-start.23 = (f32[256,128]{1,0:T(8,128)S(1)}, f32[256,128]{1,0:T(8,128)S(1)}, u32[]{:S(2)}, u32[]{:S(2)}) collective-permute-start(f32[256,128]{1,0:T(8,128)S(1)} %get-tuple-element.115), channel_id=1, source_target_pairs={{0,32},{1,2},{2,1},{3,4},{4,3},{5,6},{6,5},{7,8},{8,7},{9,10},{10,... | collective-permute-start | bytes 393224 | tf_op jit(solution)/shard_map/ppermute | solution.py:65
  83.0 6.1 %collective-permute-start.26 = (f32[192,128]{1,0:T(8,128)S(1)}, f32[192,128]{1,0:T(8,128)S(1)}, u32[]{:S(2)}, u32[]{:S(2)}) collective-permute-start(f32[192,128]{1,0:T(8,128)S(1)} %get-tuple-element.122), channel_id=1, source_target_pairs={{0,32},{1,33},{2,34},{3,35},{4,36},{5,37},{6,38},{7,39},{8,40},{9,... | collective-permute-start | bytes 294920 | tf_op jit(solution)/shard_map/ppermute | solution.py:66
  84.4 5.5 %collective-permute-start.27 = (f32[192,128]{1,0:T(8,128)S(1)}, f32[192,128]{1,0:T(8,128)S(1)}, u32[]{:S(2)}, u32[]{:S(2)}) collective-permute-start(f32[192,128]{1,0:T(8,128)S(1)} %get-tuple-element.123), channel_id=1, source_target_pairs={{0,1},{1,0},{2,3},{3,2},{4,5},{5,4},{6,7},{7,6},{8,9},{9,8},{10,11... | collective-permute-start | bytes 294920 | tf_op jit(solution)/shard_map/ppermute | solution.py:65

commit v5 on v4

--- a/solution.py
+++ b/solution.py
@@ -183,7 +183,7 @@
     loop(INNER, section)
 
 
-def load_kernel(keep, src, weight, field_in, kd_in, u_ref, rim_ref, buf, rim_buf, sems):
+def load_kernel(keep, src, field_in, kd_in, u_ref, rim_ref, buf, rim_buf, sems):
     chunk = 4
 
     def copies(i):
@@ -221,7 +221,7 @@
             number, base = count[0, a, e], slots_at(a, e)
 
             def term(k, m):
-                return jnp.full((1, LANE), jnp.where(k < number, weight[base + k], 0.0), jnp.float32)
+                return jnp.full((1, LANE), jnp.where(k < number, weight[0, a, e, k], 0.0), jnp.float32)
 
             grouped_adds(lambda k: src[base + k], number, term, dg_ref, (0,))
 
@@ -256,7 +256,7 @@
 
             def slot(k):
                 value = cc_ref[pl.ds(src[base + k], 1), :]
-                cw_ref[pl.ds((i * 3 + j) * CAP + k, 1), :] = value * jnp.where(k < number, weight[base + k], 0.0)
+                cw_ref[pl.ds((i * 3 + j) * CAP + k, 1), :] = value * jnp.where(k < number, weight[0, a, e, k], 0.0)
 
             live_slots(number, slot)
 
@@ -456,18 +456,18 @@
     asked_a, asked_b = exchange(match_target, match_target, "sec")
     which = lax.broadcasted_iota(jnp.int32, (2,) + match_source.shape[1:], 0)
     ids = flat(jnp.where(which == 0, match_source, match_target))
-    source, weight = ids.reshape(-1), match_weight.reshape(-1)
+    source = ids.reshape(-1)
     asked_a, asked_b = flat(asked_a), flat(asked_b)
     rows = [vmem(ROW_MSG, LANE), vmem(ROW_MSG, LANE)]
     field = vmem(FIELD, LANE)
     u, rim = kernel_call(
         load_kernel,
         [field, vmem(RIM, LANE)],
-        [SM, ANY, ANY, HB, HB],
+        [SM, ANY, HB, HB],
         scratch=[vmem(2, SEC, ROW, WID), vmem(SEC, WID), pltpu.SemaphoreType.DMA((3, 4))],
         cost=6_000_000,
         limit=8,
-    )(keep, source, weight, displacement, stiff_down)
+    )(keep, source, displacement, stiff_down)
 
     def pick(array, a, e):
         return lax.dynamic_slice(array, (0, a, e, 0), (1, 1, 1, CAP)).reshape(CAP)
@@ -496,7 +496,7 @@
         [SM, SM, SM, VM, VM],
         aliases={3: 0, 4: 1},
         cost=4_000_000,
-    )(source, weight, match_count, dg, u)
+    )(source, match_weight, match_count, dg, u)
     messages = [vmem(T_MSG, LANE), vmem(T_MSG, LANE)]
     u, to_a, to_b = kernel_call(pack_kernel, [field, *messages], [SM, SM, VM], aliases={2: 0}, cost=1_000_000)(
         wanted, first, u
@@ -507,7 +507,7 @@
         [SM] * 4 + [VM] * 6,
         aliases={8: 0, 9: 1},
         cost=1_000_000,
-    )(source, weight, match_count, first, dg, got_a, got_b, rim, cc, u)
+    )(source, match_weight, match_count, first, dg, got_a, got_b, rim, cc, u)
 
     whole = jax.ShapeDtypeStruct(displacement.shape, jnp.float32)
     for step in range(ITERS):

time: 92.1 us -> 92.1 us (level)
  transfers between devices with their start and end apart: 28 -> 28, of which waited for: 6 -> 6; matrix products, arithmetic and copies ran while one was open for 3% -> 2% of each run, Pallas kernels for 44% -> 45%
where the time goes in v5:
time: 92.1 us; the launch traced here: 91.9 us
  Pallas kernels  43.2 us (47%)
  starting transfers between devices  38.6 us (42%)
  waiting for transfers between devices  7.66 us (8%)
  local copies, waits for them, and re-layouts  1.55 us (2%)
    ppermute x14, starting transfers between devices, exchange(): from_b = lax.ppermute(to_b, ('sec', 'tile'), pairing(axis, 1))  31.9 us
    pallas_call x4, Pallas kernels, on_device(): kernel_call(dense_kernel, [field, vmem(2 * CAP, LANE), vmem(2 * CAP, LANE...  18.2 us
    ppermute x14, waiting for transfers between devices, exchange(): from_b = lax.ppermute(to_b, ('sec', 'tile'), pairing(axis, 1))  7.63 us
    ppermute x14, starting transfers between devices, exchange(): from_a = lax.ppermute(to_a, ('sec', 'tile'), pairing(axis, 0))  6.77 us
    pallas_call x3, Pallas kernels, on_device(): kernel_call(finish_kernel, [field] + messages, [SM] * 4 + [VM] * 5, alias...  4.68 us
    pallas_call x3, Pallas kernels, on_device(): kernel_call(tile_kernel, [field] + rows, [SM] * 3 + [VM] * 9, aliases={3:...  4.6 us
    pallas_call x1, Pallas kernels, on_device(): kernel_call(setup_kernel, [field, vmem(PART, LANE), vmem(PART + 2 * PAD,...  3.53 us
    pallas_call x1, Pallas kernels, on_device(): kernel_call(last_tile_kernel, [field, whole], [SM] * 3 + [VM] * 9, aliase...  3.36 us
  transfers between devices with their start and end apart: 28, of which 6 were waited for; matrix products, arithmetic and copies ran while one was open for 2% of the time, Pallas kernels for 45%

profile of v5, /device:TPU:7, one launch (start us, length us, event | category | flops | bytes accessed | tf_op | source)
XLA Modules:
  0.0 91.9 jit_solution(15735017062752034067)
XLA Ops:
  0.0 0.7 collective-permute-start
  0.7 2.9 %collective-permute-start.1 = (s32[1,3,3,32]{3,0,2,1:T(1,128)}, s32[1,3,3,32]{3,0,2,1:T(1,128)S(1)}, u32[]{:S(2)}, u32[]{:S(2)}) collective-permute-start(s32[1,3,3,32]{3,0,2,1:T(1,128)} %param.13), channel_id=1, source_target_pairs={{0,1},{1,0},{2,3},{3,2},{4,5},{5,4},{6,7},{7,6},{8,9},{9,8},{10,11... | collective-permute-start | bytes 3464 | tf_op jit(solution)/shard_map/ppermute | solution.py:65
  3.6 0.7 copy.60
  4.3 0.7 copy.61
  5.2 2.4 %shard_map.82 = (f32[8208,128]{1,0:T(8,128)S(1)}, f32[256,128]{1,0:T(8,128)S(1)}) custom-call(f32[1]{0:T(128)} %bitcast.5.keep, s32[576]{0:T(1024)S(1)} %reshape.130.src, f32[2,16,16,2048]{3,2,1,0:T(8,128)} %field_in.1, f32[16,16,2048]{2,1,0:T(8,128)} %kd_in.3), custom_call_target="tpu_custom_call" | custom-call | flops 6000000 | bytes 6000000 | tf_op jit(solution)/shard_map/pallas_call | solution.py:463
  7.8 4.2 %collective-permute-start.3 = (f32[264,128]{1,0:T(8,128)S(1)}, f32[264,128]{1,0:T(8,128)S(1)}, u32[]{:S(2)}, u32[]{:S(2)}) collective-permute-start(f32[264,128]{1,0:T(8,128)S(1)} %get-tuple-element.126), channel_id=1, source_target_pairs={{0,32},{1,2},{2,1},{3,4},{4,3},{5,6},{6,5},{7,8},{8,7},{9,10},{10,... | collective-permute-start | bytes 405512 | tf_op jit(solution)/shard_map/ppermute | solution.py:65
  12.1 0.1 collective-permute-start.2
  12.3 3.5 %shard_map.83 = (f32[8208,128]{1,0:T(8,128)S(1)}, f32[4096,128]{1,0:T(8,128)S(1)}, f32[4112,128]{1,0:T(8,128)S(1)}, f32[4096,128]{1,0:T(8,128)S(1)}, f32[448,128]{1,0:T(8,128)S(1)}, /*index=5*/f32[448,128]{1,0:T(8,128)S(1)}) custom-call(s32[3]{0:T(128)S(1)} %pad_add_fusion.first, ...), custom_call_target="tpu_custom_call", output_to_operand_aliasing={{0}: (3, {})} | custom-call | flops 6000000 | bytes 6000000 | tf_op jit(solution)/shard_map/pallas_call | solution.py:483
  15.8 1.5 %collective-permute-start.6 = (f32[448,128]{1,0:T(8,128)S(1)}, f32[448,128]{1,0:T(8,128)S(1)}, u32[]{:S(2)}, u32[]{:S(2)}) collective-permute-start(f32[448,128]{1,0:T(8,128)S(1)} %get-tuple-element.81), channel_id=1, source_target_pairs={{0,1},{1,0},{2,3},{3,2},{4,5},{5,4},{6,7},{7,6},{8,9},{9,8},{10,11... | collective-permute-start | bytes 688136 | tf_op jit(solution)/shard_map/ppermute | solution.py:66
  17.4 0.3 collective-permute-start.7
  17.7 1.8 %shard_map.84 = (f32[4096,128]{1,0:T(8,128)S(1)}, f32[8208,128]{1,0:T(8,128)S(1)}, f32[4096,128]{1,0:T(8,128)S(1)}) custom-call(s32[576]{0:T(1024)S(1)} %reshape.130.src, f32[1,3,3,32]{3,2,1,0:T(4,128)S(1)} %copy.42.weight, s32[1,3,3]{2,1,0:T(4,128)S(1)} %copy.55.count, ...), custom_call_target="tpu_custom_call", output_to_operand_aliasing={{0}: (3, {}), {1}: (4, {})} | custom-call | flops 4000000 | bytes 4000000 | tf_op jit(solution)/shard_map/pallas_call | solution.py:493
  19.6 0.9 shard_map.85
  20.7 4.6 %collective-permute-start.5 = (f32[256,128]{1,0:T(8,128)S(1)}, f32[256,128]{1,0:T(8,128)S(1)}, u32[]{:S(2)}, u32[]{:S(2)}) collective-permute-start(f32[256,128]{1,0:T(8,128)S(1)} %get-tuple-element.80), channel_id=1, source_target_pairs={{0,32},{1,2},{2,1},{3,4},{4,3},{5,6},{6,5},{7,8},{8,7},{9,10},{10,... | collective-permute-start | bytes 393224 | tf_op jit(solution)/shard_map/ppermute | solution.py:65
  25.3 1.6 %shard_map.86 = (f32[4096,128]{1,0:T(8,128)S(1)}, f32[8208,128]{1,0:T(8,128)S(1)}, f32[256,128]{1,0:T(8,128)S(1)}, f32[256,128]{1,0:T(8,128)S(1)}, f32[288,128]{1,0:T(8,128)S(1)}) custom-call(s32[576]{0:T(1024)S(1)} %reshape.130.src, f32[1,3,3,32]{3,2,1,0:T(4,128)S(1)} %copy.42.weight, ...), custom_call_target="tpu_custom_call", output_to_operand_aliasing={{0}: (8, {}), {1}: (9, {})} | custom-call | flops 1000000 | bytes 1000000 | tf_op jit(solution)/shard_map/pallas_call | solution.py:504
  26.9 4.5 %shard_map.87 = (f32[8208,128]{1,0:T(8,128)S(1)}, f32[64,128]{1,0:T(8,128)S(1)}, f32[64,128]{1,0:T(8,128)S(1)}) custom-call(s32[576]{0:T(1024)S(1)} %reshape.130.src, s32[1,3,3]{2,1,0:T(4,128)S(1)} %copy.55.count, s32[64]{0:T(128)S(1)} %pad_add_fusion.1.after.wanted_sec, f32[8208,128]{1,0:T(8,128)S(1)} %get-tuple-element.73.u_in, ...), custom_call_target="tpu_custom_call" | custom-call | flops 20000000 | bytes 20000000 | tf_op jit(solution)/shard_map/pallas_call | solution.py:515
  31.6 3.5 %collective-permute-start.9 = (f32[192,128]{1,0:T(8,128)S(1)}, f32[192,128]{1,0:T(8,128)S(1)}, u32[]{:S(2)}, u32[]{:S(2)}) collective-permute-start(f32[192,128]{1,0:T(8,128)S(1)} %get-tuple-element.89), channel_id=1, source_target_pairs={{0,1},{1,0},{2,3},{3,2},{4,5},{5,4},{6,7},{7,6},{8,9},{9,8},{10,11... | collective-permute-start | bytes 294920 | tf_op jit(solution)/shard_map/ppermute | solution.py:65
  35.1 1.5 %shard_map.88 = (f32[8208,128]{1,0:T(8,128)S(1)}, f32[448,128]{1,0:T(8,128)S(1)}, f32[448,128]{1,0:T(8,128)S(1)}) custom-call(s32[576]{0:T(1024)S(1)} %reshape.130.src, s32[1,3,3]{2,1,0:T(4,128)S(1)} %copy.55.count, s32[3]{0:T(128)S(1)} %pad_add_fusion.first, f32[8208,128]{1,0:T(8,128)S(1)} %get-tuple-element.78.u_in, ...), custom_call_target="tpu_custom_call", output_to_operand_aliasing={{0}: (3, {})} | custom-call | flops 2000000 | bytes 2000000 | tf_op jit(solution)/shard_map/pallas_call | solution.py:528
  36.7 0.1 collective-permute-start.12
  36.8 0.7 collective-permute-start.13
  37.5 1.6 %shard_map.90 = (f32[8208,128]{1,0:T(8,128)S(1)}, f32[256,128]{1,0:T(8,128)S(1)}, f32[256,128]{1,0:T(8,128)S(1)}) custom-call(s32[576]{0:T(1024)S(1)} %reshape.130.src, s32[1,3,3]{2,1,0:T(4,128)S(1)} %copy.55.count, s32[192]{0:T(256)S(1)} %maximum_convert_fusion.wanted, s32[3]{0:T(128)S(1)} %pad_add_fusion.first, ...), custom_call_target="tpu_custom_call", output_to_operand_aliasing={{0}: (4, {})} | custom-call | flops 2000000 | bytes 2000000 | tf_op jit(solution)/shard_map/pallas_call | solution.py:537
  39.1 0.8 collective-permute-start.10
  39.9 3.4 %collective-permute-start.11 = (f32[256,128]{1,0:T(8,128)S(1)}, f32[256,128]{1,0:T(8,128)S(1)}, u32[]{:S(2)}, u32[]{:S(2)}) collective-permute-start(f32[256,128]{1,0:T(8,128)S(1)} %get-tuple-element.93), channel_id=1, source_target_pairs={{0,32},{1,2},{2,1},{3,4},{4,3},{5,6},{6,5},{7,8},{8,7},{9,10},{10,... | collective-permute-start | bytes 393224 | tf_op jit(solution)/shard_map/ppermute | solution.py:65
  43.3 4.5 %shard_map.91 = (f32[8208,128]{1,0:T(8,128)S(1)}, f32[64,128]{1,0:T(8,128)S(1)}, f32[64,128]{1,0:T(8,128)S(1)}) custom-call(s32[576]{0:T(1024)S(1)} %reshape.130.src, s32[1,3,3]{2,1,0:T(4,128)S(1)} %copy.55.count, s32[64]{0:T(128)S(1)} %pad_add_fusion.1.after.wanted_sec, f32[8208,128]{1,0:T(8,128)S(1)} %get-tuple-element.90.u_in, ...), custom_call_target="tpu_custom_call" | custom-call | flops 20000000 | bytes 20000000 | tf_op jit(solution)/shard_map/pallas_call | solution.py:515
  47.8 1.7 %collective-permute-done.11.from_b = f32[256,128]{1,0:T(8,128)S(1)} collective-permute-done((f32[256,128]{1,0:T(8,128)S(1)}, f32[256,128]{1,0:T(8,128)S(1)}, u32[]{:S(2)}, u32[]{:S(2)}) %collective-permute-start.11) | collective-permute-done | bytes 131104 | tf_op jit(solution)/shard_map/ppermute | solution.py:65
  49.6 0.2 collective-permute-start.14
  49.7 1.7 %collective-permute-start.15 = (f32[192,128]{1,0:T(8,128)S(1)}, f32[192,128]{1,0:T(8,128)S(1)}, u32[]{:S(2)}, u32[]{:S(2)}) collective-permute-start(f32[192,128]{1,0:T(8,128)S(1)} %get-tuple-element.100), channel_id=1, source_target_pairs={{0,1},{1,0},{2,3},{3,2},{4,5},{5,4},{6,7},{7,6},{8,9},{9,8},{10,11... | collective-permute-start | bytes 294920 | tf_op jit(solution)/shard_map/ppermute | solution.py:65
  51.4 1.5 %shard_map.92 = (f32[8208,128]{1,0:T(8,128)S(1)}, f32[448,128]{1,0:T(8,128)S(1)}, f32[448,128]{1,0:T(8,128)S(1)}) custom-call(s32[576]{0:T(1024)S(1)} %reshape.130.src, s32[1,3,3]{2,1,0:T(4,128)S(1)} %copy.55.count, s32[3]{0:T(128)S(1)} %pad_add_fusion.first, f32[8208,128]{1,0:T(8,128)S(1)} %get-tuple-element.91.u_in, ...), custom_call_target="tpu_custom_call", output_to_operand_aliasing={{0}: (3, {})} | custom-call | flops 2000000 | bytes 2000000 | tf_op jit(solution)/shard_map/pallas_call | solution.py:528
  52.9 0.1 collective-permute-start.18
  53.0 1.4 %collective-permute-start.19 = (f32[448,128]{1,0:T(8,128)S(1)}, f32[448,128]{1,0:T(8,128)S(1)}, u32[]{:S(2)}, u32[]{:S(2)}) collective-permute-start(f32[448,128]{1,0:T(8,128)S(1)} %get-tuple-element.106), channel_id=1, source_target_pairs={{0,32},{1,2},{2,1},{3,4},{4,3},{5,6},{6,5},{7,8},{8,7},{9,10},{10,... | collective-permute-start | bytes 688136 | tf_op jit(solution)/shard_map/ppermute | solution.py:65
  54.5 0.8 collective-permute-done.15.from_b
  55.3 1.6 %shard_map.94 = (f32[8208,128]{1,0:T(8,128)S(1)}, f32[256,128]{1,0:T(8,128)S(1)}, f32[256,128]{1,0:T(8,128)S(1)}) custom-call(s32[576]{0:T(1024)S(1)} %reshape.130.src, s32[1,3,3]{2,1,0:T(4,128)S(1)} %copy.55.count, s32[192]{0:T(256)S(1)} %maximum_convert_fusion.wanted, s32[3]{0:T(128)S(1)} %pad_add_fusion.first, ...), custom_call_target="tpu_custom_call", output_to_operand_aliasing={{0}: (4, {})} | custom-call | flops 2000000 | bytes 2000000 | tf_op jit(solution)/shard_map/pallas_call | solution.py:537
  56.9 2.6 %collective-permute-start.17 = (f32[256,128]{1,0:T(8,128)S(1)}, f32[256,128]{1,0:T(8,128)S(1)}, u32[]{:S(2)}, u32[]{:S(2)}) collective-permute-start(f32[256,128]{1,0:T(8,128)S(1)} %get-tuple-element.104), channel_id=1, source_target_pairs={{0,32},{1,2},{2,1},{3,4},{4,3},{5,6},{6,5},{7,8},{8,7},{9,10},{10,... | collective-permute-start | bytes 393224 | tf_op jit(solution)/shard_map/ppermute | solution.py:65
  59.6 4.6 %shard_map.95 = (f32[8208,128]{1,0:T(8,128)S(1)}, f32[64,128]{1,0:T(8,128)S(1)}, f32[64,128]{1,0:T(8,128)S(1)}) custom-call(s32[576]{0:T(1024)S(1)} %reshape.130.src, s32[1,3,3]{2,1,0:T(4,128)S(1)} %copy.55.count, s32[64]{0:T(128)S(1)} %pad_add_fusion.1.after.wanted_sec, f32[8208,128]{1,0:T(8,128)S(1)} %get-tuple-element.101.u_in, ...), custom_call_target="tpu_custom_call" | custom-call | flops 20000000 | bytes 20000000 | tf_op jit(solution)/shard_map/pallas_call | solution.py:515
  64.2 1.3 %collective-permute-done.17.from_b = f32[256,128]{1,0:T(8,128)S(1)} collective-permute-done((f32[256,128]{1,0:T(8,128)S(1)}, f32[256,128]{1,0:T(8,128)S(1)}, u32[]{:S(2)}, u32[]{:S(2)}) %collective-permute-start.17) | collective-permute-done | bytes 131104 | tf_op jit(solution)/shard_map/ppermute | solution.py:65
  65.6 1.6 %collective-permute-start.20 = (f32[192,128]{1,0:T(8,128)S(1)}, f32[192,128]{1,0:T(8,128)S(1)}, u32[]{:S(2)}, u32[]{:S(2)}) collective-permute-start(f32[192,128]{1,0:T(8,128)S(1)} %get-tuple-element.110), channel_id=1, source_target_pairs={{0,32},{1,33},{2,34},{3,35},{4,36},{5,37},{6,38},{7,39},{8,40},{9,... | collective-permute-start | bytes 294920 | tf_op jit(solution)/shard_map/ppermute | solution.py:66
  67.2 1.4 %collective-permute-start.21 = (f32[192,128]{1,0:T(8,128)S(1)}, f32[192,128]{1,0:T(8,128)S(1)}, u32[]{:S(2)}, u32[]{:S(2)}) collective-permute-start(f32[192,128]{1,0:T(8,128)S(1)} %get-tuple-element.111), channel_id=1, source_target_pairs={{0,1},{1,0},{2,3},{3,2},{4,5},{5,4},{6,7},{7,6},{8,9},{9,8},{10,11... | collective-permute-start | bytes 294920 | tf_op jit(solution)/shard_map/ppermute | solution.py:65
  68.6 1.5 %shard_map.96 = (f32[8208,128]{1,0:T(8,128)S(1)}, f32[448,128]{1,0:T(8,128)S(1)}, f32[448,128]{1,0:T(8,128)S(1)}) custom-call(s32[576]{0:T(1024)S(1)} %reshape.130.src, s32[1,3,3]{2,1,0:T(4,128)S(1)} %copy.55.count, s32[3]{0:T(128)S(1)} %pad_add_fusion.first, f32[8208,128]{1,0:T(8,128)S(1)} %get-tuple-element.102.u_in, ...), custom_call_target="tpu_custom_call", output_to_operand_aliasing={{0}: (3, {})} | custom-call | flops 2000000 | bytes 2000000 | tf_op jit(solution)/shard_map/pallas_call | solution.py:528
  70.2 1.2 %collective-permute-start.25 = (f32[448,128]{1,0:T(8,128)S(1)}, f32[448,128]{1,0:T(8,128)S(1)}, u32[]{:S(2)}, u32[]{:S(2)}) collective-permute-start(f32[448,128]{1,0:T(8,128)S(1)} %get-tuple-element.117), channel_id=1, source_target_pairs={{0,32},{1,2},{2,1},{3,4},{4,3},{5,6},{6,5},{7,8},{8,7},{9,10},{10,... | collective-permute-start | bytes 688136 | tf_op jit(solution)/shard_map/ppermute | solution.py:65
  71.4 1.3 %collective-permute-done.21.from_b = f32[192,128]{1,0:T(8,128)S(1)} collective-permute-done((f32[192,128]{1,0:T(8,128)S(1)}, f32[192,128]{1,0:T(8,128)S(1)}, u32[]{:S(2)}, u32[]{:S(2)}) %collective-permute-start.21) | collective-permute-done | bytes 98336 | tf_op jit(solution)/shard_map/ppermute | solution.py:65
  72.7 1.6 %shard_map.98 = (f32[8208,128]{1,0:T(8,128)S(1)}, f32[256,128]{1,0:T(8,128)S(1)}, f32[256,128]{1,0:T(8,128)S(1)}) custom-call(s32[576]{0:T(1024)S(1)} %reshape.130.src, s32[1,3,3]{2,1,0:T(4,128)S(1)} %copy.55.count, s32[192]{0:T(256)S(1)} %maximum_convert_fusion.wanted, s32[3]{0:T(128)S(1)} %pad_add_fusion.first, ...), custom_call_target="tpu_custom_call", output_to_operand_aliasing={{0}: (4, {})} | custom-call | flops 2000000 | bytes 2000000 | tf_op jit(solution)/shard_map/pallas_call | solution.py:537
  74.4 2.4 %collective-permute-start.23 = (f32[256,128]{1,0:T(8,128)S(1)}, f32[256,128]{1,0:T(8,128)S(1)}, u32[]{:S(2)}, u32[]{:S(2)}) collective-permute-start(f32[256,128]{1,0:T(8,128)S(1)} %get-tuple-element.115), channel_id=1, source_target_pairs={{0,32},{1,2},{2,1},{3,4},{4,3},{5,6},{6,5},{7,8},{8,7},{9,10},{10,... | collective-permute-start | bytes 393224 | tf_op jit(solution)/shard_map/ppermute | solution.py:65
  76.7 4.5 %shard_map.99 = (f32[8208,128]{1,0:T(8,128)S(1)}, f32[64,128]{1,0:T(8,128)S(1)}, f32[64,128]{1,0:T(8,128)S(1)}) custom-call(s32[576]{0:T(1024)S(1)} %reshape.130.src, s32[1,3,3]{2,1,0:T(4,128)S(1)} %copy.55.count, s32[64]{0:T(128)S(1)} %pad_add_fusion.1.after.wanted_sec, f32[8208,128]{1,0:T(8,128)S(1)} %get-tuple-element.112.u_in, ...), custom_call_target="tpu_custom_call" | custom-call | flops 20000000 | bytes 20000000 | tf_op jit(solution)/shard_map/pallas_call | solution.py:515
  81.3 1.7 %collective-permute-done.23.from_b = f32[256,128]{1,0:T(8,128)S(1)} collective-permute-done((f32[256,128]{1,0:T(8,128)S(1)}, f32[256,128]{1,0:T(8,128)S(1)}, u32[]{:S(2)}, u32[]{:S(2)}) %collective-permute-start.23) | collective-permute-done | bytes 131104 | tf_op jit(solution)/shard_map/ppermute | solution.py:65
  83.0 1.3 %collective-permute-start.26 = (f32[192,128]{1,0:T(8,128)S(1)}, f32[192,128]{1,0:T(8,128)S(1)}, u32[]{:S(2)}, u32[]{:S(2)}) collective-permute-start(f32[192,128]{1,0:T(8,128)S(1)} %get-tuple-element.122), channel_id=1, source_target_pairs={{0,32},{1,33},{2,34},{3,35},{4,36},{5,37},{6,38},{7,39},{8,40},{9,... | collective-permute-start | bytes 294920 | tf_op jit(solution)/shard_map/ppermute | solution.py:66
  84.3 1.4 %collective-permute-start.27 = (f32[192,128]{1,0:T(8,128)S(1)}, f32[192,128]{1,0:T(8,128)S(1)}, u32[]{:S(2)}, u32[]{:S(2)}) collective-permute-start(f32[192,128]{1,0:T(8,128)S(1)} %get-tuple-element.123), channel_id=1, source_target_pairs={{0,1},{1,0},{2,3},{3,2},{4,5},{5,4},{6,7},{7,6},{8,9},{9,8},{10,11... | collective-permute-start | bytes 294920 | tf_op jit(solution)/shard_map/ppermute | solution.py:65
  85.7 3.4 %shard_map.100 = (f32[8208,128]{1,0:T(8,128)S(1)}, f32[2,16,16,2048]{3,2,1,0:T(8,128)}) custom-call(s32[576]{0:T(1024)S(1)} %reshape.130.src, s32[1,3,3]{2,1,0:T(4,128)S(1)} %copy.55.count, s32[3]{0:T(128)S(1)} %pad_add_fusion.first, f32[8208,128]{1,0:T(8,128)S(1)} %get-tuple-element.113.u_in, ...), custom_call_target="tpu_custom_call", output_to_operand_aliasing={{0}: (3, {})} | custom-call | flops 4000000 | bytes 4000000 | tf_op jit(solution)/shard_map/pallas_call | solution.py:546
  89.1 0.8 collective-permute-done.27.from_b
  89.9 2.0 %shard_map.102 = (f32[8208,128]{1,0:T(8,128)S(1)}, f32[2,16,16,2048]{3,2,1,0:T(8,128)}) custom-call(s32[576]{0:T(1024)S(1)} %reshape.130.src, s32[1,3,3]{2,1,0:T(4,128)S(1)} %copy.55.count, s32[3]{0:T(128)S(1)} %pad_add_fusion.first, f32[8208,128]{1,0:T(8,128)S(1)} %get-tuple-element.118.u_in, ...), custom_call_target="tpu_custom_call", output_to_operand_aliasing={{0}: (3, {}), {1}: (4, {})} | custom-call | flops 2000000 | bytes 2000000 | tf_op jit(solution)/shard_map/pallas_call | solution.py:556
  (56 shorter events, 1.1 us)
Async XLA Ops:
  0.0 12.1 %copy-start.1 = (s32[1,3,3]{2,0,1:T(1,128)S(1)}, s32[1,3,3]{2,0,1:T(1,128)}, u32[]{:S(2)}) copy-start(s32[1,3,3]{2,0,1:T(1,128)} %param.14) | copy-start | bytes 112
  0.0 12.1 %copy-start = (f32[1,3,3,32]{3,0,2,1:T(1,128)S(1)}, f32[1,3,3,32]{3,0,2,1:T(1,128)}, u32[]{:S(2)}) copy-start(f32[1,3,3,32]{3,0,2,1:T(1,128)} %param.15) | copy-start | bytes 3460
  0.0 7.6 %collective-permute-start = (s32[1,3,3,32]{3,0,2,1:T(1,128)}, s32[1,3,3,32]{3,0,2,1:T(1,128)S(1)}, u32[]{:S(2)}, u32[]{:S(2)}) collective-permute-start(s32[1,3,3,32]{3,0,2,1:T(1,128)} %param.13), channel_id=1, source_target_pairs={{0,32},{1,33},{2,34},{3,35},{4,36},{5,37},{6,38},{7,39},{8,40},{9,... | collective-permute-start | bytes 3464 | tf_op jit(solution)/shard_map/ppermute | solution.py:66
  0.7 7.0 %collective-permute-start.1 = (s32[1,3,3,32]{3,0,2,1:T(1,128)}, s32[1,3,3,32]{3,0,2,1:T(1,128)S(1)}, u32[]{:S(2)}, u32[]{:S(2)}) collective-permute-start(s32[1,3,3,32]{3,0,2,1:T(1,128)} %param.13), channel_id=1, source_target_pairs={{0,1},{1,0},{2,3},{3,2},{4,5},{5,4},{6,7},{7,6},{8,9},{9,8},{10,11... | collective-permute-start | bytes 3464 | tf_op jit(solution)/shard_map/ppermute | solution.py:65
  7.8 11.7 %collective-permute-start.3 = (f32[264,128]{1,0:T(8,128)S(1)}, f32[264,128]{1,0:T(8,128)S(1)}, u32[]{:S(2)}, u32[]{:S(2)}) collective-permute-start(f32[264,128]{1,0:T(8,128)S(1)} %get-tuple-element.126), channel_id=1, source_target_pairs={{0,32},{1,2},{2,1},{3,4},{4,3},{5,6},{6,5},{7,8},{8,7},{9,10},{10,... | collective-permute-start | bytes 405512 | tf_op jit(solution)/shard_map/ppermute | solution.py:65
  12.1 7.4 %collective-permute-start.2 = (f32[264,128]{1,0:T(8,128)S(1)}, f32[264,128]{1,0:T(8,128)S(1)}, u32[]{:S(2)}, u32[]{:S(2)}) collective-permute-start(f32[264,128]{1,0:T(8,128)S(1)} %get-tuple-element.125), channel_id=1, source_target_pairs={{0,1},{1,0},{2,3},{3,2},{4,5},{5,4},{6,7},{7,6},{8,9},{9,8},{10,11... | collective-permute-start | bytes 405512 | tf_op jit(solution)/shard_map/ppermute | solution.py:66
  15.8 19.3 %collective-permute-start.6 = (f32[448,128]{1,0:T(8,128)S(1)}, f32[448,128]{1,0:T(8,128)S(1)}, u32[]{:S(2)}, u32[]{:S(2)}) collective-permute-start(f32[448,128]{1,0:T(8,128)S(1)} %get-tuple-element.81), channel_id=1, source_target_pairs={{0,1},{1,0},{2,3},{3,2},{4,5},{5,4},{6,7},{7,6},{8,9},{9,8},{10,11... | collective-permute-start | bytes 688136 | tf_op jit(solution)/shard_map/ppermute | solution.py:66
  17.4 17.8 %collective-permute-start.7 = (f32[448,128]{1,0:T(8,128)S(1)}, f32[448,128]{1,0:T(8,128)S(1)}, u32[]{:S(2)}, u32[]{:S(2)}) collective-permute-start(f32[448,128]{1,0:T(8,128)S(1)} %get-tuple-element.82), channel_id=1, source_target_pairs={{0,32},{1,2},{2,1},{3,4},{4,3},{5,6},{6,5},{7,8},{8,7},{9,10},{10,... | collective-permute-start | bytes 688136 | tf_op jit(solution)/shard_map/ppermute | solution.py:65
  17.7 7.6 %copy-start.2 = (f32[128]{0:T(128)S(1)}, f32[128]{0:T(128)}, u32[]{:S(2)}) copy-start(f32[128]{0:T(128)} %param.11) | copy-start | bytes 1540
  20.6 10.9 %collective-permute-start.4 = (f32[256,128]{1,0:T(8,128)S(1)}, f32[256,128]{1,0:T(8,128)S(1)}, u32[]{:S(2)}, u32[]{:S(2)}) collective-permute-start(f32[256,128]{1,0:T(8,128)S(1)} %get-tuple-element.79), channel_id=1, source_target_pairs={{0,1},{1,0},{2,3},{3,2},{4,5},{5,4},{6,7},{7,6},{8,9},{9,8},{10,11... | collective-permute-start | bytes 393224 | tf_op jit(solution)/shard_map/ppermute | solution.py:66
  20.7 10.8 %collective-permute-start.5 = (f32[256,128]{1,0:T(8,128)S(1)}, f32[256,128]{1,0:T(8,128)S(1)}, u32[]{:S(2)}, u32[]{:S(2)}) collective-permute-start(f32[256,128]{1,0:T(8,128)S(1)} %get-tuple-element.80), channel_id=1, source_target_pairs={{0,32},{1,2},{2,1},{3,4},{4,3},{5,6},{6,5},{7,8},{8,7},{9,10},{10,... | collective-permute-start | bytes 393224 | tf_op jit(solution)/shard_map/ppermute | solution.py:65
  31.5 6.0 %collective-permute-start.8 = (f32[192,128]{1,0:T(8,128)S(1)}, f32[192,128]{1,0:T(8,128)S(1)}, u32[]{:S(2)}, u32[]{:S(2)}) collective-permute-start(f32[192,128]{1,0:T(8,128)S(1)} %get-tuple-element.88), channel_id=1, source_target_pairs={{0,32},{1,33},{2,34},{3,35},{4,36},{5,37},{6,38},{7,39},{8,40},{9,... | collective-permute-start | bytes 294920 | tf_op jit(solution)/shard_map/ppermute | solution.py:66
  31.6 5.9 %collective-permute-start.9 = (f32[192,128]{1,0:T(8,128)S(1)}, f32[192,128]{1,0:T(8,128)S(1)}, u32[]{:S(2)}, u32[]{:S(2)}) collective-permute-start(f32[192,128]{1,0:T(8,128)S(1)} %get-tuple-element.89), channel_id=1, source_target_pairs={{0,1},{1,0},{2,3},{3,2},{4,5},{5,4},{6,7},{7,6},{8,9},{9,8},{10,11... | collective-permute-start | bytes 294920 | tf_op jit(solution)/shard_map/ppermute | solution.py:65
  36.7 14.7 %collective-permute-start.12 = (f32[448,128]{1,0:T(8,128)S(1)}, f32[448,128]{1,0:T(8,128)S(1)}, u32[]{:S(2)}, u32[]{:S(2)}) collective-permute-start(f32[448,128]{1,0:T(8,128)S(1)} %get-tuple-element.94), channel_id=1, source_target_pairs={{0,1},{1,0},{2,3},{3,2},{4,5},{5,4},{6,7},{7,6},{8,9},{9,8},{10,11... | collective-permute-start | bytes 688136 | tf_op jit(solution)/shard_map/ppermute | solution.py:66
  36.8 14.6 %collective-permute-start.13 = (f32[448,128]{1,0:T(8,128)S(1)}, f32[448,128]{1,0:T(8,128)S(1)}, u32[]{:S(2)}, u32[]{:S(2)}) collective-permute-start(f32[448,128]{1,0:T(8,128)S(1)} %get-tuple-element.95), channel_id=1, source_target_pairs={{0,32},{1,2},{2,1},{3,4},{4,3},{5,6},{6,5},{7,8},{8,7},{9,10},{10,... | collective-permute-start | bytes 688136 | tf_op jit(solution)/shard_map/ppermute | solution.py:65
  39.1 8.7 %collective-permute-start.10 = (f32[256,128]{1,0:T(8,128)S(1)}, f32[256,128]{1,0:T(8,128)S(1)}, u32[]{:S(2)}, u32[]{:S(2)}) collective-permute-start(f32[256,128]{1,0:T(8,128)S(1)} %get-tuple-element.92), channel_id=1, source_target_pairs={{0,1},{1,0},{2,3},{3,2},{4,5},{5,4},{6,7},{7,6},{8,9},{9,8},{10,11... | collective-permute-start | bytes 393224 | tf_op jit(solution)/shard_map/ppermute | solution.py:66
  39.9 9.7 %collective-permute-start.11 = (f32[256,128]{1,0:T(8,128)S(1)}, f32[256,128]{1,0:T(8,128)S(1)}, u32[]{:S(2)}, u32[]{:S(2)}) collective-permute-start(f32[256,128]{1,0:T(8,128)S(1)} %get-tuple-element.93), channel_id=1, source_target_pairs={{0,32},{1,2},{2,1},{3,4},{4,3},{5,6},{6,5},{7,8},{8,7},{9,10},{10,... | collective-permute-start | bytes 393224 | tf_op jit(solution)/shard_map/ppermute | solution.py:65
  49.6 4.9 %collective-permute-start.14 = (f32[192,128]{1,0:T(8,128)S(1)}, f32[192,128]{1,0:T(8,128)S(1)}, u32[]{:S(2)}, u32[]{:S(2)}) collective-permute-start(f32[192,128]{1,0:T(8,128)S(1)} %get-tuple-element.99), channel_id=1, source_target_pairs={{0,32},{1,33},{2,34},{3,35},{4,36},{5,37},{6,38},{7,39},{8,40},{9,... | collective-permute-start | bytes 294920 | tf_op jit(solution)/shard_map/ppermute | solution.py:66
  49.7 5.6 %collective-permute-start.15 = (f32[192,128]{1,0:T(8,128)S(1)}, f32[192,128]{1,0:T(8,128)S(1)}, u32[]{:S(2)}, u32[]{:S(2)}) collective-permute-start(f32[192,128]{1,0:T(8,128)S(1)} %get-tuple-element.100), channel_id=1, source_target_pairs={{0,1},{1,0},{2,3},{3,2},{4,5},{5,4},{6,7},{7,6},{8,9},{9,8},{10,11... | collective-permute-start | bytes 294920 | tf_op jit(solution)/shard_map/ppermute | solution.py:65
  52.9 15.6 %collective-permute-start.18 = (f32[448,128]{1,0:T(8,128)S(1)}, f32[448,128]{1,0:T(8,128)S(1)}, u32[]{:S(2)}, u32[]{:S(2)}) collective-permute-start(f32[448,128]{1,0:T(8,128)S(1)} %get-tuple-element.105), channel_id=1, source_target_pairs={{0,1},{1,0},{2,3},{3,2},{4,5},{5,4},{6,7},{7,6},{8,9},{9,8},{10,11... | collective-permute-start | bytes 688136 | tf_op jit(solution)/shard_map/ppermute | solution.py:66
  53.0 15.5 %collective-permute-start.19 = (f32[448,128]{1,0:T(8,128)S(1)}, f32[448,128]{1,0:T(8,128)S(1)}, u32[]{:S(2)}, u32[]{:S(2)}) collective-permute-start(f32[448,128]{1,0:T(8,128)S(1)} %get-tuple-element.106), channel_id=1, source_target_pairs={{0,32},{1,2},{2,1},{3,4},{4,3},{5,6},{6,5},{7,8},{8,7},{9,10},{10,... | collective-permute-start | bytes 688136 | tf_op jit(solution)/shard_map/ppermute | solution.py:65
  56.8 7.4 %collective-permute-start.16 = (f32[256,128]{1,0:T(8,128)S(1)}, f32[256,128]{1,0:T(8,128)S(1)}, u32[]{:S(2)}, u32[]{:S(2)}) collective-permute-start(f32[256,128]{1,0:T(8,128)S(1)} %get-tuple-element.103), channel_id=1, source_target_pairs={{0,1},{1,0},{2,3},{3,2},{4,5},{5,4},{6,7},{7,6},{8,9},{9,8},{10,11... | collective-permute-start | bytes 393224 | tf_op jit(solution)/shard_map/ppermute | solution.py:66
  56.9 8.6 %collective-permute-start.17 = (f32[256,128]{1,0:T(8,128)S(1)}, f32[256,128]{1,0:T(8,128)S(1)}, u32[]{:S(2)}, u32[]{:S(2)}) collective-permute-start(f32[256,128]{1,0:T(8,128)S(1)} %get-tuple-element.104), channel_id=1, source_target_pairs={{0,32},{1,2},{2,1},{3,4},{4,3},{5,6},{6,5},{7,8},{8,7},{9,10},{10,... | collective-permute-start | bytes 393224 | tf_op jit(solution)/shard_map/ppermute | solution.py:65
  65.6 5.9 %collective-permute-start.20 = (f32[192,128]{1,0:T(8,128)S(1)}, f32[192,128]{1,0:T(8,128)S(1)}, u32[]{:S(2)}, u32[]{:S(2)}) collective-permute-start(f32[192,128]{1,0:T(8,128)S(1)} %get-tuple-element.110), channel_id=1, source_target_pairs={{0,32},{1,33},{2,34},{3,35},{4,36},{5,37},{6,38},{7,39},{8,40},{9,... | collective-permute-start | bytes 294920 | tf_op jit(solution)/shard_map/ppermute | solution.py:66
  67.2 5.5 %collective-permute-start.21 = (f32[192,128]{1,0:T(8,128)S(1)}, f32[192,128]{1,0:T(8,128)S(1)}, u32[]{:S(2)}, u32[]{:S(2)}) collective-permute-start(f32[192,128]{1,0:T(8,128)S(1)} %get-tuple-element.111), channel_id=1, source_target_pairs={{0,1},{1,0},{2,3},{3,2},{4,5},{5,4},{6,7},{7,6},{8,9},{9,8},{10,11... | collective-permute-start | bytes 294920 | tf_op jit(solution)/shard_map/ppermute | solution.py:65
  70.1 15.6 %collective-permute-start.24 = (f32[448,128]{1,0:T(8,128)S(1)}, f32[448,128]{1,0:T(8,128)S(1)}, u32[]{:S(2)}, u32[]{:S(2)}) collective-permute-start(f32[448,128]{1,0:T(8,128)S(1)} %get-tuple-element.116), channel_id=1, source_target_pairs={{0,1},{1,0},{2,3},{3,2},{4,5},{5,4},{6,7},{7,6},{8,9},{9,8},{10,11... | collective-permute-start | bytes 688136 | tf_op jit(solution)/shard_map/ppermute | solution.py:66
  70.2 15.5 %collective-permute-start.25 = (f32[448,128]{1,0:T(8,128)S(1)}, f32[448,128]{1,0:T(8,128)S(1)}, u32[]{:S(2)}, u32[]{:S(2)}) collective-permute-start(f32[448,128]{1,0:T(8,128)S(1)} %get-tuple-element.117), channel_id=1, source_target_pairs={{0,32},{1,2},{2,1},{3,4},{4,3},{5,6},{6,5},{7,8},{8,7},{9,10},{10,... | collective-permute-start | bytes 688136 | tf_op jit(solution)/shard_map/ppermute | solution.py:65
  74.3 7.0 %collective-permute-start.22 = (f32[256,128]{1,0:T(8,128)S(1)}, f32[256,128]{1,0:T(8,128)S(1)}, u32[]{:S(2)}, u32[]{:S(2)}) collective-permute-start(f32[256,128]{1,0:T(8,128)S(1)} %get-tuple-element.114), channel_id=1, source_target_pairs={{0,1},{1,0},{2,3},{3,2},{4,5},{5,4},{6,7},{7,6},{8,9},{9,8},{10,11... | collective-permute-start | bytes 393224 | tf_op jit(solution)/shard_map/ppermute | solution.py:66
  74.4 8.6 %collective-permute-start.23 = (f32[256,128]{1,0:T(8,128)S(1)}, f32[256,128]{1,0:T(8,128)S(1)}, u32[]{:S(2)}, u32[]{:S(2)}) collective-permute-start(f32[256,128]{1,0:T(8,128)S(1)} %get-tuple-element.115), channel_id=1, source_target_pairs={{0,32},{1,2},{2,1},{3,4},{4,3},{5,6},{6,5},{7,8},{8,7},{9,10},{10,... | collective-permute-start | bytes 393224 | tf_op jit(solution)/shard_map/ppermute | solution.py:65
  83.0 6.1 %collective-permute-start.26 = (f32[192,128]{1,0:T(8,128)S(1)}, f32[192,128]{1,0:T(8,128)S(1)}, u32[]{:S(2)}, u32[]{:S(2)}) collective-permute-start(f32[192,128]{1,0:T(8,128)S(1)} %get-tuple-element.122), channel_id=1, source_target_pairs={{0,32},{1,33},{2,34},{3,35},{4,36},{5,37},{6,38},{7,39},{8,40},{9,... | collective-permute-start | bytes 294920 | tf_op jit(solution)/shard_map/ppermute | solution.py:66
  84.3 5.5 %collective-permute-start.27 = (f32[192,128]{1,0:T(8,128)S(1)}, f32[192,128]{1,0:T(8,128)S(1)}, u32[]{:S(2)}, u32[]{:S(2)}) collective-permute-start(f32[192,128]{1,0:T(8,128)S(1)} %get-tuple-element.123), channel_id=1, source_target_pairs={{0,1},{1,0},{2,3},{3,2},{4,5},{5,4},{6,7},{7,6},{8,9},{9,8},{10,11... | collective-permute-start | bytes 294920 | tf_op jit(solution)/shard_map/ppermute | solution.py:65
